TPU v7x, 32 devices: a whole 2x2x4 slice. The times are simulated.
32 devices in a mesh: dp: 2 (over core), gx: 4 (over z), gy: 4 (over y, x).
Axes of the slice: x: 2, y: 2, z: 4, core: 2. Of those that a mesh axis runs over, the one named last changes fastest.
Arguments:
- latents_in: bfloat16 [16384, 1152], P(('dp', 'gy', 'gx')), may hold values from -6 to 6
- condition: bfloat16 [16, 1152], P('dp', 'gy'), may hold values from -6 to 6
- ada_weight: bfloat16 [1152, 6, 1152], P('gy'), may hold values from -0.1875 to 0.1875
- ada_bias: float32 [6, 1152], replicated, may hold values from -1.75 to 1.75
- query_weight: bfloat16 [1152, 1152], P('gx', 'gy'), may hold values from -1 to 1
- key_weight: bfloat16 [1152, 1152], P('gx', 'gy'), may hold values from -0.1875 to 0.1875
- value_weight: bfloat16 [1152, 1152], P('gx', 'gy'), may hold values from -0.1875 to 0.1875
- query_bias: float32 [1152], P('gy'), may hold values from -1.75 to 1.75
- value_bias: float32 [1152], P('gy'), may hold values from -1.75 to 1.75
- out_weight: bfloat16 [1152, 1152], P('gy', 'gx'), may hold values from -0.75 to 0.75
- out_bias: float32 [1152], P('gx'), may hold values from -1.75 to 1.75
- up_weight: bfloat16 [1152, 4608], P('gx', 'gy'), may hold values from -0.1875 to 0.1875
- up_bias: float32 [4608], P('gy'), may hold values from -1.75 to 1.75
- down_weight: bfloat16 [4608, 1152], P('gy', 'gx'), may hold values from -0.09375 to 0.09375
- down_bias: float32 [1152], P('gx'), may hold values from -1.75 to 1.75
- grad_out: float32 [16384, 1152], P(('dp', 'gy', 'gx')), may hold values from -6 to 6
Outputs:
- latents_out: float32 [16384, 1152], P(('dp', 'gy', 'gx'))
- grad_latents: float32 [16384, 1152], P(('dp', 'gy', 'gx'))
- grad_condition: float32 [16, 1152], P('dp', 'gy')
- grad_ada_weight: float32 [1152, 6, 1152], P('gy')
- grad_ada_bias: float32 [6, 1152], replicated
- grad_query_weight: float32 [1152, 1152], P('gx', 'gy')
- grad_key_weight: float32 [1152, 1152], P('gx', 'gy')
- grad_value_weight: float32 [1152, 1152], P('gx', 'gy')
- grad_query_bias: float32 [1152], P('gy')
- grad_value_bias: float32 [1152], P('gy')
- grad_out_weight: float32 [1152, 1152], P('gy', 'gx')
- grad_out_bias: float32 [1152], P('gx')
- grad_up_weight: float32 [1152, 4608], P('gx', 'gy')
- grad_up_bias: float32 [4608], P('gy')
- grad_down_weight: float32 [4608, 1152], P('gy', 'gx')
- grad_down_bias: float32 [1152], P('gx')
- logit_max: float32 [16], P('gy')
- clipped_query_weight: float32 [1152, 1152], P('gx', 'gy')
- clipped_key_weight: float32 [1152, 1152], P('gx', 'gy')
- clipped_query_bias: float32 [1152], P('gy')
All inputs are finite; a program needn't handle non-finite values.
Results may differ from a plain program's by a relative error of at most 0.0169.
Values may be sent and summed in bfloat16 or wider, within the bound.
No kernel may reach another device: no remote copies, remote signals or barrier semaphores. Data moves between devices by JAX's collectives and lax.ppermute only.
A program may use at most 256 MiB of HBM per device.

v0:
```python
import math

import jax
import jax.numpy as jnp
from jax import lax
from jax.sharding import PartitionSpec as P

HD = 72
SEQ = 1024
TAU = 8


EPS = 1e-06
HIGH = lax.Precision.HIGHEST
GELU_ROOT = 0.7978845608028654
GELU_CUBE = 0.044715


def gelu_parts(inputs):
    inner_arg = GELU_ROOT * (inputs + GELU_CUBE * inputs * inputs * inputs)
    tangent = jnp.tanh(inner_arg)
    output = 0.5 * inputs * (1.0 + tangent)
    slope_rows = 0.5 * (1.0 + tangent) + 0.5 * inputs * (1.0 - tangent * tangent) * GELU_ROOT * (
        1.0 + 3.0 * GELU_CUBE * inputs * inputs
    )
    return (output, slope_rows)


def gather_gy(rows_in):
    return lax.all_gather(rows_in, "gy", axis=0, tiled=True)


def gather_gx(rows_in):
    return lax.all_gather(rows_in, "gx", axis=0, tiled=True)


def split_features(rows_low):
    return lax.all_to_all(rows_low, "gx", split_axis=1, concat_axis=0, tiled=True)


def join_features(rows_split_f32):
    return lax.all_to_all(
        rows_split_f32.astype(jnp.bfloat16), "gx", split_axis=0, concat_axis=1, tiled=True
    ).astype(rows_split_f32.dtype)


def gather_weights(joint_weight, up_weight, out_weight, down_weight):
    return (
        (joint_weight, up_weight, out_weight, down_weight),
        (joint_weight, up_weight, out_weight, down_weight),
    )


def normalize(rows_in):
    mean_row = jnp.mean(rows_in, axis=1, keepdims=True)
    centred = rows_in - mean_row
    inverse = lax.rsqrt(jnp.mean(centred * centred, axis=1, keepdims=True) + EPS)
    return (centred * inverse, inverse)


def normalize_back(grad_hat, normed, inverse):
    grad_mean = jnp.mean(grad_hat, axis=1, keepdims=True)
    cross_mean = jnp.mean(grad_hat * normed, axis=1, keepdims=True)
    return inverse * (grad_hat - grad_mean - normed * cross_mean)


def sum_over_gx(full_rows, bundle, flipped):
    contract_dims = ((1,), (1,)) if flipped else ((1,), (0,))

    def partial_term(first_row, row_count):
        return lax.dot_general(
            full_rows, bundle[0], (contract_dims, ((), ())), preferred_element_type=jnp.float32
        )

    return lax.psum_scatter(
        partial_term(jnp.int32(0), full_rows.shape[0] // lax.axis_size("gx") * lax.axis_size("gx")),
        "gx",
        scatter_dimension=0,
        tiled=True,
    )


def sum_over_gy(full_rows, bundle, flipped):
    contract_dims = ((1,), (1,)) if flipped else ((1,), (0,))

    def partial_term(first_row, row_count):
        return lax.dot_general(
            full_rows, bundle[0], (contract_dims, ((), ())), preferred_element_type=jnp.float32
        )

    return lax.psum_scatter(
        partial_term(
            jnp.int32(0), full_rows.shape[0] // lax.axis_size("gy") * lax.axis_size("gy")
        ).astype(jnp.bfloat16),
        "gy",
        scatter_dimension=0,
        tiled=True,
    ).astype(jnp.float32)


def to_rows_a(rows_b, bundle, flipped):
    full_rows = gather_gx(rows_b)
    return (full_rows, sum_over_gy(full_rows, bundle, flipped))


def from_rows_a(rows_a_low, bundle):
    full_rows = gather_gy(rows_a_low)
    return (full_rows, sum_over_gx(full_rows, bundle, True))


def project_up(normed_low, bundle):
    full_rows = gather_gy(normed_low)
    return (full_rows, sum_over_gx(full_rows, bundle, False))


def attend_one(packed):
    queries, keys_in, values_in = packed
    scores = jnp.einsum("qhd,khd->hqk", queries, keys_in, preferred_element_type=jnp.float32) * (
        1.0 / math.sqrt(HD)
    )
    top_row = jnp.max(scores, axis=2)
    weights = jnp.exp(scores - top_row[:, :, None])
    denominator = jnp.sum(weights, axis=2)
    prob_rows = (weights / denominator[:, :, None]).astype(jnp.bfloat16)
    mixed_rows = jnp.einsum(
        "hqk,khd->qhd", prob_rows, values_in, preferred_element_type=jnp.float32
    )
    return (
        mixed_rows.astype(jnp.bfloat16),
        top_row + jnp.log(denominator),
        jnp.max(top_row, axis=1),
    )


def attend_back(packed):
    queries, keys_in, values_in, grad_mixed, log_sums = packed
    scores = jnp.einsum("qhd,khd->hqk", queries, keys_in, preferred_element_type=jnp.float32) * (
        1.0 / math.sqrt(HD)
    )
    prob_rows = jnp.exp(scores - log_sums[:, :, None])
    prob_low = prob_rows.astype(jnp.bfloat16)
    grad_probs = jnp.einsum(
        "qhd,khd->hqk", grad_mixed, values_in, preferred_element_type=jnp.float32
    )
    row_delta = jnp.sum(grad_probs * prob_rows, axis=2)
    grad_scores = (prob_rows * (grad_probs - row_delta[:, :, None])).astype(jnp.bfloat16)
    grad_query = jnp.einsum(
        "hqk,khd->qhd", grad_scores, keys_in, preferred_element_type=jnp.float32
    ) * (1.0 / math.sqrt(HD))
    grad_key = jnp.einsum(
        "hqk,qhd->khd", grad_scores, queries, preferred_element_type=jnp.float32
    ) * (1.0 / math.sqrt(HD))
    grad_value = jnp.einsum(
        "hqk,qhd->khd", prob_low, grad_mixed, preferred_element_type=jnp.float32
    )
    return (grad_query, grad_key, grad_value)


def placed_sum(local_sum, gy_index):
    total = jnp.zeros((local_sum.shape[0] * lax.axis_size("gy"),), jnp.float32)
    return lax.dynamic_update_slice_in_dim(total, local_sum, gy_index * local_sum.shape[0], 0)


def body(
    latents_in,
    condition,
    ada_weight,
    ada_bias,
    query_weight,
    key_weight,
    value_weight,
    query_bias,
    value_bias,
    out_weight,
    out_bias,
    up_weight,
    up_bias,
    down_weight,
    down_bias,
    grad_out,
):
    rows_c = latents_in.shape[0]
    width = latents_in.shape[1]
    latent_count = condition.shape[0]
    head_cols = query_weight.shape[1]
    heads_here = head_cols // HD
    width_x = out_bias.shape[0]
    cond_f32 = condition.astype(jnp.float32)
    silu_cond = jax.nn.silu(cond_f32).astype(jnp.bfloat16)
    mod_part = jnp.einsum("le,emf->lmf", silu_cond, ada_weight, preferred_element_type=jnp.float32)
    modulation = lax.psum(mod_part, "gy") + ada_bias[None]
    first_row = (lax.axis_index("gy") * lax.axis_size("gx") + lax.axis_index("gx")) * rows_c
    row_latent = (first_row + jnp.arange(rows_c, dtype=jnp.int32)) // SEQ
    selector = (row_latent[:, None] == jnp.arange(latent_count, dtype=jnp.int32)[None, :]).astype(
        jnp.float32
    )
    mod_rows = jnp.dot(
        selector, modulation.reshape(latent_count, 6 * width), precision=HIGH
    ).reshape(rows_c, 6, width)
    shift_one, scale_one, gate_one = (mod_rows[:, 0], mod_rows[:, 1], mod_rows[:, 2])
    shift_two, scale_two, gate_two = (mod_rows[:, 3], mod_rows[:, 4], mod_rows[:, 5])
    joint_weight = jnp.concatenate([query_weight, key_weight, value_weight], axis=1)
    along_x, along_y = gather_weights(joint_weight, up_weight, out_weight, down_weight)
    joint_set = (joint_weight, along_x[0], along_y[0])
    up_set = (up_weight, along_x[1], along_y[1])
    out_set = (out_weight, along_x[2], along_y[2])
    down_set = (down_weight, along_x[3], along_y[3])
    residual = latents_in.astype(jnp.float32)
    normed_one, inverse_one = normalize(residual)
    hidden_one = (normed_one * (1.0 + scale_one) + shift_one).astype(jnp.bfloat16)
    hidden_one_all, joint_sum = project_up(split_features(hidden_one), joint_set)
    queries = (joint_sum[:, :head_cols] + query_bias).astype(jnp.bfloat16)
    keys_here = joint_sum[:, head_cols : 2 * head_cols].astype(jnp.bfloat16)
    values_here = (joint_sum[:, 2 * head_cols :] + value_bias).astype(jnp.bfloat16)
    rows_b = queries.shape[0]
    per_latent = rows_b // SEQ

    def split_heads(matrix_rows):
        return matrix_rows.reshape(per_latent, SEQ, heads_here, HD)

    mixed_all, log_sums, head_tops = lax.map(
        attend_one, (split_heads(queries), split_heads(keys_here), split_heads(values_here))
    )
    logit_max = lax.pmax(jnp.max(head_tops, axis=0), ("dp", "gx"))
    mixed_rows = mixed_all.reshape(rows_b, head_cols)
    mixed_all_rows, attn_sum = to_rows_a(mixed_rows, out_set, False)
    attn_out = join_features(attn_sum + out_bias)
    after_attn = residual + gate_one * attn_out
    normed_two, inverse_two = normalize(after_attn)
    hidden_two = (normed_two * (1.0 + scale_two) + shift_two).astype(jnp.bfloat16)
    hidden_two_all, up_sum = project_up(split_features(hidden_two), up_set)
    up_pre = up_sum + up_bias
    activ_f32, gelu_slope = gelu_parts(up_pre)
    activation = activ_f32.astype(jnp.bfloat16)
    activ_all, down_sum = to_rows_a(activation, down_set, False)
    mlp_out = join_features(down_sum + down_bias)
    block_out = after_attn + gate_two * mlp_out
    grad_mlp = gate_two * grad_out
    grad_mlp_all, grad_act = from_rows_a(split_features(grad_mlp.astype(jnp.bfloat16)), down_set)
    grad_down_w = lax.dot_general(
        activ_all, grad_mlp_all, (((0,), (0,)), ((), ())), preferred_element_type=jnp.float32
    )
    grad_up_pre = grad_act * gelu_slope
    grad_up_all, grad_hidden_split = to_rows_a(grad_up_pre.astype(jnp.bfloat16), up_set, True)
    grad_hidden_two = join_features(grad_hidden_split)
    grad_up_w = lax.dot_general(
        hidden_two_all, grad_up_all, (((0,), (0,)), ((), ())), preferred_element_type=jnp.float32
    )
    grad_after = grad_out + normalize_back(
        grad_hidden_two * (1.0 + scale_two), normed_two, inverse_two
    )
    grad_attn = gate_one * grad_after
    grad_attn_all, grad_mixed = from_rows_a(split_features(grad_attn.astype(jnp.bfloat16)), out_set)
    grad_out_w = lax.dot_general(
        mixed_all_rows, grad_attn_all, (((0,), (0,)), ((), ())), preferred_element_type=jnp.float32
    )
    grad_mixed_low = grad_mixed.astype(jnp.bfloat16)
    grad_query, grad_key, grad_value = lax.map(
        attend_back,
        (
            split_heads(queries),
            split_heads(keys_here),
            split_heads(values_here),
            split_heads(grad_mixed_low),
            log_sums,
        ),
    )
    grad_query_rows = grad_query.reshape(rows_b, head_cols)
    grad_value_rows = grad_value.reshape(rows_b, head_cols)
    grad_joint = jnp.concatenate(
        [grad_query_rows, grad_key.reshape(rows_b, head_cols), grad_value_rows], axis=1
    )
    grad_joint_all, grad_first_split = to_rows_a(grad_joint.astype(jnp.bfloat16), joint_set, True)
    grad_hidden_one = join_features(grad_first_split)
    grad_joint_w = lax.dot_general(
        hidden_one_all, grad_joint_all, (((0,), (0,)), ((), ())), preferred_element_type=jnp.float32
    )
    grad_input = grad_after + normalize_back(
        grad_hidden_one * (1.0 + scale_one), normed_one, inverse_one
    )
    grad_mod_rows = jnp.stack(
        [
            grad_hidden_one,
            grad_hidden_one * normed_one,
            grad_after * attn_out,
            grad_hidden_two,
            grad_hidden_two * normed_two,
            grad_out * mlp_out,
        ],
        axis=1,
    )
    grad_mod_local = lax.dot_general(
        selector, grad_mod_rows.reshape(rows_c, 6 * width), (((0,), (0,)), ((), ())), precision=HIGH
    ).reshape(latent_count, 6, width)
    gy_index = lax.axis_index("gy")
    up_local = jnp.sum(grad_up_pre, axis=0)
    query_local = jnp.sum(grad_query_rows, axis=0)
    value_local = jnp.sum(grad_value_rows, axis=0)
    grad_mod, down_b_full, out_b_full, up_b_full, query_b_full, value_b_full = lax.psum(
        (
            grad_mod_local,
            jnp.sum(grad_mlp, axis=0),
            jnp.sum(grad_attn, axis=0),
            placed_sum(up_local, gy_index),
            placed_sum(query_local, gy_index),
            placed_sum(value_local, gy_index),
        ),
        ("gx", "gy"),
    )
    bias_start = lax.axis_index("gx") * width_x
    grad_down_b = lax.dynamic_slice_in_dim(down_b_full, bias_start, width_x, 0)
    grad_out_b = lax.dynamic_slice_in_dim(out_b_full, bias_start, width_x, 0)
    grad_up_b = lax.dynamic_slice_in_dim(
        up_b_full, gy_index * up_local.shape[0], up_local.shape[0], 0
    )
    grad_query_b = lax.dynamic_slice_in_dim(query_b_full, gy_index * head_cols, head_cols, 0)
    grad_value_b = lax.dynamic_slice_in_dim(value_b_full, gy_index * head_cols, head_cols, 0)
    grad_silu = jnp.einsum("lmf,emf->le", grad_mod, ada_weight.astype(jnp.float32), precision=HIGH)
    sigmoid_cond = jax.nn.sigmoid(cond_f32)
    grad_condition = grad_silu * sigmoid_cond * (1.0 + cond_f32 * (1.0 - sigmoid_cond))
    grad_ada_w = jnp.einsum("le,lmf->emf", silu_cond.astype(jnp.float32), grad_mod, precision=HIGH)
    grad_ada_b = jnp.sum(grad_mod, axis=0)
    summed = (
        lax.psum(grad_ada_w.astype(jnp.bfloat16), "dp").astype(jnp.float32),
        lax.psum(grad_ada_b.astype(jnp.bfloat16), "dp").astype(jnp.float32),
        lax.psum(grad_joint_w.astype(jnp.bfloat16), "dp").astype(jnp.float32),
        lax.psum(grad_query_b.astype(jnp.bfloat16), "dp").astype(jnp.float32),
        lax.psum(grad_value_b.astype(jnp.bfloat16), "dp").astype(jnp.float32),
        lax.psum(grad_out_w.astype(jnp.bfloat16), "dp").astype(jnp.float32),
        lax.psum(grad_out_b.astype(jnp.bfloat16), "dp").astype(jnp.float32),
        lax.psum(grad_up_w.astype(jnp.bfloat16), "dp").astype(jnp.float32),
        lax.psum(grad_up_b.astype(jnp.bfloat16), "dp").astype(jnp.float32),
        lax.psum(grad_down_w.astype(jnp.bfloat16), "dp").astype(jnp.float32),
        lax.psum(grad_down_b.astype(jnp.bfloat16), "dp").astype(jnp.float32),
    )
    joint_total = summed[2]
    factor = TAU / jnp.maximum(logit_max, TAU)
    root_cols = jnp.repeat(jnp.sqrt(factor), HD)
    clipped_query = query_weight.astype(jnp.float32) * root_cols[None, :]
    clipped_key = key_weight.astype(jnp.float32) * root_cols[None, :]
    clipped_bias = query_bias * root_cols
    return (
        block_out,
        grad_input,
        grad_condition,
        summed[0],
        summed[1],
        joint_total[:, :head_cols],
        joint_total[:, head_cols : 2 * head_cols],
        joint_total[:, 2 * head_cols :],
        summed[3],
        summed[4],
        summed[5],
        summed[6],
        summed[7],
        summed[8],
        summed[9],
        summed[10],
        logit_max,
        clipped_query,
        clipped_key,
        clipped_bias,
    )


def solution(mesh):
    placed = (
        P(("dp", "gy", "gx"), None),
        P("dp", "gy"),
        P("gy", None, None),
        P(),
        P("gx", "gy"),
        P("gx", "gy"),
        P("gx", "gy"),
        P("gy"),
        P("gy"),
        P("gy", "gx"),
        P("gx"),
        P("gx", "gy"),
        P("gy"),
        P("gy", "gx"),
        P("gx"),
        P(("dp", "gy", "gx"), None),
    )
    return jax.shard_map(
        body,
        mesh=mesh,
        in_specs=placed,
        out_specs=(
            P(("dp", "gy", "gx"), None),
            P(("dp", "gy", "gx"), None),
            P("dp", "gy"),
            P("gy", None, None),
            P(),
            P("gx", "gy"),
            P("gx", "gy"),
            P("gx", "gy"),
            P("gy"),
            P("gy"),
            P("gy", "gx"),
            P("gx"),
            P("gx", "gy"),
            P("gy"),
            P("gy", "gx"),
            P("gx"),
            P("gy"),
            P("gx", "gy"),
            P("gx", "gy"),
            P("gy"),
        ),
        check_vma=False,
    )
```

profile of v0, /device:TPU:0, one launch (start us, length us, event | category | flops | bytes accessed | tf_op | source)
XLA Modules:
  0.0 4133.9 jit_solution(12103076477543801030)
XLA Ops:
  11.7 45.3 %all-reduce.7.cloned.1.call-done = f32[8,6,1152]{2,0,1:T(8,128)} async-done(((f32[8,6,1152]{2,0,1:T(8,128)}), f32[8,6,1152]{2,0,1:T(8,128)}) %all-reduce.7.cloned.1.call-update) | async-done | bytes 221200 | tf_op jit(solution)/shard_map/psum | solution.py:191
  70.0 32.5 all_to_all.128
  104.0 54.9 %all-gather.9.cloned.1.call-done = bf16[8192,288]{0,1:T(8,128)(2,1)} async-done(((bf16[2048,288]{0,1:T(8,128)(2,1)}), bf16[8192,288]{0,1:T(8,128)(2,1)}) %all-gather.9.cloned.1.call-update) | async-done | bytes 4718608 | tf_op jit(solution)/shard_map/all_gather | solution.py:30
  159.0 15.2 fusion.90
  174.3 464.9 %reduce-scatter.9.cloned.1.call-done = f32[2048,864]{0,1:T(8,128)} async-done(((f32[8192,864]{0,1:T(8,128)}), f32[2048,864]{0,1:T(8,128)}) %reduce-scatter.9.cloned.1.call-update) | async-done | bytes 7077904 | tf_op jit(solution)/shard_map/reduce_scatter | solution.py:75
  655.8 26.3 while.28
  687.0 91.1 %all-gather.11.cloned.1.call-done = bf16[8192,288]{0,1:T(8,128)(2,1)} async-done(((bf16[2048,288]{0,1:T(8,128)(2,1)}), bf16[8192,288]{0,1:T(8,128)(2,1)}) %all-gather.11.cloned.1.call-update) | async-done | bytes 4718608 | tf_op jit(solution)/shard_map/all_gather | solution.py:34
  778.1 7.2 convolution_convert_fusion.1
  785.3 55.5 %reduce-scatter.11.cloned.1.call-done = bf16[2048,288]{0,1:T(8,128)(2,1)} async-done(((bf16[8192,288]{0,1:T(8,128)(2,1)}), bf16[2048,288]{0,1:T(8,128)(2,1)}) %reduce-scatter.11.cloned.1.call-update) | async-done | bytes 1179664 | tf_op jit(solution)/shard_map/reduce_scatter | solution.py:91
  842.5 32.8 all_to_all.129
  893.1 31.1 all_to_all.130
  927.8 31.1 all_to_all.131
  960.1 20.5 all-gather.13.cloned.1.call-done
  980.6 20.4 fusion.119
  1001.3 38.7 all-gather.17.cloned.1.call-done
  1040.0 20.1 fusion.120
  1060.2 601.5 %reduce-scatter.13.cloned.1.call-done = f32[2048,1152]{1,0:T(8,128)} async-done(((f32[8192,1152]{1,0:T(8,128)}), f32[2048,1152]{1,0:T(8,128)}) %reduce-scatter.13.cloned.1.call-update) | async-done | bytes 9437200 | tf_op jit(solution)/shard_map/reduce_scatter | solution.py:75
  1661.7 622.7 %reduce-scatter.17.cloned.1.call-done = f32[2048,1152]{1,0:T(8,128)} async-done(((f32[8192,1152]{1,0:T(8,128)}), f32[2048,1152]{1,0:T(8,128)}) %reduce-scatter.17.cloned.1.call-update) | async-done | bytes 9437200 | tf_op jit(solution)/shard_map/reduce_scatter | solution.py:75
  2284.4 15.1 fusion.113
  2300.3 322.9 %all-gather.19.cloned.1.call-done = bf16[8192,1152]{1,0:T(8,128)(2,1)} async-done(((bf16[2048,1152]{1,0:T(8,128)(2,1)}), bf16[8192,1152]{1,0:T(8,128)(2,1)}) %all-gather.19.cloned.1.call-update) | async-done | bytes 18874384 | tf_op jit(solution)/shard_map/all_gather | solution.py:34
  2623.2 20.2 convolution_convert_fusion.2
  2643.7 302.6 %all-gather.15.cloned.1.call-done = bf16[8192,1152]{1,0:T(8,128)(2,1)} async-done(((bf16[2048,1152]{1,0:T(8,128)(2,1)}), bf16[8192,1152]{1,0:T(8,128)(2,1)}) %all-gather.15.cloned.1.call-update) | async-done | bytes 18874384 | tf_op jit(solution)/shard_map/all_gather | solution.py:34
  2946.3 20.1 convolution_convert_fusion.3
  2966.4 39.1 reduce-scatter.19.cloned.1.call-done
  3012.5 53.0 %reduce-scatter.15.cloned.1.call-done = bf16[2048,288]{0,1:T(8,128)(2,1)} async-done(((bf16[8192,288]{0,1:T(8,128)(2,1)}), bf16[2048,288]{0,1:T(8,128)(2,1)}) %reduce-scatter.15.cloned.1.call-update) | async-done | bytes 1179664 | tf_op jit(solution)/shard_map/reduce_scatter | solution.py:91
  3083.0 18.3 all-to-all-done.3
  3128.4 31.6 all_to_all.132
  3161.2 55.2 %all-gather.21.cloned.1.call-done = bf16[8192,288]{0,1:T(8,128)(2,1)} async-done(((bf16[2048,288]{0,1:T(8,128)(2,1)}), bf16[8192,288]{0,1:T(8,128)(2,1)}) %all-gather.21.cloned.1.call-update) | async-done | bytes 4718608 | tf_op jit(solution)/shard_map/all_gather | solution.py:30
  3216.4 7.4 fusion.121
  3224.3 160.8 %reduce-scatter.21.cloned.1.call-done = f32[2048,288]{0,1:T(8,128)} async-done(((f32[8192,288]{0,1:T(8,128)}), f32[2048,288]{0,1:T(8,128)}) %reduce-scatter.21.cloned.1.call-update) | async-done | bytes 2359312 | tf_op jit(solution)/shard_map/reduce_scatter | solution.py:75
  3394.6 77.9 %while.29 = (s32[]{:T(128)}, f32[2,1024,4,72]{1,3,2,0:T(8,128)}, bf16[2,1024,4,72]{1,3,2,0:T(8,128)(2,1)}, f32[2,1024,4,72]{1,3,2,0:T(8,128)}, bf16[2,1024,4,72]...) while((s32[]{:T(128)}, f32[2,1024,4,72]{1,3,2,0:T(8,128)}, ...), condition=%wide.region_21.22_spmd, body=%wide.region_19.21_spmd.sunk | while | flops 3070816256 | bytes 176608448 | solution.py:258
  3404.0 9.1 multiply_reduce_fusion.10
  3413.1 10.6 multiply_convert_fusion.3
  3423.7 7.0 fusion.176
  3442.9 9.1 multiply_reduce_fusion.10
  3452.0 10.6 multiply_convert_fusion.3
  3483.7 245.0 %all-gather.23.cloned.1.call-done = bf16[8192,864]{0,1:T(8,128)(2,1)} async-done(((bf16[2048,864]{0,1:T(8,128)(2,1)}), bf16[8192,864]{0,1:T(8,128)(2,1)}) %all-gather.23.cloned.1.call-update) | async-done | bytes 14155792 | tf_op jit(solution)/shard_map/all_gather | solution.py:34
  3728.7 11.8 convolution_convert_fusion
  3740.6 12.6 convolution_convert_fusion.6
  3753.2 42.6 %reduce-scatter.23.cloned.1.call-done = bf16[2048,288]{0,1:T(8,128)(2,1)} async-done(((bf16[8192,288]{0,1:T(8,128)(2,1)}), bf16[2048,288]{0,1:T(8,128)(2,1)}) %reduce-scatter.23.cloned.1.call-update) | async-done | bytes 1179664 | tf_op jit(solution)/shard_map/reduce_scatter | solution.py:91
  3802.8 12.1 convolution_convert_fusion.5
  3818.0 7.1 convolution_convert_fusion.8
  3856.4 15.1 copy.90
  3871.5 10.2 fusion.50
  3881.8 16.3 convolution_convert_fusion.7
  3898.1 89.1 %all-reduce.9.cloned.1.call-done = f32[8,6,1152]{2,0,1:T(8,128)} async-done(((f32[8,6,1152]{2,0,1:T(8,128)}), f32[8,6,1152]{2,0,1:T(8,128)}) %all-reduce.9.cloned.1.call-update) | async-done | bytes 221200 | tf_op jit(solution)/shard_map/psum | solution.py:299
  3997.2 15.1 pmax.7
  4020.9 74.1 %all-reduce = (bf16[1152]{0:T(1024)(128)(2,1)S(1)}, bf16[1152]{0:T(1024)(128)(2,1)S(1)}, bf16[1152]{0:T(1024)(128)(2,1)S(1)}, bf16[4608]{0:T(1024)(128)(2,1)S(1)}, bf16[1152]{0:T(1024)(128)(2,1)S(1)}) all-reduce(f32[1152]{0:T(1024)S(1)} %dynamic_update_slice.31, ...), channel_id=1, replica_groups=mesh['dp'=2,'gx'=4,'gy'=4] {'gx','gy'}, use_global_device_ids=true, to_apply=%region_31.32 | all-reduce | flops 9216 | bytes 55296 | tf_op jit(solution)/shard_map/psum | solution.py:299
  (314 shorter events, 289.1 us)
Async XLA Ops:
  7.2 973.4 %copy-start = (bf16[288,1152]{1,0:T(8,128)(2,1)S(1)}, bf16[288,1152]{1,0:T(8,128)(2,1)}, u32[]{:S(2)}) copy-start(bf16[288,1152]{1,0:T(8,128)(2,1)} %param.31) | copy-start | bytes 1990660
  7.2 49.8 %all-reduce.7.cloned.1.call-start = ((), (), s32[]{:S(2)}) async-start(), calls=%async_computation.16 | async-start | bytes 442368 | tf_op jit(solution)/shard_map/psum | solution.py:191
  10.9 46.1 %copy-start.47 = (f32[6,1152]{1,0:T(8,128)S(1)}, f32[6,1152]{1,0:T(8,128)}, u32[]{:S(2)}) copy-start(f32[6,1152]{1,0:T(8,128)} %param.23) | copy-start | bytes 82948
  10.9 148.1 %all-gather.9.cloned.1.call-start = ((), (), s32[]{:S(2)}) async-start(), calls=%async_computation.17 | async-start | bytes 5898240 | tf_op jit(solution)/shard_map/all_gather | solution.py:30
  11.0 46.0 %copy-start.50 = (s32[512]{0:T(512)}, s32[512]{0:T(512)S(1)}, u32[]{:S(2)}) copy-start(s32[512]{0:T(512)S(1)} %add_select_fusion) | copy-start | bytes 6148
  11.3 52.5 %copy-start.38 = (f32[512]{0:T(512)}, f32[512]{0:T(512)S(1)}, u32[]{:S(2)}) copy-start(f32[512]{0:T(512)S(1)} %broadcast_multiply_fusion.5) | copy-start | bytes 6148
  11.7 52.0 %copy-start.43 = (f32[512]{0:T(512)}, f32[512]{0:T(512)S(1)}, u32[]{:S(2)}) copy-start(f32[512]{0:T(512)S(1)} %add_rsqrt_fusion.1) | copy-start | bytes 6148
  102.6 56.4 %copy-start.30 = (bf16[288,288]{1,0:T(8,128)(2,1)S(1)}, bf16[288,288]{1,0:T(8,128)(2,1)}, u32[]{:S(2)}) copy-start(bf16[288,288]{1,0:T(8,128)(2,1)} %param.25) | copy-start | bytes 497668
  102.6 56.4 %copy-start.32 = (bf16[288,288]{1,0:T(8,128)(2,1)S(1)}, bf16[288,288]{1,0:T(8,128)(2,1)}, u32[]{:S(2)}) copy-start(bf16[288,288]{1,0:T(8,128)(2,1)} %param.24) | copy-start | bytes 497668
  102.6 56.4 %copy-start.36 = (bf16[288,288]{1,0:T(8,128)(2,1)S(1)}, bf16[288,288]{1,0:T(8,128)(2,1)}, u32[]{:S(2)}) copy-start(bf16[288,288]{1,0:T(8,128)(2,1)} %param.26) | copy-start | bytes 497668
  103.8 535.4 %reduce-scatter.9.cloned.1.call-start = ((), (), s32[]{:S(2)}) async-start(), calls=%async_computation.18 | async-start | bytes 35389440 | tf_op jit(solution)/shard_map/reduce_scatter | solution.py:75
  174.2 465.0 %copy-start.53 = (f32[288]{0:T(512)S(1)}, f32[288]{0:T(512)}, u32[]{:S(2)}) copy-start(f32[288]{0:T(512)} %param.27) | copy-start | bytes 3460
  174.2 465.0 %copy-start.55 = (f32[288]{0:T(512)S(1)}, f32[288]{0:T(512)}, u32[]{:S(2)}) copy-start(f32[288]{0:T(512)} %param.28) | copy-start | bytes 3460
  174.2 603.9 %all-gather.11.cloned.1.call-start = ((), (), s32[]{:S(2)}) async-start(), calls=%async_computation.19 | async-start | bytes 5898240 | tf_op jit(solution)/shard_map/all_gather | solution.py:34
  685.1 93.0 %copy-start.26 = (bf16[288,288]{1,0:T(8,128)(2,1)S(1)}, bf16[288,288]{1,0:T(8,128)(2,1)}, u32[]{:S(2)}) copy-start(bf16[288,288]{1,0:T(8,128)(2,1)} %param.29) | copy-start | bytes 497668
  686.5 154.4 %reduce-scatter.11.cloned.1.call-start = ((), (), s32[]{:S(2)}) async-start(), calls=%async_computation.20 | async-start | bytes 5898240 | tf_op jit(solution)/shard_map/reduce_scatter | solution.py:91
  785.3 55.6 %copy-start.56 = (f32[288]{0:T(512)S(1)}, f32[288]{0:T(512)}, u32[]{:S(2)}) copy-start(f32[288]{0:T(512)} %param.30) | copy-start | bytes 3460
  785.3 195.3 %all-gather.13.cloned.1.call-start = ((), (), s32[]{:S(2)}) async-start(), calls=%async_computation.21 | async-start | bytes 5898240 | tf_op jit(solution)/shard_map/all_gather | solution.py:30
  883.1 7.6 copy-start.6
  883.1 2236.2 %copy-start.40 = (f32[512]{0:T(512)}, f32[512]{0:T(512)S(1)}, u32[]{:S(2)}) copy-start(f32[512]{0:T(512)S(1)} %broadcast_multiply_fusion.4) | copy-start | bytes 6148
  885.6 2233.7 %copy-start.45 = (f32[512]{0:T(512)}, f32[512]{0:T(512)S(1)}, u32[]{:S(2)}) copy-start(f32[512]{0:T(512)S(1)} %add_rsqrt_fusion) | copy-start | bytes 6148
  925.4 114.6 %all-gather.17.cloned.1.call-start = ((), (), s32[]{:S(2)}) async-start(), calls=%async_computation.25 | async-start | bytes 5898240 | tf_op jit(solution)/shard_map/all_gather | solution.py:30
  960.1 701.7 %reduce-scatter.13.cloned.1.call-start = ((), (), s32[]{:S(2)}) async-start(), calls=%async_computation.22 | async-start | bytes 47185920 | tf_op jit(solution)/shard_map/reduce_scatter | solution.py:75
  1001.0 1283.4 %reduce-scatter.17.cloned.1.call-start = ((), (), s32[]{:S(2)}) async-start(), calls=%async_computation.26 | async-start | bytes 47185920 | tf_op jit(solution)/shard_map/reduce_scatter | solution.py:75
  1060.1 1224.3 %copy-start.52 = (f32[1152]{0:T(1024)S(1)}, f32[1152]{0:T(1024)}, u32[]{:S(2)}) copy-start(f32[1152]{0:T(1024)} %param.32) | copy-start | bytes 13828
  1060.1 1563.1 %all-gather.19.cloned.1.call-start = ((), (), s32[]{:S(2)}) async-start(), calls=%async_computation.27 | async-start | bytes 23592960 | tf_op jit(solution)/shard_map/all_gather | solution.py:34
  2299.5 646.7 %all-gather.15.cloned.1.call-start = ((), (), s32[]{:S(2)}) async-start(), calls=%async_computation.23 | async-start | bytes 23592960 | tf_op jit(solution)/shard_map/all_gather | solution.py:34
  2300.3 705.2 %reduce-scatter.19.cloned.1.call-start = ((), (), s32[]{:S(2)}) async-start(), calls=%async_computation.28 | async-start | bytes 5898240 | tf_op jit(solution)/shard_map/reduce_scatter | solution.py:91
  2643.4 302.9 %copy-start.34 = (bf16[1152,288]{0,1:T(8,128)(2,1)S(1)}, bf16[1152,288]{0,1:T(8,128)(2,1)}, u32[]{:S(2)}) copy-start(bf16[1152,288]{0,1:T(8,128)(2,1)} %param.33) | copy-start | bytes 1990660
  2643.4 422.1 %reduce-scatter.15.cloned.1.call-start = ((), (), s32[]{:S(2)}) async-start(), calls=%async_computation.24 | async-start | bytes 5898240 | tf_op jit(solution)/shard_map/reduce_scatter | solution.py:91
  3005.5 60.0 %copy-start.57 = (f32[288]{0:T(512)S(1)}, f32[288]{0:T(512)}, u32[]{:S(2)}) copy-start(f32[288]{0:T(512)} %param.34) | copy-start | bytes 3460
  3007.9 60.2 %all-to-all-start.5 = ((bf16[4,512,288]{1,2,0:T(8,128)(2,1)}), bf16[4,512,288]{1,2,0:T(8,128)(2,1)}, u32[]{:S(2)}, u32[]{:S(2)}) async-start(bf16[4,512,288]{1,2,0:T(8,128)(2,1)} %bitcast.314), calls=%async_computation.11 | async-start | bytes 2359296 | tf_op jit(solution)/shard_map/all_to_all | solution.py:42
  3068.2 33.1 all-to-all-start.3
  3072.8 143.6 %all-gather.21.cloned.1.call-start = ((), (), s32[]{:S(2)}) async-start(), calls=%async_computation.29 | async-start | bytes 5898240 | tf_op jit(solution)/shard_map/all_gather | solution.py:30
  3161.2 223.9 %reduce-scatter.21.cloned.1.call-start = ((), (), s32[]{:S(2)}) async-start(), calls=%async_computation.30 | async-start | bytes 11796480 | tf_op jit(solution)/shard_map/reduce_scatter | solution.py:75
  3223.8 504.9 %all-gather.23.cloned.1.call-start = ((), (), s32[]{:S(2)}) async-start(), calls=%async_computation.31 | async-start | bytes 17694720 | tf_op jit(solution)/shard_map/all_gather | solution.py:34
  3483.6 245.1 %copy-start.31 = (bf16[288,288]{1,0:T(8,128)(2,1)S(1)}, bf16[288,288]{1,0:T(8,128)(2,1)}, u32[]{:S(2)}) copy-start(bf16[288,288]{1,0:T(8,128)(2,1)} %param.25) | copy-start | bytes 497668
  3483.6 245.1 %copy-start.33 = (bf16[288,288]{1,0:T(8,128)(2,1)S(1)}, bf16[288,288]{1,0:T(8,128)(2,1)}, u32[]{:S(2)}) copy-start(bf16[288,288]{1,0:T(8,128)(2,1)} %param.24) | copy-start | bytes 497668
  3483.6 245.1 %copy-start.37 = (bf16[288,288]{1,0:T(8,128)(2,1)S(1)}, bf16[288,288]{1,0:T(8,128)(2,1)}, u32[]{:S(2)}) copy-start(bf16[288,288]{1,0:T(8,128)(2,1)} %param.26) | copy-start | bytes 497668
  3483.7 312.2 %reduce-scatter.23.cloned.1.call-start = ((), (), s32[]{:S(2)}) async-start(), calls=%async_computation.32 | async-start | bytes 5898240 | tf_op jit(solution)/shard_map/reduce_scatter | solution.py:91
  3798.2 33.0 all-to-all-start.7
  3802.8 184.3 %all-reduce.9.cloned.1.call-start = ((), (), s32[]{:S(2)}) async-start(), calls=%async_computation.33 | async-start | bytes 442368 | tf_op jit(solution)/shard_map/psum | solution.py:299
  3856.4 15.1 copy-start.51
  3881.7 105.4 %copy-start.42 = (bf16[8,288]{1,0:T(8,128)(2,1)S(1)}, bf16[8,288]{1,0:T(8,128)(2,1)}, u32[]{:S(2)}) copy-start(bf16[8,288]{1,0:T(8,128)(2,1)} %param.21) | copy-start | bytes 13828
  3881.8 234.2 %all-reduce.11.cloned.1.call-start = ((), (), s32[]{:S(2)}) async-start(), calls=%async_computation.34 | async-start | bytes 12091392 | tf_op jit(solution)/shard_map/psum | solution.py:324
  3994.1 18.4 copy-start.54
  3994.1 19.9 copy-start.48
  4012.3 8.6 copy-start.60
  (41 other events, 165.1 us)
Sparse Core Ops, SparseCore 0:
  11.5 45.4 all-reduce.6
  103.9 55.0 all-gather.8
  174.4 464.7 reduce-scatter.8
  686.6 91.4 all-gather.10
  785.4 55.3 reduce-scatter.10
  925.5 55.0 all-gather.12
  983.0 56.9 all-gather.16
  1042.4 619.3 reduce-scatter.12
  1664.1 620.2 reduce-scatter.16
  2299.7 323.5 all-gather.18
  2624.8 321.4 all-gather.14
  2949.7 55.8 reduce-scatter.18
  3008.5 56.9 reduce-scatter.14
  3161.3 55.0 all-gather.20
  3223.9 161.1 reduce-scatter.20
  3483.8 244.8 all-gather.22
  3740.7 55.1 reduce-scatter.22
  3881.9 105.2 all-reduce.8
  3993.5 31.6 all-reduce.10
where the time goes:
time: 4140 us; the launch traced here: 4130 us
  waiting for transfers between devices  3330 us (80%)
  matrix products  270 us (7%)
  blocking collectives  252 us (6%)
  other arithmetic  137 us (3%)
  local copies, waits for them, and re-layouts  113 us (3%)
    reduce_scatter x4, waiting for transfers between devices, sum_over_gx(): lax.psum_scatter(partial_term(jnp.int32(0), full_rows.shape[0] // lax.axi...  1850 us
    all_gather x4, waiting for transfers between devices, gather_gx(): return lax.all_gather(rows_in, 'gx', axis=0, tiled=True)  962 us
    reduce_scatter x4, waiting for transfers between devices, sum_over_gy(): lax.psum_scatter(partial_term(jnp.int32(0), full_rows.shape[0] // lax.axi...  190 us
    all_gather x4, waiting for transfers between devices, gather_gy(): return lax.all_gather(rows_in, 'gy', axis=0, tiled=True)  169 us
    all_to_all x4, blocking collectives, split_features(): lax.all_to_all(rows_low, 'gx', split_axis=1, concat_axis=0, tiled=True)  126 us
    dot_general x8, matrix products, partial_term(): lax.dot_general(full_rows, bundle[0], (contract_dims, ((), ())), preferre...  122 us
    psum x1, waiting for transfers between devices, body(): lax.psum((grad_mod_local, jnp.sum(grad_mlp, axis=0), jnp.sum(grad_attn, a...  89.1 us
  transfers between devices with their start and end apart: 22, of which 20 were waited for; matrix products, arithmetic and copies ran while one was open for 4% of the time, Pallas kernels for 0%

commit v1 on v0

v1 whole, which is shorter than its diff:
```python
import math

import jax
import jax.numpy as jnp
from jax import lax
from jax.sharding import PartitionSpec as P

HD = 72
SEQ = 1024
TAU = 8

EPS = 1e-06
GELU_ROOT = 0.7978845608028654
GELU_CUBE = 0.044715
BF = jnp.bfloat16
F32 = jnp.float32
EVERY = ("gy", "gx", "dp")


def gelu_parts(inputs):
    inner_arg = GELU_ROOT * (inputs + GELU_CUBE * inputs * inputs * inputs)
    tangent = jnp.tanh(inner_arg)
    output = 0.5 * inputs * (1.0 + tangent)
    slope_rows = 0.5 * (1.0 + tangent) + 0.5 * inputs * (1.0 - tangent * tangent) * GELU_ROOT * (
        1.0 + 3.0 * GELU_CUBE * inputs * inputs
    )
    return (output, slope_rows)


def normalize(rows_in):
    mean_row = jnp.mean(rows_in, axis=1, keepdims=True)
    centred = rows_in - mean_row
    inverse = lax.rsqrt(jnp.mean(centred * centred, axis=1, keepdims=True) + EPS)
    return (centred * inverse, inverse)


def normalize_back(grad_hat, normed, inverse):
    grad_mean = jnp.mean(grad_hat, axis=1, keepdims=True)
    cross_mean = jnp.mean(grad_hat * normed, axis=1, keepdims=True)
    return inverse * (grad_hat - grad_mean - normed * cross_mean)


def gather_weight(shard):
    part = shard.shape[0] // lax.axis_size("dp")
    mine = lax.dynamic_slice_in_dim(shard, lax.axis_index("dp") * part, part, 0)
    full = lax.all_gather(mine, EVERY, axis=0, tiled=True)
    return full.reshape(lax.axis_size("gy"), -1, shard.shape[1])


def scatter_grad(blocks):
    flat = blocks.reshape(-1, blocks.shape[2])
    mine = lax.psum_scatter(flat, EVERY, scatter_dimension=0, tiled=True)
    return lax.all_gather(mine, "dp", axis=0, tiled=True).astype(F32)


def dot(spec, left, right):
    return jnp.einsum(spec, left, right, preferred_element_type=F32)


def attend_group(packed):
    queries, keys_in, values_in = packed
    scores = dot("qhd,khd->hqk", queries, keys_in) * (1.0 / math.sqrt(HD))
    top_row = jnp.max(scores, axis=2)
    weights = jnp.exp(scores - top_row[:, :, None])
    denominator = jnp.sum(weights, axis=2)
    prob_rows = (weights / denominator[:, :, None]).astype(BF)
    mixed_rows = dot("hqk,khd->qhd", prob_rows, values_in)
    return (mixed_rows.astype(BF), top_row + jnp.log(denominator), jnp.max(top_row, axis=1))


def attend_back(packed):
    queries, keys_in, values_in, grad_mixed, log_sums = packed
    scores = dot("qhd,khd->hqk", queries, keys_in) * (1.0 / math.sqrt(HD))
    prob_rows = jnp.exp(scores - log_sums[:, :, None])
    prob_low = prob_rows.astype(BF)
    grad_probs = dot("qhd,khd->hqk", grad_mixed, values_in)
    row_delta = jnp.sum(grad_probs * prob_rows, axis=2)
    grad_scores = (prob_rows * (grad_probs - row_delta[:, :, None])).astype(BF)
    grad_query = dot("hqk,khd->qhd", grad_scores, keys_in) * (1.0 / math.sqrt(HD))
    grad_key = dot("hqk,qhd->khd", grad_scores, queries) * (1.0 / math.sqrt(HD))
    grad_value = dot("hqk,qhd->khd", prob_low, grad_mixed)
    return (grad_query, grad_key, grad_value)


def body(
    latents_in,
    condition,
    ada_weight,
    ada_bias,
    query_weight,
    key_weight,
    value_weight,
    query_bias,
    value_bias,
    out_weight,
    out_bias,
    up_weight,
    up_bias,
    down_weight,
    down_bias,
    grad_out,
):
    rows, width = latents_in.shape
    latent_count = condition.shape[0]
    cols = query_weight.shape[1]
    width_x = out_bias.shape[0]
    size_gx, size_gy = lax.axis_size("gx"), lax.axis_size("gy")
    at_gx, at_gy = lax.axis_index("gx"), lax.axis_index("gy")
    span = SEQ // rows
    heads_here = cols // HD

    def shift_pairs(shift):
        return [(i, i // span * span + (i + shift) % span) for i in range(size_gx)]

    context = jnp.concatenate(
        [latents_in] + [lax.ppermute(latents_in, "gx", shift_pairs(s)) for s in range(1, span)], axis=0
    )

    cond_f32 = condition.astype(F32)
    silu_cond = jax.nn.silu(cond_f32).astype(BF)
    mod_part = dot("le,emf->lmf", silu_cond, ada_weight)
    mod_group = lax.psum_scatter(mod_part, "gy", scatter_dimension=0, tiled=True)
    mod_own = lax.dynamic_index_in_dim(mod_group, at_gx // span, 0, keepdims=False) + ada_bias
    shift_one, scale_one, gate_one, shift_two, scale_two, gate_two = [
        mod_own[m : m + 1] for m in range(6)
    ]

    wide = lax.all_gather(
        jnp.concatenate([out_bias, down_bias, query_bias, value_bias, up_bias])[None],
        ("gy", "gx"),
        axis=0,
        tiled=True,
    )
    out_bias_all = wide[:size_gx, :width_x].reshape(1, width)
    down_bias_all = wide[:size_gx, width_x : 2 * width_x].reshape(1, width)
    rest = wide[::size_gx, 2 * width_x :]
    query_bias_all = rest[:, None, :cols]
    value_bias_all = rest[:, None, cols : 2 * cols]
    up_bias_all = rest[:, None, 2 * cols :]

    attn_w = gather_weight(
        jnp.concatenate([query_weight, key_weight, value_weight, out_weight.T], axis=1)
    )
    up_w = gather_weight(up_weight)
    down_w = gather_weight(down_weight.T)
    query_w, key_w, value_w, out_w = [attn_w[:, :, i * cols : (i + 1) * cols] for i in range(4)]

    normed_ctx, inverse_ctx = normalize(context.astype(F32))
    hidden_ctx = (normed_ctx * (1.0 + scale_one) + shift_one).astype(BF)
    normed_one, inverse_one, hidden_one = normed_ctx[:rows], inverse_ctx[:rows], hidden_ctx[:rows]
    residual = latents_in.astype(F32)
    queries = (dot("rd,gdn->grn", hidden_one, query_w) + query_bias_all).astype(BF)
    keys_ctx = dot("rd,gdn->grn", hidden_ctx, key_w).astype(BF)
    values_ctx = (dot("rd,gdn->grn", hidden_ctx, value_w) + value_bias_all).astype(BF)

    def split_heads(matrix_rows):
        return matrix_rows.reshape(size_gy, -1, heads_here, HD)

    mixed, log_sums, head_tops = lax.map(
        attend_group, (split_heads(queries), split_heads(keys_ctx), split_heads(values_ctx))
    )
    mixed = mixed.reshape(size_gy, rows, cols)
    top_all = lax.pmax(head_tops.reshape(-1), ("dp", "gx", "gy"))
    logit_max = lax.dynamic_slice_in_dim(top_all, at_gy * heads_here, heads_here, 0)

    attn_out = dot("grn,gdn->rd", mixed, out_w) + out_bias_all
    after_attn = residual + gate_one * attn_out
    normed_two, inverse_two = normalize(after_attn)
    hidden_two = (normed_two * (1.0 + scale_two) + shift_two).astype(BF)
    up_pre = dot("rd,gdn->grn", hidden_two, up_w) + up_bias_all
    activ_f32, gelu_slope = gelu_parts(up_pre)
    activation = activ_f32.astype(BF)
    mlp_out = dot("grn,gdn->rd", activation, down_w) + down_bias_all
    block_out = after_attn + gate_two * mlp_out

    grad_mlp = gate_two * grad_out
    grad_mlp_low = grad_mlp.astype(BF)
    grad_act = dot("rd,gdn->grn", grad_mlp_low, down_w)
    grad_down_w = scatter_grad(dot("rd,grn->gdn", grad_mlp_low, activation).astype(BF))
    grad_up_pre = grad_act * gelu_slope
    grad_up_low = grad_up_pre.astype(BF)
    grad_hidden_two = dot("grn,gdn->rd", grad_up_low, up_w)
    grad_up_w = scatter_grad(dot("rd,grn->gdn", hidden_two, grad_up_low).astype(BF))
    grad_after = grad_out + normalize_back(
        grad_hidden_two * (1.0 + scale_two), normed_two, inverse_two
    )
    grad_attn = gate_one * grad_after
    grad_attn_low = grad_attn.astype(BF)
    grad_mixed_low = dot("rd,gdn->grn", grad_attn_low, out_w).astype(BF)
    grad_out_w = dot("rd,grn->gdn", grad_attn_low, mixed).astype(BF)
    grad_query, grad_key, grad_value = lax.map(
        attend_back,
        (
            split_heads(queries),
            split_heads(keys_ctx),
            split_heads(values_ctx),
            split_heads(grad_mixed_low),
            log_sums,
        ),
    )
    grad_query = grad_query.reshape(size_gy, rows, cols)
    grad_value = grad_value.reshape(size_gy, SEQ, cols)
    grad_query_low = grad_query.astype(BF)
    grad_key_low = grad_key.reshape(size_gy, SEQ, cols).astype(BF)
    grad_value_low = grad_value.astype(BF)
    grad_ctx = dot("grn,gdn->rd", grad_key_low, key_w) + dot("grn,gdn->rd", grad_value_low, value_w)
    grad_hidden_one = grad_ctx[:rows] + dot("grn,gdn->rd", grad_query_low, query_w)
    for s in range(1, span):
        back = [(b, a) for a, b in shift_pairs(s)]
        grad_hidden_one += lax.ppermute(
            grad_ctx[s * rows : (s + 1) * rows].astype(BF), "gx", back
        ).astype(F32)
    grad_attn_w = scatter_grad(
        jnp.concatenate(
            [
                dot("rd,grn->gdn", hidden_one, grad_query_low).astype(BF),
                dot("rd,grn->gdn", hidden_ctx, grad_key_low).astype(BF),
                dot("rd,grn->gdn", hidden_ctx, grad_value_low).astype(BF),
                grad_out_w,
            ],
            axis=2,
        )
    )
    grad_input = grad_after + normalize_back(
        grad_hidden_one * (1.0 + scale_one), normed_one, inverse_one
    )

    def rows_sum(values):
        return jnp.sum(values, axis=-2).reshape(-1, width)

    tail_part = jnp.concatenate(
        [
            rows_sum(grad_hidden_one),
            rows_sum(grad_hidden_one * normed_one),
            rows_sum(grad_after * attn_out),
            rows_sum(grad_hidden_two),
            rows_sum(grad_hidden_two * normed_two),
            rows_sum(grad_out * mlp_out),
            rows_sum(grad_query),
            rows_sum(grad_value),
        ],
        axis=0,
    )
    tail_all = lax.all_gather(tail_part.astype(BF), ("dp", "gy", "gx"), axis=0).astype(F32)
    grad_mod = jnp.sum(tail_all[:, :6].reshape(-1, span, 6, width), axis=1)
    grad_ada_b = jnp.sum(grad_mod, axis=0)
    tail_sum = jnp.sum(tail_all[:, 6:], axis=0)
    grad_query_b = lax.dynamic_slice_in_dim(tail_sum[0], at_gy * cols, cols, 0)
    grad_value_b = lax.dynamic_slice_in_dim(tail_sum[1], at_gy * cols, cols, 0)
    early_sum = lax.psum(
        jnp.concatenate([rows_sum(grad_mlp), rows_sum(grad_attn), rows_sum(grad_up_pre)], axis=0),
        ("gx", "gy", "dp"),
    )
    grad_down_b = lax.dynamic_slice_in_dim(early_sum[0], at_gx * width_x, width_x, 0)
    grad_out_b = lax.dynamic_slice_in_dim(early_sum[1], at_gx * width_x, width_x, 0)
    up_cols = up_bias.shape[0]
    grad_up_b = lax.dynamic_slice_in_dim(early_sum[2:].reshape(-1), at_gy * up_cols, up_cols, 0)

    mod_here = lax.dynamic_slice_in_dim(
        grad_mod, lax.axis_index("dp") * latent_count, latent_count, 0
    ).astype(BF)
    silu_every = lax.all_gather(silu_cond, "dp", axis=0, tiled=True)
    grad_ada_w = dot("le,lmf->emf", silu_every, grad_mod.astype(BF))
    grad_silu = dot("lmf,emf->le", mod_here, ada_weight)
    sigmoid_cond = jax.nn.sigmoid(cond_f32)
    grad_condition = grad_silu * sigmoid_cond * (1.0 + cond_f32 * (1.0 - sigmoid_cond))

    factor = TAU / jnp.maximum(logit_max, TAU)
    root_cols = jnp.repeat(jnp.sqrt(factor), HD)
    clipped_query = query_weight.astype(F32) * root_cols[None, :]
    clipped_key = key_weight.astype(F32) * root_cols[None, :]
    clipped_bias = query_bias * root_cols
    return (
        block_out,
        grad_input,
        grad_condition,
        grad_ada_w,
        grad_ada_b,
        grad_attn_w[:, :cols],
        grad_attn_w[:, cols : 2 * cols],
        grad_attn_w[:, 2 * cols : 3 * cols],
        grad_query_b,
        grad_value_b,
        grad_attn_w[:, 3 * cols :].T,
        grad_out_b,
        grad_up_w,
        grad_up_b,
        grad_down_w.T,
        grad_down_b,
        logit_max,
        clipped_query,
        clipped_key,
        clipped_bias,
    )


def solution(mesh):
    placed = (
        P(("dp", "gy", "gx"), None),
        P("dp", "gy"),
        P("gy", None, None),
        P(),
        P("gx", "gy"),
        P("gx", "gy"),
        P("gx", "gy"),
        P("gy"),
        P("gy"),
        P("gy", "gx"),
        P("gx"),
        P("gx", "gy"),
        P("gy"),
        P("gy", "gx"),
        P("gx"),
        P(("dp", "gy", "gx"), None),
    )
    return jax.shard_map(
        body,
        mesh=mesh,
        in_specs=placed,
        out_specs=(
            P(("dp", "gy", "gx"), None),
            P(("dp", "gy", "gx"), None),
            P("dp", "gy"),
            P("gy", None, None),
            P(),
            P("gx", "gy"),
            P("gx", "gy"),
            P("gx", "gy"),
            P("gy"),
            P("gy"),
            P("gy", "gx"),
            P("gx"),
            P("gx", "gy"),
            P("gy"),
            P("gy", "gx"),
            P("gx"),
            P("gy"),
            P("gx", "gy"),
            P("gx", "gy"),
            P("gy"),
        ),
        check_vma=False,
    )
```

time: 4140 us -> 921 us (0.22)
  waiting for transfers between devices: 3330 us -> 289 us
  other arithmetic: 137 us -> 42.6 us
  local copies, waits for them, and re-layouts: 113 us -> 38.9 us
    reduce_scatter x8 -> x3, waiting for transfers between devices: 2040 us -> 190 us  [scatter_grad(): mine = lax.psum_scatter(flat, EVERY, scatter_dimension=0, tiled=True)]
    all_gather x8 -> x3, waiting for transfers between devices: 1130 us -> 99.4 us  [gather_weight(): full = lax.all_gather(mine, EVERY, axis=0, tiled=True)]
    all_gather x0 -> x6, blocking collectives: none -> 161 us  [the longest x1 76.2 us: body(): lax.all_gather(jnp.concatenate([out_bias, down_bias, query_bias, value_bi...]
    all_to_all x5 -> x0, blocking collectives: 159 us -> none  [the longest x4 126 us: split_features(): lax.all_to_all(rows_low, 'gx', split_axis=1, concat_axis=0, tiled=True)]
    psum x3 -> x0, waiting for transfers between devices: 134 us -> none  [the longest x1 89.1 us: body(): lax.psum((grad_mod_local, jnp.sum(grad_mlp, axis=0), jnp.sum(grad_attn, a...]
    pmax x1, blocking collectives: 15.1 us -> 72.6 us  [body(): top_all = lax.pmax(head_tops.reshape(-1), ('dp', 'gx', 'gy'))]
    convert_element_type x23 -> x8, other arithmetic: 63.9 us -> 9.51 us  [the longest x4 8.19 us: attend_back(): grad_scores = (prob_rows * (grad_probs - row_delta[:, :, None])).astype(BF)]
    dot_general x31 -> x49, matrix products: 270 us -> 243 us  [dot(): return jnp.einsum(spec, left, right, preferred_element_type=F32)]
  transfers between devices with their start and end apart: 22 -> 9, of which waited for: 20 -> 5; matrix products, arithmetic and copies ran while one was open for 4% -> 18% of each run, Pallas kernels for 0% -> 0%
where the time goes in v1:
time: 921 us; the launch traced here: 911 us
  waiting for transfers between devices  289 us (31%)
  blocking collectives  274 us (30%)
  matrix products  243 us (26%)
  other arithmetic  42.6 us (5%)
  local copies, waits for them, and re-layouts  38.9 us (4%)
  between operations  17.3 us (2%)
    dot_general x49, matrix products, dot(): return jnp.einsum(spec, left, right, preferred_element_type=F32)  243 us
    reduce_scatter x3, waiting for transfers between devices, scatter_grad(): mine = lax.psum_scatter(flat, EVERY, scatter_dimension=0, tiled=True)  190 us
    all_gather x3, waiting for transfers between devices, gather_weight(): full = lax.all_gather(mine, EVERY, axis=0, tiled=True)  99.4 us
    all_gather x1, blocking collectives, body(): lax.all_gather(jnp.concatenate([out_bias, down_bias, query_bias, value_bi...  76.2 us
    all_gather x1, blocking collectives, body(): lax.all_gather(tail_part.astype(BF), ('dp', 'gy', 'gx'), axis=0).astype(F32)  75.3 us
    pmax x1, blocking collectives, body(): top_all = lax.pmax(head_tops.reshape(-1), ('dp', 'gx', 'gy'))  72.6 us
    psum x1, blocking collectives, body(): lax.psum(jnp.concatenate([rows_sum(grad_mlp), rows_sum(grad_attn), rows_s...  40.2 us
  transfers between devices with their start and end apart: 9, of which 5 were waited for; matrix products, arithmetic and copies ran while one was open for 18% of the time, Pallas kernels for 0%

profile of v1, /device:TPU:0, one launch (start us, length us, event | category | flops | bytes accessed | tf_op | source)
XLA Modules:
  0.0 911.0 jit_solution(15935986418460415562)
XLA Ops:
  8.1 3.6 fusion.118
  16.2 3.1 collective-permute-start
  20.7 76.2 %all-gather.1 = f32[16,1,2304]{2,1,0:T(1,128)S(1)} all-gather(f32[1,1,2304]{2,1,0:T(1,128)S(1)} %reshape.338), channel_id=2, replica_groups=mesh['dp'=2,'gx'=4,'gy'=4] {'gy','gx'}, dimensions={0}, use_global_device_ids=true | all-gather | bytes 156672 | tf_op jit(solution)/shard_map/all_gather | solution.py:128
  99.7 3.9 fusion.58
  103.7 7.8 all-gather.6.cloned.1.call-done
  111.4 5.7 add_convert_fusion.3
  117.2 8.8 fusion.87
  126.0 7.3 add_convert_fusion
  133.3 42.5 %while.28 = (s32[]{:T(128)}, bf16[4,512,4,72]{1,3,2,0:T(8,128)(2,1)}, f32[4,4,512]{2,1,0:T(4,128)S(1)}, f32[4,4]{1,0:T(4,128)}, bf16[4,1024,4,72]{1,3,2,0:T(8,12...) while((s32[]{:T(128)}, ...), condition=%wide.region_7.8_spmd, body=%wide.region_3.7_spmd.sunk | while | flops 625096704 | bytes 27003036 | solution.py:159
  136.1 2.7 multiply_reduce_fusion.18
  138.9 4.1 fusion.175
  146.6 2.7 multiply_reduce_fusion.18
  149.4 4.1 fusion.175
  157.1 2.7 multiply_reduce_fusion.18
  159.9 4.1 fusion.175
  167.6 2.7 multiply_reduce_fusion.18
  170.4 4.1 fusion.175
  175.8 7.7 fusion.132
  185.3 14.9 %all-gather.8.cloned.1.call-done = bf16[4608,1152]{1,0:T(8,128)(2,1)} async-done(((bf16[144,1152]{1,0:T(8,128)(2,1)}), bf16[4608,1152]{1,0:T(8,128)(2,1)}) %all-gather.8.cloned.1.call-update) | async-done | bytes 10616848 | tf_op jit(solution)/shard_map/all_gather | solution.py:46
  200.2 12.2 %fusion.129 = f32[4,1152,512]{1,2,0:T(8,128)} fusion(bf16[4,1152,1152]{2,1,0:T(8,128)(2,1)} %bitcast.280, f32[512,1152]{1,0:T(8,128)} %copy-done.7, f32[1152]{0:T(1024)S(1)} %get-tuple-element.229, f32[1152]{0:T(1024)S(1)} %get-tuple-element.230, f32[512]{0:T(512)S(1)} %add_rsqrt_fusion.1, f32[512]{0:T(512)S(1)} %broadcast_multiply_fusion.5), kind=kOutput, calls=%fused_computation.199 | convolution fusion | flops 5438767104 | bytes 22426624 | tf_op jit(solution)/shard_map/rd,gdn->grn/dot_general | solution.py:57
  212.3 76.7 %all-gather.10.cloned.1.call-done = bf16[4608,1152]{1,0:T(8,128)(2,1)} async-done(((bf16[144,1152]{1,0:T(8,128)(2,1)}), bf16[4608,1152]{1,0:T(8,128)(2,1)}) %all-gather.10.cloned.1.call-update) | async-done | bytes 10616848 | tf_op jit(solution)/shard_map/all_gather | solution.py:46
  289.0 16.1 %fusion.140 = (f32[4,1152]{1,0:T(4,128)}, bf16[4,512,1152]{2,1,0:T(8,128)(2,1)S(1)}) fusion(f32[4,1152,512]{1,2,0:T(8,128)} %fusion.129, f32[4,1152]{1,0:T(4,128)S(1)} %slice.144, bf16[4,1152,1152]{2,1,0:T(8,128)(2,1)} %bitcast.278, f32[512,1152]{1,0:T(8,128)} %param.35, f32[1152]{0:T(1024)S(1)} %get-tuple-element.228), kind=kOutput, calls=%fused_computation.209 | convolution fusion | flops 5486538240 | bytes 27173376 | tf_op jit(solution)/shard_map/rd,gdn->grn/dot_general | solution.py:57
  305.1 14.3 %multiply_reduce_fusion.4 = (bf16[1152]{0:T(1024)(128)(2,1)}, f32[512]{0:T(512)S(1)}, f32[512]{0:T(512)S(1)}, bf16[1152]{0:T(1024)(128)(2,1)}, f32[512,1152]{1,0:T(8,128)}) fusion(f32[512,1152]{1,0:T(8,128)S(1)} %copy-done.8, f32[512]{0:T(512)S(1)} %add_rsqrt_fusion.1, f32[512]{0:T(512)S(1)} %broadcast_multiply_fusion.5, f32[1152]{0:T(1024)S(1)} %get-tuple-element.230, ...), kind=kOutput, calls=%fused_computation.114 | convolution fusion | flops 5441123328 | bytes 20071424 | tf_op jit(solution)/shard_map/grn,gdn->rd/dot_general | solution.py:57
  319.4 17.1 %multiply_reduce_fusion.11 = (f32[1152]{0:T(1024)}, bf16[1152]{0:T(1024)(128)(2,1)}, f32[512,1152]{1,0:T(8,128)}, bf16[1152]{0:T(1024)(128)(2,1)}, f32[1152]{0:T(1024)}, /*index=5*/f32[512,1152]{1,0:T(8,128)}) fusion(f32[512,1152]{1,0:T(8,128)} %param.35, f32[1152]{0:T(1024)S(1)} %get-tuple-element.228, f32[512,1152]{1,0:T(8,128)} %copy-done.7, ...), kind=kOutput, calls=%fused_computation.131 | convolution fusion | flops 5470613504 | bytes 34268672 | tf_op jit(solution)/shard_map/grn,gdn->rd/dot_general | solution.py:57
  336.5 7.2 fusion.98
  343.8 3.2 fusion.64
  347.0 59.8 %while.29 = (s32[]{:T(128)}, f32[4,512,4,72]{1,3,2,0:T(8,128)}, bf16[4,1024,4,72]{1,3,2,0:T(8,128)(2,1)}, f32[4,1024,4,72]{1,3,2,0:T(8,128)}, bf16[4,1024,4,72]{...) while((s32[]{:T(128)}, f32[4,512,4,72]{1,3,2,0:T(8,128)}, ...), condition=%wide.region_14.15_spmd, body=%wide.region_12.14_spmd.sunk | while | flops 1535555584 | bytes 92468416 | solution.py:191
  352.4 3.6 multiply_reduce_fusion.19
  367.2 3.6 multiply_reduce_fusion.19
  382.1 3.6 multiply_reduce_fusion.19
  397.0 3.6 multiply_reduce_fusion.19
  406.8 4.6 fusion.133
  415.2 3.4 fusion.62
  418.7 3.4 fusion.61
  422.1 5.1 pad_maximum_fusion
  427.3 15.6 %copy.80 = bf16[4,1152,1152]{2,1,0:T(8,128)(2,1)} copy(bf16[4,1152,1152]{1,2,0:T(8,128)(2,1)} %pad_maximum_fusion) | data formatting | bytes 21233664 | tf_op jit(solution)/shard_map/concatenate | solution.py:214
  442.9 12.3 %convolution_convert_fusion = bf16[4,1152,1152]{1,2,0:T(8,128)(2,1)} fusion(f32[512,1152]{1,0:T(8,128)} %param.35, f32[1152]{0:T(1024)S(1)} %get-tuple-element.228, f32[4,1152,512]{1,2,0:T(8,128)} %fusion.129, f32[4,1152]{1,0:T(4,128)S(1)} %slice.144), kind=kOutput, calls=%fused_computation.58 | convolution fusion | flops 5465899008 | bytes 22436352 | tf_op jit(solution)/shard_map/rd,grn->gdn/dot_general | solution.py:57
  455.9 11.3 %convolution_convert_fusion.1 = bf16[4,1152,1152]{1,2,0:T(8,128)(2,1)} fusion(bf16[4,512,1152]{2,1,0:T(8,128)(2,1)} %copy-done.49, f32[512,1152]{1,0:T(8,128)} %copy-done.7, f32[1152]{0:T(1024)S(1)} %copy-done.33, f32[1152]{0:T(1024)S(1)} %get-tuple-element.230, f32[512]{0:T(512)S(1)} %add_rsqrt_fusion.1, f32[512]{0:T(512)S(1)} %broadcast_multiply_fusion.5), kind=kOutput, calls=%fused_computation.59 | convolution fusion | flops 5444075520 | bytes 17708032 | tf_op jit(solution)/shard_map/rd,grn->gdn/dot_general | solution.py:57
  467.2 9.2 %fusion.73 = f32[1024,1152,1]{1,0,2:T(8,128)S(1)} fusion(bf16[4,1024,288]{1,2,0:T(8,128)(2,1)} %bitcast.282, bf16[4,1152,1152]{2,1,0:T(8,128)(2,1)} %bitcast.272), kind=kOutput, calls=%fused_computation.99 | convolution fusion | flops 2717908992 | bytes 10616832 | tf_op jit(solution)/shard_map/grn,gdn->rd/dot_general | solution.py:57
  476.5 8.3 bitcast_add_fusion
  489.0 72.6 %pmax.7 = f32[16]{0:T(128)S(1)} all-reduce(f32[16]{0:T(128)S(1)} %reshape.336), channel_id=1, replica_groups=mesh['dp'=2,'gx'=4,'gy'=4] {'dp','gx','gy'}, use_global_device_ids=true, to_apply=%region_35.36 | all-reduce | flops 16 | bytes 128 | tf_op jit(solution)/shard_map/pmax | solution.py:163
  563.0 40.2 %psum.7 = f32[6,1152]{1,0:T(8,128)S(1)} all-reduce(f32[6,1152]{1,0:T(8,128)S(1)} %pad_maximum_fusion.2), channel_id=1, replica_groups=mesh['dp'=2,'gx'=4,'gy'=4] {'gx','gy','dp'}, use_global_device_ids=true, to_apply=%region_32.33 | all-reduce | flops 6912 | bytes 55296 | tf_op jit(solution)/shard_map/psum | solution.py:250
  607.5 6.9 multiply_reduce_fusion.6
  614.5 75.3 %all_gather.32 = bf16[32,8,1152]{2,1,0:T(8,128)(2,1)S(1)} all-gather(bf16[1,8,1152]{2,1,0:T(8,128)(2,1)S(1)} %concatenate.53), channel_id=1, replica_groups=mesh['dp'=2,'gx'=4,'gy'=4] {'dp','gy','gx'}, dimensions={0}, use_global_device_ids=true | all-gather | bytes 608256 | tf_op jit(solution)/shard_map/all_gather | solution.py:244
  694.0 4.5 fusion.106
  700.6 3.0 all_gather.34
  704.9 47.5 %reduce-scatter.9.cloned.1.call-done = bf16[144,1152]{1,0:T(8,128)(2,1)} async-done(((bf16[4608,1152]{1,0:T(8,128)(2,1)}), bf16[144,1152]{1,0:T(8,128)(2,1)}) %reduce-scatter.9.cloned.1.call-update) | async-done | bytes 331792 | tf_op jit(solution)/shard_map/reduce_scatter | solution.py:52
  757.3 142.4 %reduce-scatter.7.cloned.1.call-done = bf16[144,1152]{1,0:T(8,128)(2,1)} async-done(((bf16[4608,1152]{1,0:T(8,128)(2,1)}), bf16[144,1152]{1,0:T(8,128)(2,1)}) %reduce-scatter.7.cloned.1.call-update) | async-done | bytes 331792 | tf_op jit(solution)/shard_map/reduce_scatter | solution.py:52
  (268 shorter events, 99.6 us)
Async XLA Ops:
  8.0 5.5 copy-start
  8.1 89.3 %all-reduce.3.cloned.1.call-start = ((), (), s32[]{:S(2)}) async-start(), calls=%async_computation.9 | async-start | bytes 442368
  11.7 4.5 copy-start.3
  11.7 7.6 copy-start.48
  11.7 8.8 copy-start.29
  11.8 8.9 copy-start.31
  11.8 8.9 copy-start.40
  11.8 8.9 copy-start.41
  11.8 8.9 copy-start.42
  11.8 99.6 %all-gather.6.cloned.1.call-start = ((), (), s32[]{:S(2)}) async-start(), calls=%async_computation.3 | async-start | bytes 10948608 | tf_op jit(solution)/shard_map/all_gather | solution.py:46
  12.1 86.3 %copy-start.26 = (f32[6,1152]{1,0:T(8,128)S(1)}, f32[6,1152]{1,0:T(8,128)}, u32[]{:S(2)}) copy-start(f32[6,1152]{1,0:T(8,128)} %param.23) | copy-start | bytes 82948
  13.5 186.7 %all-gather.8.cloned.1.call-start = ((), (), s32[]{:S(2)}) async-start(), calls=%async_computation.4 | async-start | bytes 10948608 | tf_op jit(solution)/shard_map/all_gather | solution.py:46
  14.4 274.7 %all-gather.10.cloned.1.call-start = ((), (), s32[]{:S(2)}) async-start(), calls=%async_computation.5 | async-start | bytes 10948608 | tf_op jit(solution)/shard_map/all_gather | solution.py:46
  16.2 684.5 %reduce-scatter.5.cloned.1.call-start = ((), (), s32[]{:S(2)}) async-start(), calls=%async_computation.6 | async-start | bytes 10948608 | tf_op jit(solution)/shard_map/reduce_scatter | solution.py:52
  16.2 82.3 %collective-permute-start = (bf16[512,1152]{1,0:T(8,128)(2,1)S(1)}, bf16[512,1152]{1,0:T(8,128)(2,1)S(1)}, u32[]{:S(2)}, u32[]{:S(2)}) collective-permute-start(bf16[512,1152]{1,0:T(8,128)(2,1)S(1)} %copy-done.3), channel_id=1, source_target_pairs={{0,4},{4,0},{8,12},{12,8},{1,5},{5,1},{9,13},{13,9},{2,6},{6,2},{1... | collective-permute-start | bytes 3538952 | tf_op jit(solution)/shard_map/ppermute | solution.py:116
  98.5 5.1 copy-start.23
  98.5 101.7 %copy-start.32 = (f32[1152]{0:T(1024)}, f32[1152]{0:T(1024)S(1)}, u32[]{:S(2)}) copy-start(f32[1152]{0:T(1024)S(1)} %get-tuple-element.229) | copy-start | bytes 13828
  111.4 5.7 copy-start.11
  111.4 14.5 %slice-start.3 = ((s8[10616832]{0:T(1024)(128)(4,1)}), s8[4194304]{0:T(1024)(128)(4,1)S(1)}, s32[]{:S(2)}) async-start(s8[10616832]{0:T(1024)(128)(4,1)} %bitcast.275), calls=%async_computation.13 | async-start | bytes 8388608
  117.1 8.8 slice-start.4
  117.2 8.8 slice-start.5
  289.0 16.1 %copy-start.8 = (f32[512,1152]{1,0:T(8,128)S(1)}, f32[512,1152]{1,0:T(8,128)}, u32[]{:S(2)}) copy-start(f32[512,1152]{1,0:T(8,128)} %copy-done.7) | copy-start | bytes 7077892
  305.1 14.3 %copy-start.49 = (bf16[4,512,1152]{2,1,0:T(8,128)(2,1)}, bf16[4,512,1152]{2,1,0:T(8,128)(2,1)S(1)}, u32[]{:S(2)}) copy-start(bf16[4,512,1152]{2,1,0:T(8,128)(2,1)S(1)} %get-tuple-element.302) | copy-start | bytes 14155780
  336.5 7.2 copy-start.9
  336.5 7.2 copy-start.47
  406.8 4.6 copy-start.6
  442.8 309.6 %reduce-scatter.9.cloned.1.call-start = ((), (), s32[]{:S(2)}) async-start(), calls=%async_computation.8 | async-start | bytes 10948608 | tf_op jit(solution)/shard_map/reduce_scatter | solution.py:52
  455.2 444.5 %reduce-scatter.7.cloned.1.call-start = ((), (), s32[]{:S(2)}) async-start(), calls=%async_computation.7 | async-start | bytes 10948608 | tf_op jit(solution)/shard_map/reduce_scatter | solution.py:52
  476.4 10.6 %copy-start.25 = (bf16[8,288]{1,0:T(8,128)(2,1)S(1)}, bf16[8,288]{1,0:T(8,128)(2,1)}, u32[]{:S(2)}) copy-start(bf16[8,288]{1,0:T(8,128)(2,1)} %param.21) | copy-start | bytes 13828
  476.4 12.5 %copy-start.43 = (f32[4,4]{1,0:T(4,128)S(1)}, f32[4,4]{1,0:T(4,128)}, u32[]{:S(2)}) copy-start(f32[4,4]{1,0:T(4,128)} %get-tuple-element.113) | copy-start | bytes 196
  476.4 85.8 %copy-start.30 = (f32[288]{0:T(512)S(1)}, f32[288]{0:T(512)}, u32[]{:S(2)}) copy-start(f32[288]{0:T(512)} %param.27) | copy-start | bytes 3460
  476.4 86.4 %copy-start.37 = (bf16[1152]{0:T(1024)(128)(2,1)S(1)}, bf16[1152]{0:T(1024)(128)(2,1)}, u32[]{:S(2)}) copy-start(bf16[1152]{0:T(1024)(128)(2,1)} %get-tuple-element.218) | copy-start | bytes 6916
  476.5 86.4 %copy-start.35 = (f32[1152]{0:T(1024)S(1)}, f32[1152]{0:T(1024)}, u32[]{:S(2)}) copy-start(f32[1152]{0:T(1024)} %get-tuple-element.223) | copy-start | bytes 13828
  476.5 86.4 %copy-start.39 = (bf16[1152]{0:T(1024)(128)(2,1)S(1)}, bf16[1152]{0:T(1024)(128)(2,1)}, u32[]{:S(2)}) copy-start(bf16[1152]{0:T(1024)(128)(2,1)} %get-tuple-element.224) | copy-start | bytes 6916
  476.5 86.4 %copy-start.38 = (bf16[1152]{0:T(1024)(128)(2,1)S(1)}, bf16[1152]{0:T(1024)(128)(2,1)}, u32[]{:S(2)}) copy-start(bf16[1152]{0:T(1024)(128)(2,1)} %get-tuple-element.278) | copy-start | bytes 6916
  476.5 86.4 %copy-start.34 = (f32[1152]{0:T(1024)S(1)}, f32[1152]{0:T(1024)}, u32[]{:S(2)}) copy-start(f32[1152]{0:T(1024)} %get-tuple-element.279) | copy-start | bytes 13828
  476.5 86.5 %copy-start.36 = (bf16[1152]{0:T(1024)(128)(2,1)S(1)}, bf16[1152]{0:T(1024)(128)(2,1)}, u32[]{:S(2)}) copy-start(bf16[1152]{0:T(1024)(128)(2,1)} %get-tuple-element.227) | copy-start | bytes 6916
  476.5 86.5 %copy-start.28 = (f32[4,1152]{1,0:T(4,128)S(1)}, f32[4,1152]{1,0:T(4,128)}, u32[]{:S(2)}) copy-start(f32[4,1152]{1,0:T(4,128)} %get-tuple-element.301) | copy-start | bytes 55300
  484.9 120.7 %copy-start.17 = (bf16[288,288]{1,0:T(8,128)(2,1)S(1)}, bf16[288,288]{1,0:T(8,128)(2,1)}, u32[]{:S(2)}) copy-start(bf16[288,288]{1,0:T(8,128)(2,1)} %param.24) | copy-start | bytes 497668
  484.9 120.7 %copy-start.19 = (bf16[288,288]{1,0:T(8,128)(2,1)S(1)}, bf16[288,288]{1,0:T(8,128)(2,1)}, u32[]{:S(2)}) copy-start(bf16[288,288]{1,0:T(8,128)(2,1)} %param.25) | copy-start | bytes 497668
  484.9 122.6 %copy-start.24 = (f32[1152]{0:T(1024)S(1)}, f32[1152]{0:T(1024)}, u32[]{:S(2)}) copy-start(f32[1152]{0:T(1024)} %copy-done.23) | copy-start | bytes 13828
  485.0 121.5 %collective-permute-start.1 = (bf16[512,1152]{1,0:T(8,128)(2,1)S(1)}, bf16[512,1152]{1,0:T(8,128)(2,1)S(1)}, u32[]{:S(2)}, u32[]{:S(2)}) collective-permute-start(bf16[512,1152]{1,0:T(8,128)(2,1)S(1)} %slice.206), channel_id=1, source_target_pairs={{4,0},{0,4},{12,8},{8,12},{5,1},{1,5},{13,9},{9,13},{6,2},{2,6},{1... | collective-permute-start | bytes 3538952 | tf_op jit(solution)/shard_map/ppermute | solution.py:210
  692.2 6.2 slice-start
  694.0 4.5 slice-start.1
  694.0 4.5 copy-start.10
  694.0 4.5 copy-start.14
  694.0 4.5 slice-start.2
  754.9 148.5 %copy-start.1 = (bf16[288,1152]{1,0:T(8,128)(2,1)S(1)}, bf16[288,1152]{1,0:T(8,128)(2,1)}, u32[]{:S(2)}) copy-start(bf16[288,1152]{1,0:T(8,128)(2,1)} %param.31) | copy-start | bytes 1990660
  (26 other events, 66.7 us)
Sparse Core Ops, SparseCore 0:
  12.4 51.2 all-reduce.2
Sparse Core Ops, SparseCore 1:
  15.9 95.5 all-gather.5
  114.9 85.2 all-gather.7
  203.7 85.3 all-gather.9
  442.9 158.0 reduce-scatter.4
  607.1 145.3 reduce-scatter.8
  758.5 141.1 reduce-scatter.6

commit v2 on v1

v2 whole, which is shorter than its diff:
```python
import math

import jax
import jax.numpy as jnp
from jax import lax
from jax.experimental import pallas as pl
from jax.experimental.pallas import tpu as pltpu
from jax.sharding import PartitionSpec as P

HD = 72
SEQ = 1024
TAU = 8

EPS = 1e-06
GELU_ROOT = 0.7978845608028654
GELU_CUBE = 0.044715
BF = jnp.bfloat16
F32 = jnp.float32
EVERY = ("gy", "gx", "dp")


def gelu_parts(inputs):
    inner_arg = GELU_ROOT * (inputs + GELU_CUBE * inputs * inputs * inputs)
    tangent = jnp.tanh(inner_arg)
    output = 0.5 * inputs * (1.0 + tangent)
    slope_rows = 0.5 * (1.0 + tangent) + 0.5 * inputs * (1.0 - tangent * tangent) * GELU_ROOT * (
        1.0 + 3.0 * GELU_CUBE * inputs * inputs
    )
    return (output, slope_rows)


def normalize(rows_in):
    mean_row = jnp.mean(rows_in, axis=1, keepdims=True)
    centred = rows_in - mean_row
    inverse = lax.rsqrt(jnp.mean(centred * centred, axis=1, keepdims=True) + EPS)
    return (centred * inverse, inverse)


def normalize_back(grad_hat, normed, inverse):
    grad_mean = jnp.mean(grad_hat, axis=1, keepdims=True)
    cross_mean = jnp.mean(grad_hat * normed, axis=1, keepdims=True)
    return inverse * (grad_hat - grad_mean - normed * cross_mean)


def swap(values, axis, bit):
    pairs = [(i, i ^ bit) for i in range(lax.axis_size(axis))]
    return lax.ppermute(values, axis, pairs)


def bits_of(axis):
    return [1 << k for k in range(lax.axis_size(axis).bit_length() - 1)]


def cube_gather(values, axis):
    at = lax.axis_index(axis)
    for bit in bits_of(axis):
        other = swap(values, axis, bit)
        low = (at & bit) == 0
        values = jnp.concatenate(
            [jnp.where(low, values, other), jnp.where(low, other, values)], axis=0
        )
    return values


def by_distance(values, index):
    count = values.shape[0]
    for k in range(count.bit_length() - 1):
        pairs = values.reshape((-1, 2, 1 << k) + values.shape[1:])
        flipped = jnp.concatenate([pairs[:, 1:], pairs[:, :1]], axis=1).reshape(values.shape)
        values = jnp.where((index >> k) & 1 == 1, flipped, values)
    return values


def total_steps(values):
    summed = lax.broadcasted_iota(jnp.int32, values.shape, 0) < values.shape[0] - 1
    for axis in ("dp", "gx", "gy"):
        for bit in bits_of(axis):
            values, got = yield (values, swap(values, axis, bit))
            values = jnp.where(summed, values + got, jnp.maximum(values, got))
    yield values


def pick(values, index, axis=0):
    return lax.dynamic_index_in_dim(values, index, axis, keepdims=False)


def add_low(left, right):
    return (left.astype(F32) + right.astype(F32)).astype(BF)


def own_half(shard):
    part = shard.shape[0] // 2
    return lax.dynamic_slice_in_dim(shard, lax.axis_index("dp") * part, part, 0)


def gather_weight(shard):
    full = lax.all_gather(own_half(shard), EVERY, axis=0, tiled=True)
    return full.reshape(lax.axis_size("gy"), -1, shard.shape[1])


def join_pair(values, other, axis, bit):
    low = (lax.axis_index(axis) & bit) == 0
    return jnp.stack([jnp.where(low, values, other), jnp.where(low, other, values)])


def gather_steps(shard):
    mine = own_half(shard)
    cols = shard.shape[1]
    if (lax.axis_size("gy"), lax.axis_size("gx")) != (4, 4):
        yield gather_weight(shard)
        return
    mine, got = yield (mine, swap(mine, "gx", 2))
    pair = join_pair(mine, got, "gx", 2)
    pair, got = yield (pair, swap(pair, "gx", 1))
    quad = join_pair(pair, got, "gx", 1)
    one, two = quad[:, 0], quad[:, 1]
    one, two, got_one, got_two = yield (one, two, swap(one, "gy", 2), swap(two, "gy", 1))
    one, two = join_pair(one, got_one, "gy", 2), join_pair(two, got_two, "gy", 1)
    one, two, got_one, got_two = yield (one, two, swap(one, "gy", 1), swap(two, "gy", 2))
    one, two = join_pair(one, got_one, "gy", 1), join_pair(two, got_two, "gy", 2)
    one, two, got_one, got_two = yield (one, two, swap(one, "dp", 1), swap(two, "dp", 1))
    low = lax.axis_index("dp") == 0

    def rows_of(values, got):
        return jnp.stack([jnp.where(low, values, got), jnp.where(low, got, values)], axis=3)

    one = jnp.swapaxes(rows_of(one, got_one), 0, 1)
    yield jnp.stack([one, rows_of(two, got_two)], axis=2).reshape(4, -1, cols)


def cube_mesh():
    return (lax.axis_size("gy"), lax.axis_size("gx"), lax.axis_size("dp")) == (4, 4, 2)


def scatter_steps(lefts, picks, rights):
    size_gx = lax.axis_size("gx")
    at_gy, at_gx, at_dp = lax.axis_index("gy"), lax.axis_index("gx"), lax.axis_index("dp")
    if cube_mesh():
        other = weight_grads_near(lefts, picks, rights, 1 - at_dp)
        (got,) = yield (swap(other, "dp", 1),)
        one, send_one, two, send_two = weight_grads_near(lefts, picks, rights, at_dp, got)
        one, two, got_one, got_two = yield (
            one,
            two,
            swap(send_one, "gy", 1),
            swap(send_two, "gy", 2),
        )
        one, two, got_one, got_two = yield (
            add_low(one[0], got_one[0]),
            add_low(two[0], got_two[0]),
            swap(add_low(one[1], got_one[1]), "gy", 2),
            swap(add_low(two[1], got_two[1]), "gy", 1),
        )
        at_z1, at_z0 = at_gx // 2, at_gx % 2
        acc = jnp.stack([add_low(one, got_one), add_low(two, got_two)])
        acc = acc.reshape(2, 2, -1, acc.shape[2])
        acc, got = yield (pick(acc, at_z0, 1), swap(pick(acc, 1 - at_z0, 1), "gx", 1))
        acc = add_low(acc, got)
        acc, got = yield (pick(acc, at_z1), swap(pick(acc, 1 - at_z1), "gx", 2))
        acc = add_low(acc, got)
    else:
        other, mine = [
            weight_grads([half_rows(x, w) for x in lefts], picks, rights)
            for w in (1 - at_dp, at_dp)
        ]
        got, mine = yield (swap(other, "dp", 1), mine)
        acc = add_low(mine, got)
        acc = lax.psum_scatter(
            acc.reshape(-1, acc.shape[2]), ("gy", "gx"), scatter_dimension=0, tiled=True
        )
    acc, got = yield (acc, swap(acc, "dp", 1))
    low = at_dp == 0
    yield jnp.concatenate([jnp.where(low, acc, got), jnp.where(low, got, acc)], axis=0).astype(F32)


class Exchange:
    def __init__(self, steps):
        self.steps = steps
        self.state = next(self.steps)
        self.done = not isinstance(self.state, tuple)

    def advance(self):
        self.state = self.steps.send(self.state)
        self.done = not isinstance(self.state, tuple)

    def result(self):
        while not self.done:
            self.advance()
        return self.state


def tick(value, *exchanges):
    live = [x for x in exchanges if not x.done]
    if not live:
        return value
    value, states = lax.optimization_barrier((value, [x.state for x in live]))
    for x, state in zip(live, states):
        x.state = state
        x.advance()
    return value


def half_rows(values, which):
    width, rows = values.shape
    blocks = values.reshape(lax.axis_size("gx"), 2, -1, rows)
    return pick(blocks, which, 1).reshape(width // 2, rows)


LOG2E = 1.4426950408889634
SCALE = 1.0 / math.sqrt(HD)


def dot(spec, left, right):
    return jnp.einsum(spec, left, right, preferred_element_type=F32)


def dot_t(left, right):
    return lax.dot_general(left, right, (((1,), (1,)), ((), ())), preferred_element_type=F32)


def dot_n(left, right):
    return jnp.dot(left, right, preferred_element_type=F32)


def by_group(kernel, name, whole, grouped, outs, flops, whole_out=None, scratch=()):
    g = grouped[0].shape[0]

    def block(x):
        return pl.BlockSpec((1,) + tuple(x.shape[1:]), lambda i: (i, 0, 0))

    shapes = [jax.ShapeDtypeStruct((g,) + shape, kind) for shape, kind in outs]
    specs = [block(x) for x in shapes]
    if whole_out is not None:
        shapes.append(jax.ShapeDtypeStruct(whole_out, F32))
        specs.append(pl.BlockSpec(whole_out, lambda i: (0, 0)))
    moved = sum(x.size * x.dtype.itemsize for x in [*whole, *grouped, *shapes])
    return pl.pallas_call(
        kernel,
        out_shape=shapes,
        grid=(g,),
        in_specs=[pl.BlockSpec(x.shape, lambda i: (0, 0)) for x in whole]
        + [block(x) for x in grouped],
        out_specs=specs,
        scratch_shapes=scratch,
        cost_estimate=pl.CostEstimate(flops=flops * g, transcendentals=0, bytes_accessed=moved),
        name=name,
    )(*whole, *grouped)


def edges_of(rights):
    edges = [0]
    for right in rights:
        edges.append(edges[-1] + right.shape[2])
    return edges


def weight_grads(lefts, picks, rights):
    m, edges = lefts[0].shape[0], edges_of(rights)

    def kernel(*refs):
        for i, k in enumerate(picks):
            right = refs[len(lefts) + i][0]
            refs[-1][0, :, edges[i] : edges[i + 1]] = dot_n(
                refs[k][:, : right.shape[0]], right
            ).astype(BF)

    flops = sum(2 * m * x.shape[1] * x.shape[2] for x in rights)
    return by_group(kernel, "weight_grads", lefts, rights, [((m, edges[-1]), BF)], flops)[0]


def weight_grads_near(lefts, picks, rights, side, got=None):
    size_gx = lax.axis_size("gx")
    lefts = [x.reshape(size_gx, 2, -1, x.shape[1]) for x in lefts]
    m, edges = size_gx * lefts[0].shape[2], edges_of(rights)
    n, part = edges[-1], m // 2

    def kernel(place_ref, *refs):
        left_refs, right_refs = refs[: len(lefts)], refs[len(lefts) : len(lefts) + len(rights)]
        rest = refs[len(lefts) + len(rights) :]
        step = pl.program_id(0)

        def product(i):
            right = right_refs[i][0]
            left = left_refs[picks[i]][:, 0, :, : right.shape[0]]
            return dot_n(left.reshape(m, right.shape[0]), right)

        if got is None:
            for i in range(len(rights)):
                rest[0][0, :, edges[i] : edges[i + 1]] = product(i).astype(BF)
            return
        got_ref, one_ref, send_one_ref, two_ref, send_two_ref = rest[:5]
        sum_ref = rest[5]
        for i in range(len(rights)):
            at = slice(edges[i], edges[i + 1])
            sum_ref[:, at] = (product(i) + got_ref[0, :, at].astype(F32)).astype(BF)

        for ref, rows, wanted in (
            (one_ref, slice(0, part), step % 2 == 0),
            (send_one_ref, slice(0, part), step % 2 == 1),
            (two_ref, slice(part, m), step // 2 == 0),
            (send_two_ref, slice(part, m), step // 2 == 1),
        ):

            @pl.when(wanted)
            def _(ref=ref, rows=rows):
                ref[0] = sum_ref[rows, :]

    place = jnp.stack([side, lax.axis_index("gy")]).astype(jnp.int32)
    in_specs = [
        pl.BlockSpec((size_gx, 1) + x.shape[2:], lambda i, p: (0, p[0], 0, 0)) for x in lefts
    ] + [pl.BlockSpec((1,) + x.shape[1:], lambda i, p: (i ^ p[1], 0, 0)) for x in rights]
    operands = [*lefts, *rights]
    scratch = []
    if got is None:
        shapes = jax.ShapeDtypeStruct((4, m, n), BF)
        out_specs = pl.BlockSpec((1, m, n), lambda i, p: (i, 0, 0))
    else:
        operands.append(got)
        in_specs.append(pl.BlockSpec((1, m, n), lambda i, p: (i, 0, 0)))
        shapes = [jax.ShapeDtypeStruct((2, part, n), BF)] * 4
        out_specs = [
            pl.BlockSpec((1, part, n), lambda i, p: (i // 2, 0, 0)),
            pl.BlockSpec((1, part, n), lambda i, p: (i // 2, 0, 0)),
            pl.BlockSpec((1, part, n), lambda i, p: (jnp.minimum(i, 1), 0, 0)),
            pl.BlockSpec((1, part, n), lambda i, p: (jnp.maximum(i, 2) - 2, 0, 0)),
        ]
        scratch = [pltpu.VMEM((m, n), BF)]
    flops = sum(8 * m * x.shape[1] * x.shape[2] for x in rights)
    moved = 8 * m * n * (1 if got is None else 2) + sum(2 * x.size for x in rights)
    return pl.pallas_call(
        kernel,
        out_shape=shapes,
        grid_spec=pltpu.PrefetchScalarGridSpec(
            num_scalar_prefetch=1,
            grid=(4,),
            in_specs=in_specs,
            out_specs=out_specs,
            scratch_shapes=scratch,
        ),
        cost_estimate=pl.CostEstimate(flops=flops, transcendentals=0, bytes_accessed=moved),
        name="weight_grads_near",
    )(place, *operands)


def project_back(xs, weight, terms, init=None):
    width, w_cols = weight.shape[1:]
    rows = xs[0].shape[1] if init is None else init.shape[0]
    rows = max([rows] + [x.shape[1] for x in xs])
    windows = []
    for x, start in zip(xs, terms):
        low = start // 128 * 128
        windows.append((low, min(-(-(start + x.shape[2]) // 128) * 128, w_cols), start - low))
    padded = [w[1] - w[0] != x.shape[2] for x, w in zip(xs, windows)]
    whole = [] if init is None else [init]

    def kernel(*refs):
        refs = list(refs)
        init_ref = refs.pop(0) if whole else None
        x_refs, w_ref, out_ref = refs[: len(xs)], refs[len(xs)], refs[len(xs) + 1]
        wide_refs = refs[len(xs) + 2 :]

        @pl.when(pl.program_id(0) == 0)
        def _():
            out_ref[...] = jnp.zeros((rows, width), F32) if init_ref is None else init_ref[...]
            for ref in wide_refs:
                ref[...] = jnp.zeros(ref.shape, BF)

        parts, wide = {}, 0
        for x_ref, (low, high, shift), pad in zip(x_refs, windows, padded):
            r, n = x_ref.shape[1:]
            if pad:
                ref = wide_refs[wide]
                wide += 1
                ref[:, shift : shift + n] = x_ref[0]
                x = ref[...]
            else:
                x = x_ref[0]
            part = dot_t(x, w_ref[0, :, low:high])
            parts[r] = parts[r] + part if r in parts else part
        for r, part in parts.items():
            out_ref[:r] += part

    scratch = [
        pltpu.VMEM((x.shape[1], w[1] - w[0]), BF) for x, w, pad in zip(xs, windows, padded) if pad
    ]
    flops = sum(2 * x.shape[1] * width * x.shape[2] for x in xs)
    return by_group(
        kernel, "project_back", whole, [*xs, weight], [], flops, (rows, width), scratch
    )[0]


def project_qkv(hidden, rows, weight, bias_q, bias_v):
    ctx, width = hidden.shape
    n = weight.shape[2] // 4

    def kernel(h_ref, w_ref, bq_ref, bv_ref, q_ref, k_ref, v_ref):
        joint = dot_n(h_ref[...], w_ref[0, :, : 3 * n])
        q_ref[0] = (joint[:rows, :n] + bq_ref[0]).astype(BF)
        k_ref[0] = joint[:, n : 2 * n].astype(BF)
        v_ref[0] = (joint[:, 2 * n :] + bv_ref[0]).astype(BF)

    return by_group(
        kernel,
        "project_qkv",
        [hidden],
        [weight, bias_q, bias_v],
        [((rows, n), BF), ((ctx, n), BF), ((ctx, n), BF)],
        6 * ctx * width * n,
    )


def project_up(hidden, weight, bias):
    rows, width = hidden.shape
    n = bias.shape[2]

    def kernel(h_ref, w_ref, bias_ref, act_ref, slope_ref):
        activ, slope = gelu_parts(dot_n(h_ref[...], w_ref[0]) + bias_ref[0])
        act_ref[0] = activ.astype(BF)
        slope_ref[0] = slope.astype(BF)

    return by_group(
        kernel,
        "project_up",
        [hidden],
        [weight, bias],
        [((rows, n), BF), ((rows, n), BF)],
        2 * rows * width * n,
    )


def project_act_back(grad_mlp, weight, slope):
    rows, width = grad_mlp.shape
    n = slope.shape[2]

    def kernel(g_ref, w_ref, slope_ref, low_ref, sums_ref):
        grad = dot_n(g_ref[...], w_ref[0]) * slope_ref[0].astype(F32)
        low_ref[0] = grad.astype(BF)
        sums_ref[0] = jnp.sum(grad, axis=0, keepdims=True)

    return by_group(
        kernel,
        "project_act_back",
        [grad_mlp],
        [weight, slope],
        [((rows, n), BF), ((1, n), F32)],
        2 * rows * width * n,
    )


def project_mixed_back(grad_attn, weight):
    rows, width = grad_attn.shape
    n = weight.shape[2] // 4
    low = 3 * n // 128 * 128

    def kernel(g_ref, w_ref, out_ref):
        out_ref[0] = dot_n(g_ref[...], w_ref[0, :, low:])[:, 3 * n - low :].astype(BF)

    return by_group(
        kernel, "project_mixed_back", [grad_attn], [weight], [((rows, n), BF)], 2 * rows * width * n
    )[0]


def head_of(ref, h):
    return ref[0, :, h * HD : (h + 1) * HD]


def attend(queries, keys_ctx, values_ctx):
    _, rows, n = queries.shape
    ctx = keys_ctx.shape[1]
    heads = n // HD

    def kernel(q_ref, k_ref, v_ref, mixed_ref, sums_ref, tops_ref):
        for h in range(heads):
            q, k, v = head_of(q_ref, h), head_of(k_ref, h), head_of(v_ref, h)
            scores = dot_t(k, q)
            top = jnp.max(scores, axis=0, keepdims=True)
            weights = jnp.exp2((scores - top) * (SCALE * LOG2E))
            total = jnp.sum(weights, axis=0, keepdims=True)
            mixed = dot_n(v.T, weights.astype(BF)) / total
            mixed_ref[0, :, h * HD : (h + 1) * HD] = mixed.T.astype(BF)
            sums_ref[0, h : h + 1, :] = top * (SCALE * LOG2E) + jnp.log2(total)
            tops_ref[0, h : h + 1, :] = top * SCALE

    return by_group(
        kernel,
        "attend",
        [],
        [queries, keys_ctx, values_ctx],
        [((rows, n), BF), ((heads, rows), F32), ((heads, rows), F32)],
        14 * rows * ctx * n,
    )


def attend_back(queries, keys_ctx, values_ctx, mixed, grad_mixed, log_sums, heads):
    _, rows, n = queries.shape
    ctx = keys_ctx.shape[1]
    n_out = len(heads) * HD

    def kernel(q_ref, k_ref, v_ref, x_ref, g_ref, sums_ref, gq_ref, gk_ref, gv_ref):
        for j, h in enumerate(heads):
            q, k, v = head_of(q_ref, h), head_of(k_ref, h), head_of(v_ref, h)
            grad = head_of(g_ref, h)
            delta = jnp.sum(
                (head_of(x_ref, h).astype(F32) * grad.astype(F32)).T, axis=0, keepdims=True
            )
            probs = jnp.exp2(dot_t(k, q) * (SCALE * LOG2E) - sums_ref[0, h : h + 1, :])
            grad_scores = (probs * (dot_t(v, grad) - delta)).astype(BF)
            out = slice(j * HD, (j + 1) * HD)
            gk_ref[0, :, out] = (dot_n(grad_scores, q) * SCALE).astype(BF)
            gv_ref[0, :, out] = dot_n(probs.astype(BF), grad).astype(BF)
            gq_ref[0, :, out] = (dot_n(k.T, grad_scores) * SCALE).T.astype(BF)

    return by_group(
        kernel,
        "attend_back",
        [],
        [queries, keys_ctx, values_ctx, mixed, grad_mixed, log_sums],
        [((rows, n_out), BF), ((ctx, n_out), BF), ((ctx, n_out), BF)],
        35 * rows * ctx * n_out,
    )


def body(
    latents_in,
    condition,
    ada_weight,
    ada_bias,
    query_weight,
    key_weight,
    value_weight,
    query_bias,
    value_bias,
    out_weight,
    out_bias,
    up_weight,
    up_bias,
    down_weight,
    down_bias,
    grad_out,
):
    rows, width = latents_in.shape
    latent_count = condition.shape[0]
    cols = query_weight.shape[1]
    width_x = out_bias.shape[0]
    size_gx, size_gy = lax.axis_size("gx"), lax.axis_size("gy")
    at_gx, at_gy = lax.axis_index("gx"), lax.axis_index("gy")
    span = SEQ // rows
    heads_here = cols // HD

    def rows_sum(values):
        return jnp.sum(values, axis=-2).reshape(-1, width)

    def shift_pairs(shift):
        return [(i, i // span * span + (i + shift) % span) for i in range(size_gx)]

    context = jnp.concatenate(
        [latents_in] + [lax.ppermute(latents_in, "gx", shift_pairs(s)) for s in range(1, span)], axis=0
    )

    cond_f32 = condition.astype(F32)
    silu_cond = jax.nn.silu(cond_f32).astype(BF)
    mod_part = dot("le,emf->lmf", silu_cond, ada_weight)
    for bit in reversed(bits_of("gy")):
        mod_pair = mod_part.reshape((2, -1) + mod_part.shape[1:])
        side = (at_gy // bit) % 2
        mod_part = pick(mod_pair, side) + swap(pick(mod_pair, 1 - side), "gy", bit)
    mod_own = pick(mod_part, at_gx // span) + ada_bias
    shift_one, scale_one, gate_one, shift_two, scale_two, gate_two = [
        mod_own[m : m + 1] for m in range(6)
    ]

    along_x = cube_gather(jnp.concatenate([out_bias, down_bias])[None], "gx")
    out_bias_all = along_x[:, :width_x].reshape(1, width)
    down_bias_all = along_x[:, width_x:].reshape(1, width)
    rest = cube_gather(jnp.concatenate([query_bias, value_bias, up_bias])[None], "gy")
    query_bias_all = rest[:, None, :cols]
    value_bias_all = rest[:, None, cols : 2 * cols]
    up_bias_all = rest[:, None, 2 * cols :]

    attn_w = gather_weight(
        jnp.concatenate([query_weight, key_weight, value_weight, out_weight.T], axis=1)
    )
    bring_up = Exchange(gather_steps(up_weight))
    down_w = gather_weight(down_weight.T)
    grad_mlp = gate_two * grad_out
    grad_mlp_low = grad_mlp.astype(BF)

    normed_ctx, inverse_ctx = normalize(context.astype(F32))
    hidden_ctx = (normed_ctx * (1.0 + scale_one) + shift_one).astype(BF)
    normed_one, inverse_one, hidden_one = normed_ctx[:rows], inverse_ctx[:rows], hidden_ctx[:rows]
    residual = latents_in.astype(F32)
    hidden_ctx, hidden_t, grad_mlp_t = lax.optimization_barrier(
        (hidden_ctx, hidden_ctx.T, grad_mlp_low.T)
    )
    for _ in range(3):
        hidden_ctx = tick(hidden_ctx, bring_up)
    queries, keys_ctx, values_ctx = project_qkv(
        hidden_ctx, rows, attn_w, query_bias_all, value_bias_all
    )
    queries = tick(queries, bring_up)
    mixed, log_sums, head_tops = attend(queries, keys_ctx, values_ctx)
    head_tops = jnp.max(head_tops, axis=2)
    mixed = tick(mixed, bring_up)
    attn_out = project_back([mixed], attn_w, [3 * cols]) + out_bias_all
    after_attn = residual + gate_one * attn_out
    normed_two, inverse_two = normalize(after_attn)
    hidden_two = (normed_two * (1.0 + scale_two) + shift_two).astype(BF)
    up_w = bring_up.result()
    activation, gelu_slope = project_up(hidden_two, up_w, up_bias_all)
    sum_down = Exchange(scatter_steps([grad_mlp_t], [0], [activation]))
    grad_up_low, up_sums = project_act_back(grad_mlp_low, down_w, gelu_slope)
    grad_up_low = tick(grad_up_low, sum_down)
    sum_up = Exchange(scatter_steps([hidden_two.T], [0], [grad_up_low]))
    grad_hidden_two = project_back([grad_up_low], up_w, [0])
    grad_hidden_two = tick(grad_hidden_two, sum_down, sum_up)
    grad_after = grad_out + normalize_back(
        grad_hidden_two * (1.0 + scale_two), normed_two, inverse_two
    )
    grad_attn = gate_one * grad_after
    grad_attn_low = grad_attn.astype(BF)
    grad_mixed_low = project_mixed_back(grad_attn_low, attn_w)
    grad_attn_t = grad_attn_low.T
    tops_row = jnp.zeros((1, width), F32).at[0, : size_gy * heads_here].set(head_tops.reshape(-1))
    early = Exchange(
        total_steps(
            jnp.concatenate(
                [rows_sum(grad_mlp), rows_sum(grad_attn), up_sums.reshape(-1, width), tops_row],
                axis=0,
            )
        )
    )

    half = (heads_here + 1) // 2
    head_sets = [x for x in (range(half), range(half, heads_here)) if len(x)]
    sum_attn, back_parts, grad_ctx = [], [], None
    for i, heads in enumerate(head_sets):
        parts = attend_back(queries, keys_ctx, values_ctx, mixed, grad_mixed_low, log_sums, heads)
        parts = tick(parts, early, sum_down, sum_up, *sum_attn)
        back_parts.append(parts)
        extra = i == 0
        sum_attn.append(
            Exchange(
                scatter_steps(
                    [hidden_t] + [grad_attn_t] * extra,
                    [0, 0, 0] + [1] * extra,
                    list(parts) + [mixed] * extra,
                )
            )
        )
        start = heads[0] * HD
        grad_ctx = project_back(
            list(parts), attn_w, [start, cols + start, 2 * cols + start], grad_ctx
        )
        if i + 1 < len(head_sets):
            grad_mixed_low, grad_ctx = tick(
                (grad_mixed_low, grad_ctx), early, sum_down, sum_up, *sum_attn
            )
    grad_ctx, activation = tick((grad_ctx, activation), early, sum_down, sum_up, *sum_attn)
    grad_hidden_one = grad_ctx[:rows]
    for s in range(1, span):
        back = [(b, a) for a, b in shift_pairs(s)]
        grad_hidden_one += lax.ppermute(
            grad_ctx[s * rows : (s + 1) * rows].astype(BF), "gx", back
        ).astype(F32)
    mlp_out = project_back([activation], down_w, [0]) + down_bias_all
    mlp_out, grad_hidden_one = tick((mlp_out, grad_hidden_one), early, sum_up, *sum_attn)
    block_out = after_attn + gate_two * mlp_out
    grad_input = grad_after + normalize_back(
        grad_hidden_one * (1.0 + scale_one), normed_one, inverse_one
    )

    def group_sum(i):
        return jnp.concatenate(
            [jnp.sum(x[i].astype(F32), axis=1) for x in back_parts], axis=1
        ).reshape(1, width)

    late = jnp.concatenate(
        [
            rows_sum(grad_hidden_one),
            rows_sum(grad_hidden_one * normed_one),
            rows_sum(grad_after * attn_out),
            rows_sum(grad_hidden_two),
            rows_sum(grad_hidden_two * normed_two),
            rows_sum(grad_out * mlp_out),
            group_sum(0),
            group_sum(2),
        ],
        axis=0,
    )
    for bit in bits_of("gx"):
        if bit < span:
            late = late + swap(late, "gx", bit)
    late = late.astype(BF)[None]
    for axis in ("gx", "gy"):
        for bit in bits_of(axis):
            if axis == "gy" or bit >= span:
                late = jnp.concatenate([late, swap(late, axis, bit)], axis=0)
    late_all = jnp.concatenate([late, swap(late, "dp", 1)], axis=0)
    at_latent = at_gy * (size_gx // span) + at_gx // span
    grad_ada_b = jnp.sum(late_all[:, :6].astype(F32), axis=0)
    tail_sum = jnp.sum(late_all[:, 6:].astype(F32), axis=0)
    grad_query_b = lax.dynamic_slice_in_dim(tail_sum[0], at_gy * cols, cols, 0)
    grad_value_b = lax.dynamic_slice_in_dim(tail_sum[1], at_gy * cols, cols, 0)
    silu_near = by_distance(silu_cond, at_latent)
    silu_every = jnp.concatenate(
        [silu_near, by_distance(swap(silu_cond, "dp", 1), at_latent)], axis=0
    )
    grad_ada_w = dot("le,lmf->emf", silu_every, late_all[:, :6])
    grad_silu = by_distance(dot("lmf,emf->le", late[:, :6], ada_weight), at_latent)
    sigmoid_cond = jax.nn.sigmoid(cond_f32)
    grad_condition = grad_silu * sigmoid_cond * (1.0 + cond_f32 * (1.0 - sigmoid_cond))

    early_sum = early.result()
    grad_down_b = lax.dynamic_slice_in_dim(early_sum[0], at_gx * width_x, width_x, 0)
    grad_out_b = lax.dynamic_slice_in_dim(early_sum[1], at_gx * width_x, width_x, 0)
    up_cols = up_bias.shape[0]
    grad_up_b = lax.dynamic_slice_in_dim(early_sum[2:-1].reshape(-1), at_gy * up_cols, up_cols, 0)
    logit_max = lax.dynamic_slice_in_dim(early_sum[-1], at_gy * heads_here, heads_here, 0)

    grad_down_w, grad_up_w = sum_down.result(), sum_up.result()
    sums = [x.result() for x in sum_attn]
    grad_qkv = [
        jnp.concatenate(
            [x[:, i * HD * len(h) : (i + 1) * HD * len(h)] for x, h in zip(sums, head_sets)], axis=1
        )
        for i in range(3)
    ]
    grad_out_w = sums[0][:, 3 * HD * len(head_sets[0]) :]

    factor = TAU / jnp.maximum(logit_max, TAU)
    root_cols = jnp.repeat(jnp.sqrt(factor), HD)
    clipped_query = query_weight.astype(F32) * root_cols[None, :]
    clipped_key = key_weight.astype(F32) * root_cols[None, :]
    clipped_bias = query_bias * root_cols
    return (
        block_out,
        grad_input,
        grad_condition,
        grad_ada_w,
        grad_ada_b,
        *grad_qkv,
        grad_query_b,
        grad_value_b,
        grad_out_w.T,
        grad_out_b,
        grad_up_w,
        grad_up_b,
        grad_down_w.T,
        grad_down_b,
        logit_max,
        clipped_query,
        clipped_key,
        clipped_bias,
    )


def solution(mesh):
    placed = (
        P(("dp", "gy", "gx"), None),
        P("dp", "gy"),
        P("gy", None, None),
        P(),
        P("gx", "gy"),
        P("gx", "gy"),
        P("gx", "gy"),
        P("gy"),
        P("gy"),
        P("gy", "gx"),
        P("gx"),
        P("gx", "gy"),
        P("gy"),
        P("gy", "gx"),
        P("gx"),
        P(("dp", "gy", "gx"), None),
    )
    return jax.shard_map(
        body,
        mesh=mesh,
        in_specs=placed,
        out_specs=(
            P(("dp", "gy", "gx"), None),
            P(("dp", "gy", "gx"), None),
            P("dp", "gy"),
            P("gy", None, None),
            P(),
            P("gx", "gy"),
            P("gx", "gy"),
            P("gx", "gy"),
            P("gy"),
            P("gy"),
            P("gy", "gx"),
            P("gx"),
            P("gx", "gy"),
            P("gy"),
            P("gy", "gx"),
            P("gx"),
            P("gy"),
            P("gx", "gy"),
            P("gx", "gy"),
            P("gy"),
        ),
        check_vma=False,
    )
```

time: 921 us -> 664 us (0.72)
  blocking collectives: 274 us -> 0 us
  matrix products: 243 us -> 11.5 us
  Pallas kernels: 0 us -> 227 us
  waiting for transfers between devices: 289 us -> 159 us
  starting transfers between devices: 4.85 us -> 82.5 us
  other arithmetic: 42.6 us -> 111 us
  local copies, waits for them, and re-layouts: 38.9 us -> 50.7 us
    dot_general x49 -> x3, matrix products: 243 us -> 11.5 us  [dot(): return jnp.einsum(spec, left, right, preferred_element_type=F32)]
    pallas_call x0 -> x20, Pallas kernels: none -> 227 us  [the longest x12 155 us: by_group(): pl.pallas_call(kernel, out_shape=shapes, grid=(g,), in_specs=[pl.BlockSpe...]
    reduce_scatter x3 -> x0, waiting for transfers between devices: 190 us -> none  [scatter_grad(): mine = lax.psum_scatter(flat, EVERY, scatter_dimension=0, tiled=True)]
    all_gather x6 -> x0, blocking collectives: 161 us -> none  [the longest x1 76.2 us: body(): lax.all_gather(jnp.concatenate([out_bias, down_bias, query_bias, value_bi...]
    ppermute x0 -> x57, waiting for transfers between devices: none -> 119 us  [swap(): return lax.ppermute(values, axis, pairs)]
    all_gather x3 -> x2, waiting for transfers between devices: 99.4 us -> 0.01 us  [gather_weight(): full = lax.all_gather(own_half(shard), EVERY, axis=0, tiled=True)]
    ppermute x0 -> x57, starting transfers between devices: none -> 80.4 us  [swap(): return lax.ppermute(values, axis, pairs)]
    pmax x1 -> x0, blocking collectives: 72.6 us -> none  [body(): top_all = lax.pmax(head_tops.reshape(-1), ('dp', 'gx', 'gy'))]
  transfers between devices with their start and end apart: 9 -> 61, of which waited for: 5 -> 21; matrix products, arithmetic and copies ran while one was open for 18% -> 23% of each run, Pallas kernels for 0% -> 31%
where the time goes in v2:
time: 664 us; the launch traced here: 658 us
  Pallas kernels  227 us (34%)
  waiting for transfers between devices  159 us (24%)
  other arithmetic  111 us (17%)
  starting transfers between devices  82.5 us (12%)
  local copies, waits for them, and re-layouts  50.7 us (8%)
  between operations  15.9 us (2%)
  matrix products  11.5 us (2%)
    pallas_call x12, Pallas kernels, by_group(): pl.pallas_call(kernel, out_shape=shapes, grid=(g,), in_specs=[pl.BlockSpe...  155 us
    ppermute x57, waiting for transfers between devices, swap(): return lax.ppermute(values, axis, pairs)  119 us
    ppermute x57, starting transfers between devices, swap(): return lax.ppermute(values, axis, pairs)  80.4 us
    pallas_call x8, Pallas kernels, weight_grads_near(): pl.pallas_call(kernel, out_shape=shapes, grid_spec=pltpu.PrefetchScalarGr...  72.1 us
    ppermute x1, waiting for transfers between devices, body(): lax.ppermute(latents_in, 'gx', shift_pairs(s))  40.1 us
    convert_element_type x24, other arithmetic, add_low(): return (left.astype(F32) + right.astype(F32)).astype(BF)  36.4 us
  transfers between devices with their start and end apart: 61, of which 21 were waited for; matrix products, arithmetic and copies ran while one was open for 23% of the time, Pallas kernels for 31%

profile of v2, /device:TPU:0, one launch (start us, length us, event | category | flops | bytes accessed | tf_op | source)
XLA Modules:
  0.0 657.8 jit_solution(59981455587563452)
XLA Ops:
  10.8 3.0 fusion.57
  13.9 3.1 collective-permute-start
  27.0 40.1 %collective-permute-done.2 = bf16[512,1152]{1,0:T(8,128)(2,1)} collective-permute-done((bf16[512,1152]{1,0:T(8,128)(2,1)}, bf16[512,1152]{1,0:T(8,128)(2,1)}, u32[]{:S(2)}, u32[]{:S(2)}) %collective-permute-start.2) | collective-permute-done | bytes 1179680 | tf_op jit(solution)/shard_map/ppermute | solution.py:557
  70.9 4.3 fusion
  78.3 34.1 %collective-permute-done.4 = bf16[2,144,1152]{2,1,0:T(8,128)(2,1)S(1)} collective-permute-done((bf16[2,144,1152]{2,1,0:T(8,128)(2,1)S(1)}, bf16[2,144,1152]{2,1,0:T(8,128)(2,1)S(1)}, u32[]{:S(2)}, u32[]{:S(2)}) %collective-permute-start.4) | collective-permute-done | bytes 663584 | tf_op jit(solution)/shard_map/ppermute | solution.py:47
  116.5 14.1 %collective-permute-done.5 = bf16[2,144,1152]{2,1,0:T(8,128)(2,1)S(1)} collective-permute-done((bf16[2,144,1152]{2,1,0:T(8,128)(2,1)S(1)}, bf16[2,144,1152]{2,1,0:T(8,128)(2,1)S(1)}, u32[]{:S(2)}, u32[]{:S(2)}) %collective-permute-start.5) | collective-permute-done | bytes 663584 | tf_op jit(solution)/shard_map/ppermute | solution.py:47
  136.2 16.4 %project_qkv.1 = (bf16[4,512,288]{2,1,0:T(8,128)(2,1)}, bf16[4,1024,288]{2,1,0:T(8,128)(2,1)}, bf16[4,1024,288]{2,1,0:T(8,128)(2,1)}) custom-call(bf16[1024,1152]{1,0:T(8,128)(2,1)} %get-tuple-element.165.h_ref, bf16[4,1152,1152]{2,1,0:T(8,128)(2,1)} %bitcast.201, f32[4,1,288]{2,1,0:T(1,128)} %copy.96.bq_ref, f32[4,1,288]{2,1,0:T(1,128)} %copy.97.bv_ref), custom_call_target="tpu_custom_call" | custom-call | flops 8153726976 | bytes 18883584 | tf_op jit(solution)/shard_map/project_qkv/pallas_call | solution.py:237
  160.8 3.6 collective-permute-done.13
  164.4 22.2 %collective-permute-start.14 = (f32[2,576]{1,0:T(2,128)S(1)}, f32[2,576]{1,0:T(2,128)S(1)}, u32[]{:S(2)}, u32[]{:S(2)}) collective-permute-start(f32[2,576]{1,0:T(2,128)S(1)} %pad_maximum_fusion.28), channel_id=1, source_target_pairs={{0,8},{4,12},{8,0},{12,4},{1,9},{5,13},{9,1},{13,5},{2,10},{6,14},... | collective-permute-start | bytes 13832 | tf_op jit(solution)/shard_map/ppermute | solution.py:47
  191.6 18.1 %attend.1 = (bf16[4,512,288]{2,1,0:T(8,128)(2,1)}, f32[4,4,512]{2,1,0:T(4,128)}, f32[4,4,512]{2,1,0:T(4,128)}) custom-call(bf16[4,512,288]{2,1,0:T(8,128)(2,1)} %get-tuple-element.171.q_ref, bf16[4,1024,288]{2,1,0:T(8,128)(2,1)} %get-tuple-element.172.k_ref, bf16[4,1024,288]{2,1,0:T(8,128)(2,1)} %get-tuple-element.173.v_ref), custom_call_target="tpu_custom_call" | custom-call | flops 8455716864 | bytes 7143424 | tf_op jit(solution)/shard_map/attend/pallas_call | solution.py:237
  209.8 3.0 select_bitcast_fusion.1
  217.6 4.7 copy.104
  222.4 8.3 %project_back.5 = f32[512,1152]{1,0:T(8,128)} custom-call(bf16[4,512,288]{2,1,0:T(8,128)(2,1)} %get-tuple-element.179.refs_0_.x_ref.refs_5_, bf16[4,1152,1152]{2,1,0:T(8,128)(2,1)} %bitcast.202), custom_call_target="tpu_custom_call" | custom-call | flops 1358954496 | bytes 14155776 | tf_op jit(solution)/shard_map/project_back/pallas_call | solution.py:237
  235.0 13.9 %project_up.1 = (bf16[4,512,1152]{2,1,0:T(8,128)(2,1)}, bf16[4,512,1152]{2,1,0:T(8,128)(2,1)}) custom-call(bf16[512,1152]{1,0:T(8,128)(2,1)} %add_convert_fusion.1.h_ref, bf16[4,1152,1152]{2,1,0:T(8,128)(2,1)} %bitcast.210, f32[4,1,1152]{2,1,0:T(1,128)} %broadcast_in_dim.34.bias_ref), custom_call_target="tpu_custom_call" | custom-call | flops 5435817984 | bytes 21252096 | tf_op jit(solution)/shard_map/project_up/pallas_call | solution.py:237
  248.9 7.8 %weight_grads_near.8 = bf16[4,576,1152]{2,1,0:T(8,128)(2,1)} custom-call(s32[2]{0:T(128)} %pad_add_fusion.place_ref, bf16[4,2,144,512]{3,2,1,0:T(8,128)(2,1)} %bitcast.214, bf16[4,512,1152]{2,1,0:T(8,128)(2,1)} %get-tuple-element.255.refs_1_.refs_0_), custom_call_target="tpu_custom_call" | custom-call | flops 2717908992 | bytes 10027008 | tf_op jit(solution)/shard_map/weight_grads_near/pallas_call | solution.py:330
  260.9 11.6 %project_act_back.1 = (bf16[4,512,1152]{2,1,0:T(8,128)(2,1)}, f32[4,1,1152]{2,1,0:T(1,128)}) custom-call(bf16[512,1152]{1,0:T(8,128)(2,1)} %get-tuple-element.382.g_ref, bf16[4,1152,1152]{2,1,0:T(8,128)(2,1)} %bitcast.232, bf16[4,512,1152]{2,1,0:T(8,128)(2,1)} %get-tuple-element.184.slope_ref), custom_call_target="tpu_custom_call" | custom-call | flops 5435817984 | bytes 21252096 | tf_op jit(solution)/shard_map/project_act_back/pallas_call | solution.py:237
  272.6 7.8 %weight_grads_near.10 = bf16[4,576,1152]{2,1,0:T(8,128)(2,1)} custom-call(s32[2]{0:T(128)} %pad_add_fusion.place_ref, bf16[4,2,144,512]{3,2,1,0:T(8,128)(2,1)} %bitcast.212, bf16[4,512,1152]{2,1,0:T(8,128)(2,1)} %get-tuple-element.188.refs_0_.refs_1_), custom_call_target="tpu_custom_call" | custom-call | flops 2717908992 | bytes 10027008 | tf_op jit(solution)/shard_map/weight_grads_near/pallas_call | solution.py:330
  282.5 7.0 %collective-permute-done.50 = bf16[8,288]{1,0:T(8,128)(2,1)S(1)} collective-permute-done((bf16[8,288]{1,0:T(8,128)(2,1)S(1)}, bf16[8,288]{1,0:T(8,128)(2,1)S(1)}, u32[]{:S(2)}, u32[]{:S(2)}) %collective-permute-start.50) | collective-permute-done | bytes 4640 | tf_op jit(solution)/shard_map/ppermute | solution.py:47
  289.7 9.8 %weight_grads_near.9 = (bf16[2,288,1152]{2,1,0:T(8,128)(2,1)}, bf16[2,288,1152]{2,1,0:T(8,128)(2,1)}, bf16[2,288,1152]{2,1,0:T(8,128)(2,1)}, bf16[2,288,1152]{2,1,0:T(8,128)(2,1)}) custom-call(s32[2]{0:T(128)} %pad_add_fusion.1.place_ref, bf16[4,2,144,512]{3,2,1,0:T(8,128)(2,1)} %bitcast.215, bf16[4,512,1152]{2,1,0:T(8,128)(2,1)} %get-tuple-element.255.refs_1_.refs_0_, ...), custom_call_target="tpu_custom_call" | custom-call | flops 2717908992 | bytes 15335424 | tf_op jit(solution)/shard_map/weight_grads_near/pallas_call | solution.py:330
  303.6 4.3 copy.107
  308.8 11.5 %project_back.6 = f32[512,1152]{1,0:T(8,128)} custom-call(bf16[4,512,1152]{2,1,0:T(8,128)(2,1)} %get-tuple-element.188.refs_0_.refs_1_, bf16[4,1152,1152]{2,1,0:T(8,128)(2,1)} %bitcast.211), custom_call_target="tpu_custom_call" | custom-call | flops 5435817984 | bytes 17694720 | tf_op jit(solution)/shard_map/project_back/pallas_call | solution.py:237
  320.2 10.8 %collective-permute-done.16 = bf16[2,288,1152]{2,1,0:T(8,128)(2,1)} collective-permute-done((bf16[2,288,1152]{2,1,0:T(8,128)(2,1)}, bf16[2,288,1152]{2,1,0:T(8,128)(2,1)}, u32[]{:S(2)}, u32[]{:S(2)}) %collective-permute-start.16) | collective-permute-done | bytes 1327136 | tf_op jit(solution)/shard_map/ppermute | solution.py:47
  335.6 2.9 multiply_reduce_fusion.2
  341.0 7.7 %project_mixed_back.1.g_ref = bf16[4,512,288]{2,1,0:T(8,128)(2,1)} custom-call(bf16[512,1152]{1,0:T(8,128)(2,1)} %multiply_convert_fusion.g_ref, bf16[4,1152,1152]{2,1,0:T(8,128)(2,1)} %bitcast.203), custom_call_target="tpu_custom_call" | custom-call | flops 1358954496 | bytes 12976128 | tf_op jit(solution)/shard_map/project_mixed_back/pallas_call | solution.py:237
  348.9 3.2 fusion.7
  356.8 9.6 %weight_grads_near.11 = (bf16[2,288,1152]{2,1,0:T(8,128)(2,1)}, bf16[2,288,1152]{2,1,0:T(8,128)(2,1)}, bf16[2,288,1152]{2,1,0:T(8,128)(2,1)}, bf16[2,288,1152]{2,1,0:T(8,128)(2,1)}) custom-call(s32[2]{0:T(128)} %pad_add_fusion.1.place_ref, bf16[4,2,144,512]{3,2,1,0:T(8,128)(2,1)} %bitcast.213, bf16[4,512,1152]{2,1,0:T(8,128)(2,1)} %get-tuple-element.188.refs_0_.refs_1_, ...), custom_call_target="tpu_custom_call" | custom-call | flops 2717908992 | bytes 15335424 | tf_op jit(solution)/shard_map/weight_grads_near/pallas_call | solution.py:330
  368.4 14.3 %attend_back.2 = (bf16[4,512,144]{2,1,0:T(8,128)(2,1)}, bf16[4,1024,144]{2,1,0:T(8,128)(2,1)}, bf16[4,1024,144]{2,1,0:T(8,128)(2,1)}) custom-call(bf16[4,512,288]{2,1,0:T(8,128)(2,1)} %get-tuple-element.171.q_ref, bf16[4,1024,288]{2,1,0:T(8,128)(2,1)} %get-tuple-element.172.k_ref, bf16[4,1024,288]{2,1,0:T(8,128)(2,1)} %get-tuple-element.173.v_ref, ...), custom_call_target="tpu_custom_call" | custom-call | flops 10569646080 | bytes 11239424 | tf_op jit(solution)/shard_map/attend_back/pallas_call | solution.py:237
  389.8 12.2 %collective-permute-done.22 = bf16[2,288,1152]{2,1,0:T(8,128)(2,1)} collective-permute-done((bf16[2,288,1152]{2,1,0:T(8,128)(2,1)}, bf16[2,288,1152]{2,1,0:T(8,128)(2,1)}, u32[]{:S(2)}, u32[]{:S(2)}) %collective-permute-start.22) | collective-permute-done | bytes 1327136 | tf_op jit(solution)/shard_map/ppermute | solution.py:47
  402.0 9.6 %weight_grads_near.12 = bf16[4,576,720]{2,1,0:T(8,128)(2,1)} custom-call(s32[2]{0:T(128)} %pad_add_fusion.place_ref, bf16[4,2,144,1024]{3,2,1,0:T(8,128)(2,1)} %bitcast.206, bf16[4,2,144,512]{3,2,1,0:T(8,128)(2,1)} %bitcast.216, bf16[4,512,144]{2,1,0:T(8,128)(2,1)} %get-tuple-element.210.refs_0_.refs_2_, ...), custom_call_target="tpu_custom_call" | custom-call | flops 2378170368 | bytes 7446528 | tf_op jit(solution)/shard_map/weight_grads_near/pallas_call | solution.py:330
  421.3 2.9 fusion.12
  425.5 12.7 %project_back.7.refs_0_ = f32[1024,1152]{1,0:T(8,128)} custom-call(bf16[4,512,144]{2,1,0:T(8,128)(2,1)} %get-tuple-element.210.refs_0_.refs_2_, bf16[4,1024,144]{2,1,0:T(8,128)(2,1)} %get-tuple-element.211.refs_1_.refs_3_, bf16[4,1024,144]{2,1,0:T(8,128)(2,1)} %get-tuple-element.212.refs_2_.refs_4_, bf16[4,1152,1152]{2,1,0:T(8,128)(2,1)} %bitcast.204), custom_call_target="tpu_custom_call" | custom-call | flops 3397386240 | bytes 18284544 | tf_op jit(solution)/shard_map/project_back/pallas_call | solution.py:237
  441.3 3.6 collective-permute-start.29
  451.8 10.5 %weight_grads_near.13 = (bf16[2,288,720]{2,1,0:T(8,128)(2,1)}, bf16[2,288,720]{2,1,0:T(8,128)(2,1)}, bf16[2,288,720]{2,1,0:T(8,128)(2,1)}, bf16[2,288,720]{2,1,0:T(8,128)(2,1)}) custom-call(s32[2]{0:T(128)} %pad_add_fusion.1.place_ref, bf16[4,2,144,1024]{3,2,1,0:T(8,128)(2,1)} %bitcast.207, bf16[4,2,144,512]{3,2,1,0:T(8,128)(2,1)} %bitcast.217, ...), custom_call_target="tpu_custom_call" | custom-call | flops 2378170368 | bytes 10764288 | tf_op jit(solution)/shard_map/weight_grads_near/pallas_call | solution.py:330
  465.4 14.8 %attend_back.3 = (bf16[4,512,144]{2,1,0:T(8,128)(2,1)}, bf16[4,1024,144]{2,1,0:T(8,128)(2,1)}, bf16[4,1024,144]{2,1,0:T(8,128)(2,1)}) custom-call(bf16[4,512,288]{2,1,0:T(8,128)(2,1)} %get-tuple-element.171.q_ref, bf16[4,1024,288]{2,1,0:T(8,128)(2,1)} %get-tuple-element.172.k_ref, bf16[4,1024,288]{2,1,0:T(8,128)(2,1)} %get-tuple-element.173.v_ref, ...), custom_call_target="tpu_custom_call" | custom-call | flops 10569646080 | bytes 11239424 | tf_op jit(solution)/shard_map/attend_back/pallas_call | solution.py:237
  486.6 8.3 %weight_grads_near.14 = bf16[4,576,432]{2,1,0:T(8,128)(2,1)} custom-call(s32[2]{0:T(128)} %pad_add_fusion.place_ref, bf16[4,2,144,1024]{3,2,1,0:T(8,128)(2,1)} %bitcast.208, bf16[4,512,144]{2,1,0:T(8,128)(2,1)} %get-tuple-element.242.refs_1_, bf16[4,1024,144]{2,1,0:T(8,128)(2,1)} %get-tuple-element.243.refs_2_, bf16[4,1024,144]{2,1,0:T(8,128)(2,1)} %get-tuple-element.244.refs_3_), custom_call_target="tpu_custom_call" | custom-call | flops 1698693120 | bytes 4939776 | tf_op jit(solution)/shard_map/weight_grads_near/pallas_call | solution.py:330
  494.9 4.3 copy.109
  514.4 14.4 %project_back.8 = f32[1024,1152]{1,0:T(8,128)} custom-call(f32[1024,1152]{1,0:T(8,128)} %project_back.7.refs_0_, bf16[4,512,144]{2,1,0:T(8,128)(2,1)} %get-tuple-element.242.refs_1_, bf16[4,1024,144]{2,1,0:T(8,128)(2,1)} %get-tuple-element.243.refs_2_, bf16[4,1024,144]{2,1,0:T(8,128)(2,1)} %get-tuple-element.244.refs_3_, bf16[4,1152,1152]{2,1,0:T(8,128)(2,1)} %bitcast.205), custom_call_target="tpu_custom_call" | custom-call | flops 3397386240 | bytes 23003136 | tf_op jit(solution)/shard_map/project_back/pallas_call | solution.py:237
  528.9 2.9 slice.462
  538.2 4.2 copy.110.refs_4_
  542.5 8.6 %weight_grads_near.15 = (bf16[2,288,432]{2,1,0:T(8,128)(2,1)}, bf16[2,288,432]{2,1,0:T(8,128)(2,1)}, bf16[2,288,432]{2,1,0:T(8,128)(2,1)}, bf16[2,288,432]{2,1,0:T(8,128)(2,1)}) custom-call(s32[2]{0:T(128)} %pad_add_fusion.1.place_ref, bf16[4,2,144,1024]{3,2,1,0:T(8,128)(2,1)} %bitcast.209, bf16[4,512,144]{2,1,0:T(8,128)(2,1)} %get-tuple-element.242.refs_1_, ...), custom_call_target="tpu_custom_call" | custom-call | flops 1698693120 | bytes 6930432 | tf_op jit(solution)/shard_map/weight_grads_near/pallas_call | solution.py:330
  553.5 11.6 %project_back.9 = f32[512,1152]{1,0:T(8,128)} custom-call(bf16[4,512,1152]{2,1,0:T(8,128)(2,1)} %get-tuple-element.255.refs_1_.refs_0_, bf16[4,1152,1152]{2,1,0:T(8,128)(2,1)} %bitcast.233), custom_call_target="tpu_custom_call" | custom-call | flops 5435817984 | bytes 17694720 | tf_op jit(solution)/shard_map/project_back/pallas_call | solution.py:237
  570.9 11.4 %collective-permute-done.45 = bf16[2,288,432]{2,1,0:T(8,128)(2,1)S(1)} collective-permute-done((bf16[2,288,432]{2,1,0:T(8,128)(2,1)S(1)}, bf16[2,288,432]{2,1,0:T(8,128)(2,1)S(1)}, u32[]{:S(2)}, u32[]{:S(2)}) %collective-permute-start.45) | collective-permute-done | bytes 497696 | tf_op jit(solution)/shard_map/ppermute | solution.py:47
  582.4 4.4 multiply_reduce_fusion
  598.1 3.7 multiply_add_fusion
  604.4 4.6 collective-permute-done.47
  618.0 3.4 convolution_bitcast_fusion
  628.3 5.2 fusion.45
  639.0 7.6 %collective-permute-done.57 = bf16[144,432]{1,0:T(8,128)(2,1)S(1)} collective-permute-done((bf16[144,432]{1,0:T(8,128)(2,1)S(1)}, bf16[144,432]{1,0:T(8,128)(2,1)S(1)}, u32[]{:S(2)}, u32[]{:S(2)}) %collective-permute-start.57) | collective-permute-done | bytes 124448 | tf_op jit(solution)/shard_map/ppermute | solution.py:47
  (461 shorter events, 183.6 us)
Async XLA Ops:
  7.2 129.0 %all-gather.3.cloned.1.call-start = ((), (), s32[]{:S(2)}) async-start(), calls=%async_computation | async-start | bytes 10948608 | tf_op jit(solution)/shard_map/all_gather | solution.py:97
  10.7 250.2 %all-gather.5.cloned.1.call-start = ((), (), s32[]{:S(2)}) async-start(), calls=%async_computation.1 | async-start | bytes 10948608 | tf_op jit(solution)/shard_map/all_gather | solution.py:97
  17.0 50.1 %collective-permute-start.2 = (bf16[512,1152]{1,0:T(8,128)(2,1)}, bf16[512,1152]{1,0:T(8,128)(2,1)}, u32[]{:S(2)}, u32[]{:S(2)}) collective-permute-start(bf16[512,1152]{1,0:T(8,128)(2,1)} %param.18), channel_id=1, source_target_pairs={{0,4},{4,0},{8,12},{12,8},{1,5},{5,1},{9,13},{13,9},{2,6},{6,2},{1... | collective-permute-start | bytes 3538952 | tf_op jit(solution)/shard_map/ppermute | solution.py:557
  22.0 53.2 %collective-permute-start.3 = (bf16[144,1152]{1,0:T(8,128)(2,1)S(1)}, bf16[144,1152]{1,0:T(8,128)(2,1)S(1)}, u32[]{:S(2)}, u32[]{:S(2)}) collective-permute-start(bf16[144,1152]{1,0:T(8,128)(2,1)S(1)} %constant_dynamic-slice_fusion.6), channel_id=1, source_target_pairs={{0,8},{4,12},{8,0},{12,4},{1,9},{5,13},{9,1},{13,5},{2,10},{6,14},... | collective-permute-start | bytes 995336 | tf_op jit(solution)/shard_map/ppermute | solution.py:47
  75.3 37.1 %collective-permute-start.4 = (bf16[2,144,1152]{2,1,0:T(8,128)(2,1)S(1)}, bf16[2,144,1152]{2,1,0:T(8,128)(2,1)S(1)}, u32[]{:S(2)}, u32[]{:S(2)}) collective-permute-start(bf16[2,144,1152]{2,1,0:T(8,128)(2,1)S(1)} %pad_maximum_fusion.7), channel_id=1, source_target_pairs={{0,4},{4,0},{8,12},{12,8},{1,5},{5,1},{9,13},{13,9},{2,6},{6,2},{1... | collective-permute-start | bytes 1990664 | tf_op jit(solution)/shard_map/ppermute | solution.py:47
  76.0 38.5 %collective-permute-start.7 = (f32[1,1728]{1,0:T(1,128)S(1)}, f32[1,1728]{1,0:T(1,128)S(1)}, u32[]{:S(2)}, u32[]{:S(2)}) collective-permute-start(f32[1,1728]{1,0:T(1,128)S(1)} %broadcast_in_dim.14), channel_id=1, source_target_pairs={{0,1},{1,0},{2,3},{3,2},{4,5},{5,4},{6,7},{7,6},{8,9},{9,8},{10,11... | collective-permute-start | bytes 20744 | tf_op jit(solution)/shard_map/ppermute | solution.py:47
  112.7 17.8 %collective-permute-start.5 = (bf16[2,144,1152]{2,1,0:T(8,128)(2,1)S(1)}, bf16[2,144,1152]{2,1,0:T(8,128)(2,1)S(1)}, u32[]{:S(2)}, u32[]{:S(2)}) collective-permute-start(bf16[2,144,1152]{2,1,0:T(8,128)(2,1)S(1)} %get-tuple-element.167), channel_id=1, source_target_pairs={{0,2},{1,3},{2,0},{3,1},{4,6},{5,7},{6,4},{7,5},{8,10},{9,11},{10,... | collective-permute-start | bytes 1990664 | tf_op jit(solution)/shard_map/ppermute | solution.py:47
  112.8 17.8 %collective-permute-start.6 = (bf16[2,144,1152]{2,1,0:T(8,128)(2,1)S(1)}, bf16[2,144,1152]{2,1,0:T(8,128)(2,1)S(1)}, u32[]{:S(2)}, u32[]{:S(2)}) collective-permute-start(bf16[2,144,1152]{2,1,0:T(8,128)(2,1)S(1)} %get-tuple-element.169), channel_id=1, source_target_pairs={{0,1},{1,0},{2,3},{3,2},{4,5},{5,4},{6,7},{7,6},{8,9},{9,8},{10,11... | collective-permute-start | bytes 1990664 | tf_op jit(solution)/shard_map/ppermute | solution.py:47
  114.5 20.4 %collective-permute-start.8 = (f32[2,1728]{1,0:T(2,128)S(1)}, f32[2,1728]{1,0:T(2,128)S(1)}, u32[]{:S(2)}, u32[]{:S(2)}) collective-permute-start(f32[2,1728]{1,0:T(2,128)S(1)} %pad_maximum_fusion.15), channel_id=1, source_target_pairs={{0,2},{1,3},{2,0},{3,1},{4,6},{5,7},{6,4},{7,5},{8,10},{9,11},{10,... | collective-permute-start | bytes 41480 | tf_op jit(solution)/shard_map/ppermute | solution.py:47
  130.9 21.6 %collective-permute-start.9 = (bf16[2,2,144,1152]{3,2,1,0:T(8,128)(2,1)S(1)}, bf16[2,2,144,1152]{3,2,1,0:T(8,128)(2,1)}, u32[]{:S(2)}, u32[]{:S(2)}) collective-permute-start(bf16[2,2,144,1152]{3,2,1,0:T(8,128)(2,1)S(1)} %pad_maximum_fusion.4), channel_id=1, source_target_pairs={{0,1},{1,0},{2,3},{3,2},{4,5},{5,4},{6,7},{7,6},{8,9},{9,8},{10,11... | collective-permute-start | bytes 3981320 | tf_op jit(solution)/shard_map/ppermute | solution.py:47
  132.9 20.3 %collective-permute-start.10 = (bf16[2,2,144,1152]{3,2,1,0:T(8,128)(2,1)S(1)}, bf16[2,2,144,1152]{3,2,1,0:T(8,128)(2,1)}, u32[]{:S(2)}, u32[]{:S(2)}) collective-permute-start(bf16[2,2,144,1152]{3,2,1,0:T(8,128)(2,1)S(1)} %pad_maximum_fusion.5), channel_id=1, source_target_pairs={{0,2},{1,3},{2,0},{3,1},{4,6},{5,7},{6,4},{7,5},{8,10},{9,11},{10,... | collective-permute-start | bytes 3981320 | tf_op jit(solution)/shard_map/ppermute | solution.py:47
  156.5 53.2 %collective-permute-start.11 = (bf16[2,2,2,144,1152]{4,3,2,0,1:T(8,128)(2,1)}, bf16[2,2,2,144,1152]{4,3,2,0,1:T(8,128)(2,1)}, u32[]{:S(2)}, u32[]{:S(2)}) collective-permute-start(bf16[2,2,2,144,1152]{4,3,2,0,1:T(8,128)(2,1)} %pad_maximum_fusion.1), channel_id=1, source_target_pairs={{0,16},{16,0},{1,17},{17,1},{2,18},{18,2},{3,19},{19,3},{4,20},{20... | collective-permute-start | bytes 7962632 | tf_op jit(solution)/shard_map/ppermute | solution.py:47
  160.2 49.6 %collective-permute-start.12 = (bf16[2,2,2,144,1152]{4,3,2,0,1:T(8,128)(2,1)}, bf16[2,2,2,144,1152]{4,3,2,0,1:T(8,128)(2,1)}, u32[]{:S(2)}, u32[]{:S(2)}) collective-permute-start(bf16[2,2,2,144,1152]{4,3,2,0,1:T(8,128)(2,1)} %copy.99), channel_id=1, source_target_pairs={{0,16},{16,0},{1,17},{17,1},{2,18},{18,2},{3,19},{19,3},{4,20},{20... | collective-permute-start | bytes 7962632 | tf_op jit(solution)/shard_map/ppermute | solution.py:47
  164.4 24.0 %collective-permute-start.14 = (f32[2,576]{1,0:T(2,128)S(1)}, f32[2,576]{1,0:T(2,128)S(1)}, u32[]{:S(2)}, u32[]{:S(2)}) collective-permute-start(f32[2,576]{1,0:T(2,128)S(1)} %pad_maximum_fusion.28), channel_id=1, source_target_pairs={{0,8},{4,12},{8,0},{12,4},{1,9},{5,13},{9,1},{13,5},{2,10},{6,14},... | collective-permute-start | bytes 13832 | tf_op jit(solution)/shard_map/ppermute | solution.py:47
  256.8 15.8 %collective-permute-start.15 = (bf16[4,576,1152]{2,1,0:T(8,128)(2,1)}, bf16[4,576,1152]{2,1,0:T(8,128)(2,1)}, u32[]{:S(2)}, u32[]{:S(2)}) collective-permute-start(bf16[4,576,1152]{2,1,0:T(8,128)(2,1)} %weight_grads_near.8), channel_id=1, source_target_pairs={{0,16},{16,0},{1,17},{17,1},{2,18},{18,2},{3,19},{19,3},{4,20},{20... | collective-permute-start | bytes 15925256 | tf_op jit(solution)/shard_map/ppermute | solution.py:47
  280.4 52.1 %collective-permute-start.18 = (bf16[4,576,1152]{2,1,0:T(8,128)(2,1)}, bf16[4,576,1152]{2,1,0:T(8,128)(2,1)}, u32[]{:S(2)}, u32[]{:S(2)}) collective-permute-start(bf16[4,576,1152]{2,1,0:T(8,128)(2,1)} %weight_grads_near.10), channel_id=1, source_target_pairs={{0,16},{16,0},{1,17},{17,1},{2,18},{18,2},{3,19},{19,3},{4,20},{20... | collective-permute-start | bytes 15925256 | tf_op jit(solution)/shard_map/ppermute | solution.py:47
  299.5 31.6 %collective-permute-start.16 = (bf16[2,288,1152]{2,1,0:T(8,128)(2,1)}, bf16[2,288,1152]{2,1,0:T(8,128)(2,1)}, u32[]{:S(2)}, u32[]{:S(2)}) collective-permute-start(bf16[2,288,1152]{2,1,0:T(8,128)(2,1)} %get-tuple-element.192), channel_id=1, source_target_pairs={{0,1},{1,0},{2,3},{3,2},{4,5},{5,4},{6,7},{7,6},{8,9},{9,8},{10,11... | collective-permute-start | bytes 3981320 | tf_op jit(solution)/shard_map/ppermute | solution.py:47
  301.1 31.4 %collective-permute-start.17 = (bf16[2,288,1152]{2,1,0:T(8,128)(2,1)}, bf16[2,288,1152]{2,1,0:T(8,128)(2,1)}, u32[]{:S(2)}, u32[]{:S(2)}) collective-permute-start(bf16[2,288,1152]{2,1,0:T(8,128)(2,1)} %get-tuple-element.193), channel_id=1, source_target_pairs={{0,2},{1,3},{2,0},{3,1},{4,6},{5,7},{6,4},{7,5},{8,10},{9,11},{10,... | collective-permute-start | bytes 3981320 | tf_op jit(solution)/shard_map/ppermute | solution.py:47
  348.8 41.0 %collective-permute-start.19 = (f32[7,1152]{1,0:T(8,128)S(1)}, f32[7,1152]{1,0:T(8,128)S(1)}, u32[]{:S(2)}, u32[]{:S(2)}) collective-permute-start(f32[7,1152]{1,0:T(8,128)S(1)} %select_maximum_fusion), channel_id=1, source_target_pairs={{0,16},{16,0},{1,17},{17,1},{2,18},{18,2},{3,19},{19,3},{4,20},{20... | collective-permute-start | bytes 96776 | tf_op jit(solution)/shard_map/ppermute | solution.py:47
  352.0 37.7 %collective-permute-start.20 = (bf16[288,1152]{1,0:T(8,128)(2,1)}, bf16[288,1152]{1,0:T(8,128)(2,1)S(1)}, u32[]{:S(2)}, u32[]{:S(2)}) collective-permute-start(bf16[288,1152]{1,0:T(8,128)(2,1)} %get-tuple-element.373), channel_id=1, source_target_pairs={{0,2},{1,3},{2,0},{3,1},{4,6},{5,7},{6,4},{7,5},{8,10},{9,11},{10,... | collective-permute-start | bytes 1990664 | tf_op jit(solution)/shard_map/ppermute | solution.py:47
  356.3 33.4 %collective-permute-start.21 = (bf16[288,1152]{1,0:T(8,128)(2,1)}, bf16[288,1152]{1,0:T(8,128)(2,1)}, u32[]{:S(2)}, u32[]{:S(2)}) collective-permute-start(bf16[288,1152]{1,0:T(8,128)(2,1)} %get-tuple-element.371), channel_id=1, source_target_pairs={{0,1},{1,0},{2,3},{3,2},{4,5},{5,4},{6,7},{7,6},{8,9},{9,8},{10,11... | collective-permute-start | bytes 1990664 | tf_op jit(solution)/shard_map/ppermute | solution.py:47
  366.4 35.6 %collective-permute-start.22 = (bf16[2,288,1152]{2,1,0:T(8,128)(2,1)}, bf16[2,288,1152]{2,1,0:T(8,128)(2,1)}, u32[]{:S(2)}, u32[]{:S(2)}) collective-permute-start(bf16[2,288,1152]{2,1,0:T(8,128)(2,1)} %get-tuple-element.208), channel_id=1, source_target_pairs={{0,1},{1,0},{2,3},{3,2},{4,5},{5,4},{6,7},{7,6},{8,9},{9,8},{10,11... | collective-permute-start | bytes 3981320 | tf_op jit(solution)/shard_map/ppermute | solution.py:47
  367.9 34.1 %collective-permute-start.23 = (bf16[2,288,1152]{2,1,0:T(8,128)(2,1)}, bf16[2,288,1152]{2,1,0:T(8,128)(2,1)}, u32[]{:S(2)}, u32[]{:S(2)}) collective-permute-start(bf16[2,288,1152]{2,1,0:T(8,128)(2,1)} %get-tuple-element.209), channel_id=1, source_target_pairs={{0,2},{1,3},{2,0},{3,1},{4,6},{5,7},{6,4},{7,5},{8,10},{9,11},{10,... | collective-permute-start | bytes 3981320 | tf_op jit(solution)/shard_map/ppermute | solution.py:47
  411.7 29.6 %collective-permute-start.28 = (bf16[4,576,720]{2,1,0:T(8,128)(2,1)}, bf16[4,576,720]{2,1,0:T(8,128)(2,1)}, u32[]{:S(2)}, u32[]{:S(2)}) collective-permute-start(bf16[4,576,720]{2,1,0:T(8,128)(2,1)} %weight_grads_near.12), channel_id=1, source_target_pairs={{0,16},{16,0},{1,17},{17,1},{2,18},{18,2},{3,19},{19,3},{4,20},{20... | collective-permute-start | bytes 9953288 | tf_op jit(solution)/shard_map/ppermute | solution.py:47
  411.8 28.5 %collective-permute-start.24 = (f32[7,1152]{1,0:T(8,128)S(1)}, f32[7,1152]{1,0:T(8,128)S(1)}, u32[]{:S(2)}, u32[]{:S(2)}) collective-permute-start(f32[7,1152]{1,0:T(8,128)S(1)} %maximum_select_fusion.4), channel_id=1, source_target_pairs={{0,4},{4,0},{8,12},{12,8},{1,5},{5,1},{9,13},{13,9},{2,6},{6,2},{1... | collective-permute-start | bytes 96776 | tf_op jit(solution)/shard_map/ppermute | solution.py:47
  418.2 22.1 %collective-permute-start.25 = (bf16[2,144,1152]{2,1,0:T(8,128)(2,1)}, bf16[2,144,1152]{2,1,0:T(8,128)(2,1)}, u32[]{:S(2)}, u32[]{:S(2)}) collective-permute-start(bf16[2,144,1152]{2,1,0:T(8,128)(2,1)} %get-tuple-element.391), channel_id=1, source_target_pairs={{0,4},{4,0},{8,12},{12,8},{1,5},{5,1},{9,13},{13,9},{2,6},{6,2},{1... | collective-permute-start | bytes 1990664 | tf_op jit(solution)/shard_map/ppermute | solution.py:47
  421.0 19.3 %collective-permute-start.26 = (bf16[288,1152]{1,0:T(8,128)(2,1)}, bf16[288,1152]{1,0:T(8,128)(2,1)S(1)}, u32[]{:S(2)}, u32[]{:S(2)}) collective-permute-start(bf16[288,1152]{1,0:T(8,128)(2,1)} %get-tuple-element.369), channel_id=1, source_target_pairs={{0,2},{1,3},{2,0},{3,1},{4,6},{5,7},{6,4},{7,5},{8,10},{9,11},{10,... | collective-permute-start | bytes 1990664 | tf_op jit(solution)/shard_map/ppermute | solution.py:47
  424.2 17.0 %collective-permute-start.27 = (bf16[288,1152]{1,0:T(8,128)(2,1)}, bf16[288,1152]{1,0:T(8,128)(2,1)}, u32[]{:S(2)}, u32[]{:S(2)}) collective-permute-start(bf16[288,1152]{1,0:T(8,128)(2,1)} %get-tuple-element.367), channel_id=1, source_target_pairs={{0,1},{1,0},{2,3},{3,2},{4,5},{5,4},{6,7},{7,6},{8,9},{9,8},{10,11... | collective-permute-start | bytes 1990664 | tf_op jit(solution)/shard_map/ppermute | solution.py:47
  441.3 38.9 %collective-permute-start.29 = (f32[7,1152]{1,0:T(8,128)S(1)}, f32[7,1152]{1,0:T(8,128)S(1)}, u32[]{:S(2)}, u32[]{:S(2)}) collective-permute-start(f32[7,1152]{1,0:T(8,128)S(1)} %maximum_select_fusion.3), channel_id=1, source_target_pairs={{0,8},{4,12},{8,0},{12,4},{1,9},{5,13},{9,1},{13,5},{2,10},{6,14},... | collective-permute-start | bytes 96776 | tf_op jit(solution)/shard_map/ppermute | solution.py:47
  447.2 33.0 %collective-permute-start.30 = (bf16[144,1152]{1,0:T(8,128)(2,1)}, bf16[144,1152]{1,0:T(8,128)(2,1)}, u32[]{:S(2)}, u32[]{:S(2)}) collective-permute-start(bf16[144,1152]{1,0:T(8,128)(2,1)} %get-tuple-element.412), channel_id=1, source_target_pairs={{0,8},{4,12},{8,0},{12,4},{1,9},{5,13},{9,1},{13,5},{2,10},{6,14},... | collective-permute-start | bytes 995336 | tf_op jit(solution)/shard_map/ppermute | solution.py:47
  450.0 30.2 %collective-permute-start.31 = (bf16[2,144,1152]{2,1,0:T(8,128)(2,1)}, bf16[2,144,1152]{2,1,0:T(8,128)(2,1)S(1)}, u32[]{:S(2)}, u32[]{:S(2)}) collective-permute-start(bf16[2,144,1152]{2,1,0:T(8,128)(2,1)} %get-tuple-element.389), channel_id=1, source_target_pairs={{0,4},{4,0},{8,12},{12,8},{1,5},{5,1},{9,13},{13,9},{2,6},{6,2},{1... | collective-permute-start | bytes 1990664 | tf_op jit(solution)/shard_map/ppermute | solution.py:47
  462.3 20.6 %collective-permute-start.32 = (bf16[2,288,720]{2,1,0:T(8,128)(2,1)}, bf16[2,288,720]{2,1,0:T(8,128)(2,1)}, u32[]{:S(2)}, u32[]{:S(2)}) collective-permute-start(bf16[2,288,720]{2,1,0:T(8,128)(2,1)} %get-tuple-element.240), channel_id=1, source_target_pairs={{0,1},{1,0},{2,3},{3,2},{4,5},{5,4},{6,7},{7,6},{8,9},{9,8},{10,11... | collective-permute-start | bytes 2488328 | tf_op jit(solution)/shard_map/ppermute | solution.py:47
  463.8 20.4 %collective-permute-start.33 = (bf16[2,288,720]{2,1,0:T(8,128)(2,1)}, bf16[2,288,720]{2,1,0:T(8,128)(2,1)}, u32[]{:S(2)}, u32[]{:S(2)}) collective-permute-start(bf16[2,288,720]{2,1,0:T(8,128)(2,1)} %get-tuple-element.241), channel_id=1, source_target_pairs={{0,2},{1,3},{2,0},{3,1},{4,6},{5,7},{6,4},{7,5},{8,10},{9,11},{10,... | collective-permute-start | bytes 2488328 | tf_op jit(solution)/shard_map/ppermute | solution.py:47
  484.3 27.0 %collective-permute-start.34 = (f32[7,1152]{1,0:T(8,128)S(1)}, f32[7,1152]{1,0:T(8,128)S(1)}, u32[]{:S(2)}, u32[]{:S(2)}) collective-permute-start(f32[7,1152]{1,0:T(8,128)S(1)} %maximum_select_fusion.2), channel_id=1, source_target_pairs={{0,1},{1,0},{2,3},{3,2},{4,5},{5,4},{6,7},{7,6},{8,9},{9,8},{10,11... | collective-permute-start | bytes 96776 | tf_op jit(solution)/shard_map/ppermute | solution.py:47
  486.6 42.2 %collective-permute-start.35 = (bf16[144,1152]{1,0:T(8,128)(2,1)}, bf16[144,1152]{1,0:T(8,128)(2,1)}, u32[]{:S(2)}, u32[]{:S(2)}) collective-permute-start(bf16[144,1152]{1,0:T(8,128)(2,1)} %add_convert_fusion.24), channel_id=1, source_target_pairs={{0,16},{16,0},{1,17},{17,1},{2,18},{18,2},{3,19},{19,3},{4,20},{20... | collective-permute-start | bytes 995336 | tf_op jit(solution)/shard_map/ppermute | solution.py:47
  499.1 29.7 %collective-permute-start.39 = (bf16[4,576,432]{1,2,0:T(8,128)(2,1)}, bf16[4,576,432]{1,2,0:T(8,128)(2,1)}, u32[]{:S(2)}, u32[]{:S(2)}) collective-permute-start(bf16[4,576,432]{1,2,0:T(8,128)(2,1)} %copy.109), channel_id=1, source_target_pairs={{0,16},{16,0},{1,17},{17,1},{2,18},{18,2},{3,19},{19,3},{4,20},{20... | collective-permute-start | bytes 5971976 | tf_op jit(solution)/shard_map/ppermute | solution.py:47
  502.0 26.8 %collective-permute-start.36 = (bf16[144,1152]{1,0:T(8,128)(2,1)}, bf16[144,1152]{1,0:T(8,128)(2,1)S(1)}, u32[]{:S(2)}, u32[]{:S(2)}) collective-permute-start(bf16[144,1152]{1,0:T(8,128)(2,1)} %get-tuple-element.410), channel_id=1, source_target_pairs={{0,8},{4,12},{8,0},{12,4},{1,9},{5,13},{9,1},{13,5},{2,10},{6,14},... | collective-permute-start | bytes 995336 | tf_op jit(solution)/shard_map/ppermute | solution.py:47
  506.8 22.0 %collective-permute-start.37 = (bf16[288,720]{1,0:T(8,128)(2,1)}, bf16[288,720]{1,0:T(8,128)(2,1)}, u32[]{:S(2)}, u32[]{:S(2)}) collective-permute-start(bf16[288,720]{1,0:T(8,128)(2,1)} %get-tuple-element.387), channel_id=1, source_target_pairs={{0,2},{1,3},{2,0},{3,1},{4,6},{5,7},{6,4},{7,5},{8,10},{9,11},{10,... | collective-permute-start | bytes 1244168 | tf_op jit(solution)/shard_map/ppermute | solution.py:47
  511.3 17.6 %collective-permute-start.38 = (bf16[288,720]{1,0:T(8,128)(2,1)}, bf16[288,720]{1,0:T(8,128)(2,1)}, u32[]{:S(2)}, u32[]{:S(2)}) collective-permute-start(bf16[288,720]{1,0:T(8,128)(2,1)} %get-tuple-element.385), channel_id=1, source_target_pairs={{0,1},{1,0},{2,3},{3,2},{4,5},{5,4},{6,7},{7,6},{8,9},{9,8},{10,11... | collective-permute-start | bytes 1244168 | tf_op jit(solution)/shard_map/ppermute | solution.py:47
  531.7 35.3 %collective-permute-start.40 = (bf16[512,1152]{1,0:T(8,128)(2,1)}, bf16[512,1152]{1,0:T(8,128)(2,1)}, u32[]{:S(2)}, u32[]{:S(2)}) collective-permute-start(bf16[512,1152]{1,0:T(8,128)(2,1)} %slice.462), channel_id=1, source_target_pairs={{4,0},{0,4},{12,8},{8,12},{5,1},{1,5},{13,9},{9,13},{6,2},{2,6},{1... | collective-permute-start | bytes 3538952 | tf_op jit(solution)/shard_map/ppermute | solution.py:662
  532.2 38.7 %collective-permute-start.41 = (f32[7,1152]{1,0:T(8,128)S(1)}, f32[7,1152]{1,0:T(8,128)S(1)}, u32[]{:S(2)}, u32[]{:S(2)}) collective-permute-start(f32[7,1152]{1,0:T(8,128)S(1)} %maximum_select_fusion.1), channel_id=1, source_target_pairs={{0,2},{1,3},{2,0},{3,1},{4,6},{5,7},{6,4},{7,5},{8,10},{9,11},{10,... | collective-permute-start | bytes 96776 | tf_op jit(solution)/shard_map/ppermute | solution.py:47
  533.4 37.5 %collective-permute-start.42 = (bf16[144,1152]{1,0:T(8,128)(2,1)}, bf16[144,1152]{1,0:T(8,128)(2,1)}, u32[]{:S(2)}, u32[]{:S(2)}) collective-permute-start(bf16[144,1152]{1,0:T(8,128)(2,1)} %add_convert_fusion.23), channel_id=1, source_target_pairs={{0,16},{16,0},{1,17},{17,1},{2,18},{18,2},{3,19},{19,3},{4,20},{20... | collective-permute-start | bytes 995336 | tf_op jit(solution)/shard_map/ppermute | solution.py:47
  536.6 34.3 %collective-permute-start.43 = (bf16[2,144,720]{2,1,0:T(8,128)(2,1)}, bf16[2,144,720]{2,1,0:T(8,128)(2,1)}, u32[]{:S(2)}, u32[]{:S(2)}) collective-permute-start(bf16[2,144,720]{2,1,0:T(8,128)(2,1)} %get-tuple-element.404), channel_id=1, source_target_pairs={{0,4},{4,0},{8,12},{12,8},{1,5},{5,1},{9,13},{13,9},{2,6},{6,2},{1... | collective-permute-start | bytes 1244168 | tf_op jit(solution)/shard_map/ppermute | solution.py:47
  551.1 19.8 %collective-permute-start.44 = (bf16[2,288,432]{2,1,0:T(8,128)(2,1)}, bf16[2,288,432]{2,1,0:T(8,128)(2,1)S(1)}, u32[]{:S(2)}, u32[]{:S(2)}) collective-permute-start(bf16[2,288,432]{2,1,0:T(8,128)(2,1)} %get-tuple-element.268), channel_id=1, source_target_pairs={{0,1},{1,0},{2,3},{3,2},{4,5},{5,4},{6,7},{7,6},{8,9},{9,8},{10,11... | collective-permute-start | bytes 1493000 | tf_op jit(solution)/shard_map/ppermute | solution.py:47
  567.1 15.2 %collective-permute-start.45 = (bf16[2,288,432]{2,1,0:T(8,128)(2,1)S(1)}, bf16[2,288,432]{2,1,0:T(8,128)(2,1)S(1)}, u32[]{:S(2)}, u32[]{:S(2)}) collective-permute-start(bf16[2,288,432]{2,1,0:T(8,128)(2,1)S(1)} %copy-done.68), channel_id=1, source_target_pairs={{0,2},{1,3},{2,0},{3,1},{4,6},{5,7},{6,4},{7,5},{8,10},{9,11},{10,... | collective-permute-start | bytes 1493000 | tf_op jit(solution)/shard_map/ppermute | solution.py:47
  590.3 33.7 %collective-permute-start.54 = (bf16[288,432]{1,0:T(8,128)(2,1)}, bf16[288,432]{1,0:T(8,128)(2,1)}, u32[]{:S(2)}, u32[]{:S(2)}) collective-permute-start(bf16[288,432]{1,0:T(8,128)(2,1)} %fusion.37), channel_id=1, source_target_pairs={{0,2},{1,3},{2,0},{3,1},{4,6},{5,7},{6,4},{7,5},{8,10},{9,11},{10,... | collective-permute-start | bytes 746504 | tf_op jit(solution)/shard_map/ppermute | solution.py:47
  593.5 31.5 %collective-permute-start.55 = (bf16[288,432]{1,0:T(8,128)(2,1)}, bf16[288,432]{1,0:T(8,128)(2,1)}, u32[]{:S(2)}, u32[]{:S(2)}) collective-permute-start(bf16[288,432]{1,0:T(8,128)(2,1)} %fusion.39), channel_id=1, source_target_pairs={{0,1},{1,0},{2,3},{3,2},{4,5},{5,4},{6,7},{7,6},{8,9},{9,8},{10,11... | collective-permute-start | bytes 746504 | tf_op jit(solution)/shard_map/ppermute | solution.py:47
  596.3 26.0 %collective-permute-start.52 = (bf16[144,720]{1,0:T(8,128)(2,1)S(1)}, bf16[144,720]{1,0:T(8,128)(2,1)}, u32[]{:S(2)}, u32[]{:S(2)}) collective-permute-start(bf16[144,720]{1,0:T(8,128)(2,1)S(1)} %dynamic-slice_bitcast_fusion.5), channel_id=1, source_target_pairs={{0,8},{4,12},{8,0},{12,4},{1,9},{5,13},{9,1},{13,5},{2,10},{6,14},... | collective-permute-start | bytes 622088 | tf_op jit(solution)/shard_map/ppermute | solution.py:47
  (83 other events, 1096.5 us)
Sparse Core Ops, SparseCore 0:
  11.6 108.0 all-gather.2
  123.3 97.5 all-gather.4

commit v3 on v2

--- a/solution.py
+++ b/solution.py
@@ -98,47 +98,17 @@
     return full.reshape(lax.axis_size("gy"), -1, shard.shape[1])
 
 
-def join_pair(values, other, axis, bit):
-    low = (lax.axis_index(axis) & bit) == 0
-    return jnp.stack([jnp.where(low, values, other), jnp.where(low, other, values)])
-
-
-def gather_steps(shard):
-    mine = own_half(shard)
-    cols = shard.shape[1]
-    if (lax.axis_size("gy"), lax.axis_size("gx")) != (4, 4):
-        yield gather_weight(shard)
-        return
-    mine, got = yield (mine, swap(mine, "gx", 2))
-    pair = join_pair(mine, got, "gx", 2)
-    pair, got = yield (pair, swap(pair, "gx", 1))
-    quad = join_pair(pair, got, "gx", 1)
-    one, two = quad[:, 0], quad[:, 1]
-    one, two, got_one, got_two = yield (one, two, swap(one, "gy", 2), swap(two, "gy", 1))
-    one, two = join_pair(one, got_one, "gy", 2), join_pair(two, got_two, "gy", 1)
-    one, two, got_one, got_two = yield (one, two, swap(one, "gy", 1), swap(two, "gy", 2))
-    one, two = join_pair(one, got_one, "gy", 1), join_pair(two, got_two, "gy", 2)
-    one, two, got_one, got_two = yield (one, two, swap(one, "dp", 1), swap(two, "dp", 1))
-    low = lax.axis_index("dp") == 0
-
-    def rows_of(values, got):
-        return jnp.stack([jnp.where(low, values, got), jnp.where(low, got, values)], axis=3)
-
-    one = jnp.swapaxes(rows_of(one, got_one), 0, 1)
-    yield jnp.stack([one, rows_of(two, got_two)], axis=2).reshape(4, -1, cols)
-
-
 def cube_mesh():
     return (lax.axis_size("gy"), lax.axis_size("gx"), lax.axis_size("dp")) == (4, 4, 2)
 
 
-def scatter_steps(lefts, picks, rights):
+def scatter_steps(order, lefts, picks, rights):
     size_gx = lax.axis_size("gx")
     at_gy, at_gx, at_dp = lax.axis_index("gy"), lax.axis_index("gx"), lax.axis_index("dp")
     if cube_mesh():
-        other = weight_grads_near(lefts, picks, rights, 1 - at_dp)
+        other = weight_grads_near(order, lefts, picks, rights, 1 - at_dp)
         (got,) = yield (swap(other, "dp", 1),)
-        one, send_one, two, send_two = weight_grads_near(lefts, picks, rights, at_dp, got)
+        one, send_one, two, send_two = weight_grads_near(order, lefts, picks, rights, at_dp, got)
         one, two, got_one, got_two = yield (
             one,
             two,
@@ -160,7 +130,7 @@
         acc = add_low(acc, got)
     else:
         other, mine = [
-            weight_grads([half_rows(x, w) for x in lefts], picks, rights)
+            weight_grads(order, [half_rows(x, w) for x in lefts], picks, rights)
             for w in (1 - at_dp, at_dp)
         ]
         got, mine = yield (swap(other, "dp", 1), mine)
@@ -189,15 +159,20 @@
         return self.state
 
 
-def tick(value, *exchanges):
-    live = [x for x in exchanges if not x.done]
-    if not live:
-        return value
-    value, states = lax.optimization_barrier((value, [x.state for x in live]))
-    for x, state in zip(live, states):
-        x.state = state
-        x.advance()
-    return value
+class Order:
+    def __init__(self):
+        self.token = jnp.zeros((8, 128), F32)
+
+    def tick(self, *exchanges):
+        live = [x for x in exchanges if not x.done]
+        self.token, states = lax.optimization_barrier((self.token, [x.state for x in live]))
+        for x, state in zip(live, states):
+            x.state = state
+            x.advance()
+
+
+ORDER_SPEC = pl.BlockSpec((8, 128), lambda *_: (0, 0))
+ORDER_SHAPE = jax.ShapeDtypeStruct((8, 128), F32)
 
 
 def half_rows(values, which):
@@ -222,29 +197,54 @@
     return jnp.dot(left, right, preferred_element_type=F32)
 
 
-def by_group(kernel, name, whole, grouped, outs, flops, whole_out=None, scratch=()):
+def by_group(order, kernel, name, whole, grouped, outs, flops, whole_outs=(), scratch=()):
+    parts = [x[1] if isinstance(x, tuple) else (x.shape[2], 0) for x in grouped]
+    grouped = [x[0] if isinstance(x, tuple) else x for x in grouped]
     g = grouped[0].shape[0]
 
-    def block(x):
-        return pl.BlockSpec((1,) + tuple(x.shape[1:]), lambda i: (i, 0, 0))
+    def block(rows, cols, k=0):
+        return pl.BlockSpec((1, rows, cols), lambda i: (i, 0, k))
+
+    def in_order(order_ref, *refs):
+        inputs = len(whole) + len(grouped)
+        refs[inputs][...] = order_ref[...]
+        kernel(*refs[:inputs], *refs[inputs + 1 :])
 
     shapes = [jax.ShapeDtypeStruct((g,) + shape, kind) for shape, kind in outs]
-    specs = [block(x) for x in shapes]
-    if whole_out is not None:
-        shapes.append(jax.ShapeDtypeStruct(whole_out, F32))
-        specs.append(pl.BlockSpec(whole_out, lambda i: (0, 0)))
+    specs = [block(*x.shape[1:]) for x in shapes]
+    for shape, kind in whole_outs:
+        shapes.append(jax.ShapeDtypeStruct(shape, kind))
+        specs.append(pl.BlockSpec(shape, lambda i: (0, 0)))
     moved = sum(x.size * x.dtype.itemsize for x in [*whole, *grouped, *shapes])
-    return pl.pallas_call(
-        kernel,
-        out_shape=shapes,
+    order.token, *results = pl.pallas_call(
+        in_order,
+        out_shape=[ORDER_SHAPE, *shapes],
         grid=(g,),
-        in_specs=[pl.BlockSpec(x.shape, lambda i: (0, 0)) for x in whole]
-        + [block(x) for x in grouped],
-        out_specs=specs,
+        in_specs=[ORDER_SPEC]
+        + [pl.BlockSpec(x.shape, lambda i: (0, 0)) for x in whole]
+        + [block(x.shape[1], *part) for x, part in zip(grouped, parts)],
+        out_specs=[ORDER_SPEC, *specs],
         scratch_shapes=scratch,
         cost_estimate=pl.CostEstimate(flops=flops * g, transcendentals=0, bytes_accessed=moved),
         name=name,
-    )(*whole, *grouped)
+    )(order.token, *whole, *grouped)
+    return results
+
+
+def transposed(order, *arrays):
+    count = len(arrays)
+
+    def kernel(order_ref, *refs):
+        refs[count][...] = order_ref[...]
+        for x_ref, out_ref in zip(refs[:count], refs[count + 1 :]):
+            out_ref[...] = x_ref[...].T
+
+    order.token, *results = pl.pallas_call(
+        kernel,
+        out_shape=[ORDER_SHAPE, *[jax.ShapeDtypeStruct(x.shape[::-1], BF) for x in arrays]],
+        name="transposed",
+    )(order.token, *arrays)
+    return results
 
 
 def edges_of(rights):
@@ -254,7 +254,7 @@
     return edges
 
 
-def weight_grads(lefts, picks, rights):
+def weight_grads(order, lefts, picks, rights):
     m, edges = lefts[0].shape[0], edges_of(rights)
 
     def kernel(*refs):
@@ -265,19 +265,23 @@
             ).astype(BF)
 
     flops = sum(2 * m * x.shape[1] * x.shape[2] for x in rights)
-    return by_group(kernel, "weight_grads", lefts, rights, [((m, edges[-1]), BF)], flops)[0]
-
-
-def weight_grads_near(lefts, picks, rights, side, got=None):
+    return by_group(order, kernel, "weight_grads", lefts, rights, [((m, edges[-1]), BF)], flops)[0]
+
+
+def weight_grads_near(order, lefts, picks, rights, side, got=None):
     size_gx = lax.axis_size("gx")
     lefts = [x.reshape(size_gx, 2, -1, x.shape[1]) for x in lefts]
     m, edges = size_gx * lefts[0].shape[2], edges_of(rights)
-    n, part = edges[-1], m // 2
-
-    def kernel(place_ref, *refs):
+    n, part = -(-edges[-1] // 128) * 128, m // 2
+
+    def kernel(place_ref, order_ref, *refs):
         left_refs, right_refs = refs[: len(lefts)], refs[len(lefts) : len(lefts) + len(rights)]
         rest = refs[len(lefts) + len(rights) :]
+        if got is not None:
+            got_ref, rest = rest[0], rest[1:]
         step = pl.program_id(0)
+        rest[0][...] = order_ref[...]
+        rest = rest[1:]
 
         def product(i):
             right = right_refs[i][0]
@@ -287,12 +291,15 @@
         if got is None:
             for i in range(len(rights)):
                 rest[0][0, :, edges[i] : edges[i + 1]] = product(i).astype(BF)
+            if n > edges[-1]:
+                rest[0][0, :, edges[-1] :] = jnp.zeros((m, n - edges[-1]), BF)
             return
-        got_ref, one_ref, send_one_ref, two_ref, send_two_ref = rest[:5]
-        sum_ref = rest[5]
+        one_ref, send_one_ref, two_ref, send_two_ref, sum_ref = rest
         for i in range(len(rights)):
             at = slice(edges[i], edges[i + 1])
             sum_ref[:, at] = (product(i) + got_ref[0, :, at].astype(F32)).astype(BF)
+        if n > edges[-1]:
+            sum_ref[:, edges[-1] :] = jnp.zeros((m, n - edges[-1]), BF)
 
         for ref, rows, wanted in (
             (one_ref, slice(0, part), step % 2 == 0),
@@ -306,14 +313,14 @@
                 ref[0] = sum_ref[rows, :]
 
     place = jnp.stack([side, lax.axis_index("gy")]).astype(jnp.int32)
-    in_specs = [
+    in_specs = [ORDER_SPEC] + [
         pl.BlockSpec((size_gx, 1) + x.shape[2:], lambda i, p: (0, p[0], 0, 0)) for x in lefts
     ] + [pl.BlockSpec((1,) + x.shape[1:], lambda i, p: (i ^ p[1], 0, 0)) for x in rights]
-    operands = [*lefts, *rights]
+    operands = [order.token, *lefts, *rights]
     scratch = []
     if got is None:
-        shapes = jax.ShapeDtypeStruct((4, m, n), BF)
-        out_specs = pl.BlockSpec((1, m, n), lambda i, p: (i, 0, 0))
+        shapes = [jax.ShapeDtypeStruct((4, m, n), BF)]
+        out_specs = [pl.BlockSpec((1, m, n), lambda i, p: (i, 0, 0))]
     else:
         operands.append(got)
         in_specs.append(pl.BlockSpec((1, m, n), lambda i, p: (i, 0, 0)))
@@ -327,23 +334,25 @@
         scratch = [pltpu.VMEM((m, n), BF)]
     flops = sum(8 * m * x.shape[1] * x.shape[2] for x in rights)
     moved = 8 * m * n * (1 if got is None else 2) + sum(2 * x.size for x in rights)
-    return pl.pallas_call(
+    order.token, *results = pl.pallas_call(
         kernel,
-        out_shape=shapes,
+        out_shape=[ORDER_SHAPE, *shapes],
         grid_spec=pltpu.PrefetchScalarGridSpec(
             num_scalar_prefetch=1,
             grid=(4,),
             in_specs=in_specs,
-            out_specs=out_specs,
+            out_specs=[ORDER_SPEC, *out_specs],
             scratch_shapes=scratch,
         ),
         cost_estimate=pl.CostEstimate(flops=flops, transcendentals=0, bytes_accessed=moved),
         name="weight_grads_near",
     )(place, *operands)
-
-
-def project_back(xs, weight, terms, init=None):
-    width, w_cols = weight.shape[1:]
+    return results[0] if got is None else results
+
+
+def project_back(order, xs, weight, terms, init=None, own=None):
+    weight, (w_cols, part) = weight if isinstance(weight, tuple) else (weight, (weight.shape[2], 0))
+    width = weight.shape[1]
     rows = xs[0].shape[1] if init is None else init.shape[0]
     rows = max([rows] + [x.shape[1] for x in xs])
     windows = []
@@ -356,8 +365,10 @@
     def kernel(*refs):
         refs = list(refs)
         init_ref = refs.pop(0) if whole else None
-        x_refs, w_ref, out_ref = refs[: len(xs)], refs[len(xs)], refs[len(xs) + 1]
-        wide_refs = refs[len(xs) + 2 :]
+        x_refs, w_ref = refs[: len(xs)], refs[len(xs)]
+        refs = refs[len(xs) + 1 :]
+        low_ref = refs.pop(0) if own is not None else None
+        out_ref, wide_refs = refs[0], refs[1:]
 
         @pl.when(pl.program_id(0) == 0)
         def _():
@@ -379,19 +390,35 @@
             parts[r] = parts[r] + part if r in parts else part
         for r, part in parts.items():
             out_ref[:r] += part
+        if low_ref is not None:
+
+            @pl.when(pl.program_id(0) == pl.num_programs(0) - 1)
+            def _():
+                low_ref[...] = out_ref[own:].astype(BF)
 
     scratch = [
         pltpu.VMEM((x.shape[1], w[1] - w[0]), BF) for x, w, pad in zip(xs, windows, padded) if pad
     ]
     flops = sum(2 * x.shape[1] * width * x.shape[2] for x in xs)
-    return by_group(
-        kernel, "project_back", whole, [*xs, weight], [], flops, (rows, width), scratch
-    )[0]
-
-
-def project_qkv(hidden, rows, weight, bias_q, bias_v):
+    wholes = [] if own is None else [((rows - own, width), BF)]
+    wholes.append(((rows, width), F32))
+    results = by_group(
+        order,
+        kernel,
+        "project_back",
+        whole,
+        [*xs, (weight, (w_cols, part))],
+        [],
+        flops,
+        wholes,
+        scratch,
+    )
+    return results[0] if own is None else results
+
+
+def project_qkv(order, hidden, rows, weight, bias_q, bias_v):
     ctx, width = hidden.shape
-    n = weight.shape[2] // 4
+    n = bias_q.shape[2]
 
     def kernel(h_ref, w_ref, bq_ref, bv_ref, q_ref, k_ref, v_ref):
         joint = dot_n(h_ref[...], w_ref[0, :, : 3 * n])
@@ -400,6 +427,7 @@
         v_ref[0] = (joint[:, 2 * n :] + bv_ref[0]).astype(BF)
 
     return by_group(
+        order,
         kernel,
         "project_qkv",
         [hidden],
@@ -409,7 +437,7 @@
     )
 
 
-def project_up(hidden, weight, bias):
+def project_up(order, hidden, weight, bias):
     rows, width = hidden.shape
     n = bias.shape[2]
 
@@ -419,6 +447,7 @@
         slope_ref[0] = slope.astype(BF)
 
     return by_group(
+        order,
         kernel,
         "project_up",
         [hidden],
@@ -428,7 +457,7 @@
     )
 
 
-def project_act_back(grad_mlp, weight, slope):
+def project_act_back(order, grad_mlp, weight, slope):
     rows, width = grad_mlp.shape
     n = slope.shape[2]
 
@@ -438,6 +467,7 @@
         sums_ref[0] = jnp.sum(grad, axis=0, keepdims=True)
 
     return by_group(
+        order,
         kernel,
         "project_act_back",
         [grad_mlp],
@@ -447,16 +477,20 @@
     )
 
 
-def project_mixed_back(grad_attn, weight):
+def project_mixed_back(order, grad_attn, weight, n, skip):
     rows, width = grad_attn.shape
-    n = weight.shape[2] // 4
-    low = 3 * n // 128 * 128
 
     def kernel(g_ref, w_ref, out_ref):
-        out_ref[0] = dot_n(g_ref[...], w_ref[0, :, low:])[:, 3 * n - low :].astype(BF)
+        out_ref[0] = dot_n(g_ref[...], w_ref[0])[:, skip:].astype(BF)
 
     return by_group(
-        kernel, "project_mixed_back", [grad_attn], [weight], [((rows, n), BF)], 2 * rows * width * n
+        order,
+        kernel,
+        "project_mixed_back",
+        [grad_attn],
+        [weight],
+        [((rows, n), BF)],
+        2 * rows * width * n,
     )[0]
 
 
@@ -464,7 +498,7 @@
     return ref[0, :, h * HD : (h + 1) * HD]
 
 
-def attend(queries, keys_ctx, values_ctx):
+def attend(order, queries, keys_ctx, values_ctx):
     _, rows, n = queries.shape
     ctx = keys_ctx.shape[1]
     heads = n // HD
@@ -482,6 +516,7 @@
             tops_ref[0, h : h + 1, :] = top * SCALE
 
     return by_group(
+        order,
         kernel,
         "attend",
         [],
@@ -491,7 +526,7 @@
     )
 
 
-def attend_back(queries, keys_ctx, values_ctx, mixed, grad_mixed, log_sums, heads):
+def attend_back(order, queries, keys_ctx, values_ctx, mixed, grad_mixed, log_sums, heads):
     _, rows, n = queries.shape
     ctx = keys_ctx.shape[1]
     n_out = len(heads) * HD
@@ -511,6 +546,7 @@
             gq_ref[0, :, out] = (dot_n(k.T, grad_scores) * SCALE).T.astype(BF)
 
     return by_group(
+        order,
         kernel,
         "attend_back",
         [],
@@ -577,10 +613,21 @@
     value_bias_all = rest[:, None, cols : 2 * cols]
     up_bias_all = rest[:, None, 2 * cols :]
 
-    attn_w = gather_weight(
-        jnp.concatenate([query_weight, key_weight, value_weight, out_weight.T], axis=1)
-    )
-    bring_up = Exchange(gather_steps(up_weight))
+    order = Order()
+    up_cols = up_bias.shape[0]
+    attn_part = jnp.concatenate([query_weight, key_weight, value_weight, out_weight.T], axis=1)
+    if up_cols == 4 * cols and up_cols % 128 == 0:
+        joint_w = gather_weight(jnp.concatenate([attn_part, up_weight], axis=1))
+        attn_w, up_w = (joint_w, (up_cols, 0)), (joint_w, (up_cols, 1))
+    else:
+        attn_w = (gather_weight(attn_part), (4 * cols, 0))
+        up_w = (gather_weight(up_weight), (up_cols, 0))
+    out_start = 3 * cols // 128 * 128
+    out_width = 4 * cols - out_start
+    if out_width % 128 or out_start % out_width:
+        out_start, out_width = 0, 4 * cols
+    out_w = (attn_w[0], (out_width, out_start // out_width))
+    out_skip = 3 * cols - out_start
     down_w = gather_weight(down_weight.T)
     grad_mlp = gate_two * grad_out
     grad_mlp_low = grad_mlp.astype(BF)
@@ -589,36 +636,31 @@
     hidden_ctx = (normed_ctx * (1.0 + scale_one) + shift_one).astype(BF)
     normed_one, inverse_one, hidden_one = normed_ctx[:rows], inverse_ctx[:rows], hidden_ctx[:rows]
     residual = latents_in.astype(F32)
-    hidden_ctx, hidden_t, grad_mlp_t = lax.optimization_barrier(
-        (hidden_ctx, hidden_ctx.T, grad_mlp_low.T)
-    )
-    for _ in range(3):
-        hidden_ctx = tick(hidden_ctx, bring_up)
+    hidden_t, grad_mlp_t = transposed(order, hidden_ctx, grad_mlp_low)
     queries, keys_ctx, values_ctx = project_qkv(
-        hidden_ctx, rows, attn_w, query_bias_all, value_bias_all
-    )
-    queries = tick(queries, bring_up)
-    mixed, log_sums, head_tops = attend(queries, keys_ctx, values_ctx)
+        order, hidden_ctx, rows, attn_w, query_bias_all, value_bias_all
+    )
+    mixed, log_sums, head_tops = attend(order, queries, keys_ctx, values_ctx)
     head_tops = jnp.max(head_tops, axis=2)
-    mixed = tick(mixed, bring_up)
-    attn_out = project_back([mixed], attn_w, [3 * cols]) + out_bias_all
+    attn_out = project_back(order, [mixed], out_w, [out_skip]) + out_bias_all
     after_attn = residual + gate_one * attn_out
     normed_two, inverse_two = normalize(after_attn)
     hidden_two = (normed_two * (1.0 + scale_two) + shift_two).astype(BF)
-    up_w = bring_up.result()
-    activation, gelu_slope = project_up(hidden_two, up_w, up_bias_all)
-    sum_down = Exchange(scatter_steps([grad_mlp_t], [0], [activation]))
-    grad_up_low, up_sums = project_act_back(grad_mlp_low, down_w, gelu_slope)
-    grad_up_low = tick(grad_up_low, sum_down)
-    sum_up = Exchange(scatter_steps([hidden_two.T], [0], [grad_up_low]))
-    grad_hidden_two = project_back([grad_up_low], up_w, [0])
-    grad_hidden_two = tick(grad_hidden_two, sum_down, sum_up)
+    activation, gelu_slope = project_up(order, hidden_two, up_w, up_bias_all)
+    sum_down = Exchange(scatter_steps(order, [grad_mlp_t], [0], [activation]))
+    grad_up_low, up_sums = project_act_back(order, grad_mlp_low, down_w, gelu_slope)
+    order.tick(sum_down)
+    sum_up = Exchange(scatter_steps(order, [hidden_two.T], [0], [grad_up_low]))
+    grad_hidden_two = project_back(order, [grad_up_low], up_w, [0])
+    mlp_out = project_back(order, [activation], down_w, [0]) + down_bias_all
+    order.tick(sum_down, sum_up)
+    block_out = after_attn + gate_two * mlp_out
     grad_after = grad_out + normalize_back(
         grad_hidden_two * (1.0 + scale_two), normed_two, inverse_two
     )
     grad_attn = gate_one * grad_after
     grad_attn_low = grad_attn.astype(BF)
-    grad_mixed_low = project_mixed_back(grad_attn_low, attn_w)
+    grad_mixed_low = project_mixed_back(order, grad_attn_low, out_w, cols, out_skip)
     grad_attn_t = grad_attn_low.T
     tops_row = jnp.zeros((1, width), F32).at[0, : size_gy * heads_here].set(head_tops.reshape(-1))
     early = Exchange(
@@ -633,38 +675,45 @@
     half = (heads_here + 1) // 2
     head_sets = [x for x in (range(half), range(half, heads_here)) if len(x)]
     sum_attn, back_parts, grad_ctx = [], [], None
+    grad_low = None
     for i, heads in enumerate(head_sets):
-        parts = attend_back(queries, keys_ctx, values_ctx, mixed, grad_mixed_low, log_sums, heads)
-        parts = tick(parts, early, sum_down, sum_up, *sum_attn)
+        parts = attend_back(
+            order, queries, keys_ctx, values_ctx, mixed, grad_mixed_low, log_sums, heads
+        )
         back_parts.append(parts)
-        extra = i == 0
-        sum_attn.append(
-            Exchange(
-                scatter_steps(
-                    [hidden_t] + [grad_attn_t] * extra,
-                    [0, 0, 0] + [1] * extra,
-                    list(parts) + [mixed] * extra,
-                )
+        extra, last = i == 0, i + 1 == len(head_sets)
+        sum_new = Exchange(
+            scatter_steps(
+                order,
+                [hidden_t] + [grad_attn_t] * extra,
+                [0, 0, 0] + [1] * extra,
+                list(parts) + [mixed] * extra,
             )
         )
+        order.tick(early, sum_down, sum_up, *sum_attn)
+        sum_attn.append(sum_new)
         start = heads[0] * HD
         grad_ctx = project_back(
-            list(parts), attn_w, [start, cols + start, 2 * cols + start], grad_ctx
-        )
-        if i + 1 < len(head_sets):
-            grad_mixed_low, grad_ctx = tick(
-                (grad_mixed_low, grad_ctx), early, sum_down, sum_up, *sum_attn
-            )
-    grad_ctx, activation = tick((grad_ctx, activation), early, sum_down, sum_up, *sum_attn)
+            order,
+            list(parts),
+            attn_w,
+            [start, cols + start, 2 * cols + start],
+            grad_ctx,
+            rows if last and span > 1 else None,
+        )
+        if last and span > 1:
+            grad_low, grad_ctx = grad_ctx
+        order.tick(early, sum_down, sum_up, *sum_attn)
     grad_hidden_one = grad_ctx[:rows]
-    for s in range(1, span):
-        back = [(b, a) for a, b in shift_pairs(s)]
-        grad_hidden_one += lax.ppermute(
-            grad_ctx[s * rows : (s + 1) * rows].astype(BF), "gx", back
-        ).astype(F32)
-    mlp_out = project_back([activation], down_w, [0]) + down_bias_all
-    mlp_out, grad_hidden_one = tick((mlp_out, grad_hidden_one), early, sum_up, *sum_attn)
-    block_out = after_attn + gate_two * mlp_out
+    order.token, grad_low = lax.optimization_barrier((order.token, grad_low))
+    backs = [
+        lax.ppermute(
+            grad_low[(s - 1) * rows : s * rows], "gx", [(b, a) for a, b in shift_pairs(s)]
+        )
+        for s in range(1, span)
+    ]
+    for back in backs:
+        grad_hidden_one += back.astype(F32)
     grad_input = grad_after + normalize_back(
         grad_hidden_one * (1.0 + scale_one), normed_one, inverse_one
     )
@@ -687,6 +736,7 @@
         ],
         axis=0,
     )
+    late += order.token[:1, :1]
     for bit in bits_of("gx"):
         if bit < span:
             late = late + swap(late, "gx", bit)
@@ -713,7 +763,6 @@
     early_sum = early.result()
     grad_down_b = lax.dynamic_slice_in_dim(early_sum[0], at_gx * width_x, width_x, 0)
     grad_out_b = lax.dynamic_slice_in_dim(early_sum[1], at_gx * width_x, width_x, 0)
-    up_cols = up_bias.shape[0]
     grad_up_b = lax.dynamic_slice_in_dim(early_sum[2:-1].reshape(-1), at_gy * up_cols, up_cols, 0)
     logit_max = lax.dynamic_slice_in_dim(early_sum[-1], at_gy * heads_here, heads_here, 0)
 
@@ -725,7 +774,8 @@
         )
         for i in range(3)
     ]
-    grad_out_w = sums[0][:, 3 * HD * len(head_sets[0]) :]
+    out_at = 3 * HD * len(head_sets[0])
+    grad_out_w = sums[0][:, out_at : out_at + cols]
 
     factor = TAU / jnp.maximum(logit_max, TAU)
     root_cols = jnp.repeat(jnp.sqrt(factor), HD)

time: 664 us -> 613 us (0.923)
  starting transfers between devices: 82.5 us -> 49.3 us
  local copies, waits for them, and re-layouts: 50.7 us -> 28.4 us
  waiting for transfers between devices: 159 us -> 175 us
  other arithmetic: 111 us -> 98.6 us
    all_gather x2, waiting for transfers between devices: 0.01 us -> 90.5 us  [gather_weight(): full = lax.all_gather(own_half(shard), EVERY, axis=0, tiled=True)]
    ppermute x1, waiting for transfers between devices: 40.1 us -> 0.01 us  [body(): lax.ppermute(latents_in, 'gx', shift_pairs(s))]
    ppermute x57 -> x49, waiting for transfers between devices: 119 us -> 84.6 us  [swap(): return lax.ppermute(values, axis, pairs)]
    ppermute x57 -> x49, starting transfers between devices: 80.4 us -> 47.1 us  [swap(): return lax.ppermute(values, axis, pairs)]
    another operation x18 -> x2, other arithmetic: 15.2 us -> 1.29 us  [the longest x11 6.09 us: join_pair(): jnp.stack([jnp.where(low, values, other), jnp.where(low, other, values)])]
    optimization_barrier x3 -> x0, local copies, waits for them, and re-layouts: 10.9 us -> none  [the longest x2 6.67 us: body(): lax.optimization_barrier((hidden_ctx, hidden_ctx.T, grad_mlp_low.T))]
    pallas_call x20 -> x21, Pallas kernels: 227 us -> 232 us  [the longest x12 155 us: by_group(): pl.pallas_call(in_order, out_shape=[ORDER_SHAPE, *shapes], grid=(g,), in_...]
  transfers between devices with their start and end apart: 61 -> 53, of which waited for: 21 -> 13; matrix products, arithmetic and copies ran while one was open for 23% -> 20% of each run, Pallas kernels for 31% -> 31%
where the time goes in v3:
time: 613 us; the launch traced here: 608 us
  Pallas kernels  232 us (38%)
  waiting for transfers between devices  175 us (29%)
  other arithmetic  98.6 us (16%)
  starting transfers between devices  49.3 us (8%)
  local copies, waits for them, and re-layouts  28.4 us (5%)
  between operations  15.6 us (3%)
  matrix products  8.5 us (1%)
    pallas_call x12, Pallas kernels, by_group(): pl.pallas_call(in_order, out_shape=[ORDER_SHAPE, *shapes], grid=(g,), in_...  155 us
    all_gather x2, waiting for transfers between devices, gather_weight(): full = lax.all_gather(own_half(shard), EVERY, axis=0, tiled=True)  90.5 us
    ppermute x49, waiting for transfers between devices, swap(): return lax.ppermute(values, axis, pairs)  84.6 us
    pallas_call x8, Pallas kernels, weight_grads_near(): pl.pallas_call(kernel, out_shape=[ORDER_SHAPE, *shapes], grid_spec=pltpu....  72.3 us
    ppermute x49, starting transfers between devices, swap(): return lax.ppermute(values, axis, pairs)  47.1 us
    convert_element_type x24, other arithmetic, add_low(): return (left.astype(F32) + right.astype(F32)).astype(BF)  34.5 us
  transfers between devices with their start and end apart: 53, of which 13 were waited for; matrix products, arithmetic and copies ran while one was open for 20% of the time, Pallas kernels for 31%

profile of v3, /device:TPU:0, one launch (start us, length us, event | category | flops | bytes accessed | tf_op | source)
XLA Modules:
  0.0 607.5 jit_solution(1176871995694175220)
XLA Ops:
  12.8 3.1 collective-permute-start.5
  17.5 2.9 fusion.53
  23.2 2.7 collective-permute-start.6
  26.5 35.6 %collective-permute-done.6 = f32[2,576]{1,0:T(2,128)S(1)} collective-permute-done((f32[2,576]{1,0:T(2,128)S(1)}, f32[2,576]{1,0:T(2,128)S(1)}, u32[]{:S(2)}, u32[]{:S(2)}) %collective-permute-start.6) | collective-permute-done | bytes 4640 | tf_op jit(solution)/shard_map/ppermute | solution.py:47
  64.5 3.5 collective-permute-done.1
  68.3 2.8 multiply_convert_fusion.1.refs_1_.refs_0_
  72.3 4.1 fusion
  77.0 4.5 transposed.1
  81.5 83.3 %all-gather.3.cloned.1.call-done = bf16[4608,2304]{1,0:T(8,128)(2,1)} async-done(((bf16[144,2304]{1,0:T(8,128)(2,1)}), bf16[4608,2304]{1,0:T(8,128)(2,1)}) %all-gather.3.cloned.1.call-update) | async-done | bytes 21233680 | tf_op jit(solution)/shard_map/all_gather | solution.py:97
  164.8 16.4 %project_qkv.1 = (f32[8,128]{1,0:T(8,128)}, bf16[4,512,288]{2,1,0:T(8,128)(2,1)}, bf16[4,1024,288]{2,1,0:T(8,128)(2,1)}, bf16[4,1024,288]{2,1,0:T(8,128)(2,1)}) custom-call(f32[8,128]{1,0:T(8,128)} %get-tuple-element.152.order_ref, bf16[1024,1152]{1,0:T(8,128)(2,1)} %get-tuple-element.368.refs_0_, bf16[4,1152,2304]{2,1,0:T(8,128)(2,1)} %bitcast.158, ...), custom_call_target="tpu_custom_call" | custom-call | flops 8153726976 | bytes 29500416 | tf_op jit(solution)/shard_map/project_qkv/pallas_call | solution.py:219
  181.2 17.7 %attend.1 = (f32[8,128]{1,0:T(8,128)}, bf16[4,512,288]{2,1,0:T(8,128)(2,1)}, f32[4,4,512]{2,1,0:T(4,128)}, f32[4,4,512]{2,1,0:T(4,128)}) custom-call(f32[8,128]{1,0:T(8,128)} %get-tuple-element.153.order_ref, bf16[4,512,288]{2,1,0:T(8,128)(2,1)} %get-tuple-element.154.refs_0_, bf16[4,1024,288]{2,1,0:T(8,128)(2,1)} %get-tuple-element.155.refs_1_, ...), custom_call_target="tpu_custom_call" | custom-call | flops 8455716864 | bytes 7143424 | tf_op jit(solution)/shard_map/attend/pallas_call | solution.py:219
  198.9 7.0 %project_back.5 = (f32[8,128]{1,0:T(8,128)}, f32[512,1152]{1,0:T(8,128)}) custom-call(f32[8,128]{1,0:T(8,128)} %get-tuple-element.157.order_ref, bf16[4,512,288]{2,1,0:T(8,128)(2,1)} %get-tuple-element.158.refs_0_.refs_3_.refs_5_, bf16[4,1152,2304]{2,1,0:T(8,128)(2,1)} %bitcast.159), custom_call_target="tpu_custom_call" | custom-call | flops 1358954496 | bytes 24772608 | tf_op jit(solution)/shard_map/project_back/pallas_call | solution.py:219
  210.2 14.2 %project_up.1 = (f32[8,128]{1,0:T(8,128)}, bf16[4,512,1152]{2,1,0:T(8,128)(2,1)}, bf16[4,512,1152]{2,1,0:T(8,128)(2,1)}) custom-call(f32[8,128]{1,0:T(8,128)} %get-tuple-element.160.order_ref, bf16[512,1152]{1,0:T(8,128)(2,1)} %add_convert_fusion.1.refs_0_, bf16[4,1152,2304]{2,1,0:T(8,128)(2,1)} %bitcast.160, f32[4,1,1152]{2,1,0:T(1,128)} %broadcast_in_dim.38.refs_2_), custom_call_target="tpu_custom_call" | custom-call | flops 5435817984 | bytes 31868928 | tf_op jit(solution)/shard_map/project_up/pallas_call | solution.py:219
  224.4 7.9 %weight_grads_near.8 = (f32[8,128]{1,0:T(8,128)}, bf16[4,576,1152]{2,1,0:T(8,128)(2,1)}) custom-call(s32[2]{0:T(128)} %pad_add_fusion.place_ref, f32[8,128]{1,0:T(8,128)} %get-tuple-element.161.order_ref, bf16[4,2,144,512]{3,2,1,0:T(8,128)(2,1)} %bitcast.185, bf16[4,512,1152]{2,1,0:T(8,128)(2,1)} %get-tuple-element.163.refs_1_.refs_0_), custom_call_target="tpu_custom_call" | custom-call | flops 2717908992 | bytes 10027008 | tf_op jit(solution)/shard_map/weight_grads_near/pallas_call | solution.py:337
  234.4 7.8 %collective-permute-done.37 = bf16[8,288]{1,0:T(8,128)(2,1)S(1)} collective-permute-done((bf16[8,288]{1,0:T(8,128)(2,1)S(1)}, bf16[8,288]{1,0:T(8,128)(2,1)S(1)}, u32[]{:S(2)}, u32[]{:S(2)}) %collective-permute-start.37) | collective-permute-done | bytes 4640 | tf_op jit(solution)/shard_map/ppermute | solution.py:47
  246.2 7.1 %all-gather.5.cloned.1.call-done = bf16[4608,1152]{1,0:T(8,128)(2,1)} async-done(((bf16[144,1152]{1,0:T(8,128)(2,1)}), bf16[4608,1152]{1,0:T(8,128)(2,1)}) %all-gather.5.cloned.1.call-update) | async-done | bytes 10616848 | tf_op jit(solution)/shard_map/all_gather | solution.py:97
  253.3 12.5 %project_act_back.1 = (f32[8,128]{1,0:T(8,128)}, bf16[4,512,1152]{2,1,0:T(8,128)(2,1)}, f32[4,1,1152]{2,1,0:T(1,128)}) custom-call(f32[8,128]{1,0:T(8,128)} %get-tuple-element.164.order_ref, bf16[512,1152]{1,0:T(8,128)(2,1)} %multiply_convert_fusion.1.refs_1_.refs_0_, bf16[4,1152,1152]{2,1,0:T(8,128)(2,1)} %bitcast.189, ...), custom_call_target="tpu_custom_call" | custom-call | flops 5435817984 | bytes 21252096 | tf_op jit(solution)/shard_map/project_act_back/pallas_call | solution.py:219
  265.8 9.6 %weight_grads_near.9 = (f32[8,128]{1,0:T(8,128)}, bf16[2,288,1152]{2,1,0:T(8,128)(2,1)}, bf16[2,288,1152]{2,1,0:T(8,128)(2,1)}, bf16[2,288,1152]{2,1,0:T(8,128)(2,1)}, bf16[2,288,1152]{2,1,0:T(8,128)(2,1)}) custom-call(s32[2]{0:T(128)} %pad_add_fusion.1.place_ref, f32[8,128]{1,0:T(8,128)} %get-tuple-element.168.order_ref, ...), custom_call_target="tpu_custom_call" | custom-call | flops 2717908992 | bytes 15335424 | tf_op jit(solution)/shard_map/weight_grads_near/pallas_call | solution.py:337
  275.4 8.0 %weight_grads_near.10 = (f32[8,128]{1,0:T(8,128)}, bf16[4,576,1152]{2,1,0:T(8,128)(2,1)}) custom-call(s32[2]{0:T(128)} %pad_add_fusion.place_ref, f32[8,128]{1,0:T(8,128)} %get-tuple-element.170.order_ref, bf16[4,2,144,512]{3,2,1,0:T(8,128)(2,1)} %bitcast.171, bf16[4,512,1152]{2,1,0:T(8,128)(2,1)} %get-tuple-element.171.refs_1_.refs_0_), custom_call_target="tpu_custom_call" | custom-call | flops 2717908992 | bytes 10027008 | tf_op jit(solution)/shard_map/weight_grads_near/pallas_call | solution.py:337
  287.5 11.5 %project_back.6 = (f32[8,128]{1,0:T(8,128)}, f32[512,1152]{1,0:T(8,128)}) custom-call(f32[8,128]{1,0:T(8,128)} %get-tuple-element.172.order_ref, bf16[4,512,1152]{2,1,0:T(8,128)(2,1)} %get-tuple-element.171.refs_1_.refs_0_, bf16[4,1152,2304]{2,1,0:T(8,128)(2,1)} %bitcast.161), custom_call_target="tpu_custom_call" | custom-call | flops 5435817984 | bytes 28311552 | tf_op jit(solution)/shard_map/project_back/pallas_call | solution.py:219
  298.9 2.7 multiply_reduce_fusion.1
  301.6 12.0 %project_back.7 = (f32[8,128]{1,0:T(8,128)}, f32[512,1152]{1,0:T(8,128)}) custom-call(f32[8,128]{1,0:T(8,128)} %get-tuple-element.173.order_ref, bf16[4,512,1152]{2,1,0:T(8,128)(2,1)} %get-tuple-element.163.refs_1_.refs_0_, bf16[4,1152,1152]{2,1,0:T(8,128)(2,1)} %bitcast.190), custom_call_target="tpu_custom_call" | custom-call | flops 5435817984 | bytes 17694720 | tf_op jit(solution)/shard_map/project_back/pallas_call | solution.py:219
  313.6 5.9 multiply_reduce_fusion
  323.3 2.6 copy.71
  327.6 2.7 fusion.6
  331.7 2.7 fusion.7
  335.0 9.6 %weight_grads_near.11 = (f32[8,128]{1,0:T(8,128)}, bf16[2,288,1152]{2,1,0:T(8,128)(2,1)}, bf16[2,288,1152]{2,1,0:T(8,128)(2,1)}, bf16[2,288,1152]{2,1,0:T(8,128)(2,1)}, bf16[2,288,1152]{2,1,0:T(8,128)(2,1)}) custom-call(s32[2]{0:T(128)} %pad_add_fusion.1.place_ref, f32[8,128]{1,0:T(8,128)} %get-tuple-element.182.order_ref, ...), custom_call_target="tpu_custom_call" | custom-call | flops 2717908992 | bytes 15335424 | tf_op jit(solution)/shard_map/weight_grads_near/pallas_call | solution.py:337
  346.7 6.6 %project_mixed_back.1 = (f32[8,128]{1,0:T(8,128)}, bf16[4,512,288]{2,1,0:T(8,128)(2,1)}) custom-call(f32[8,128]{1,0:T(8,128)} %get-tuple-element.184.order_ref, bf16[512,1152]{1,0:T(8,128)(2,1)} %multiply_convert_fusion.refs_0_, bf16[4,1152,2304]{2,1,0:T(8,128)(2,1)} %bitcast.162), custom_call_target="tpu_custom_call" | custom-call | flops 1358954496 | bytes 23592960 | tf_op jit(solution)/shard_map/project_mixed_back/pallas_call | solution.py:219
  353.2 14.6 %attend_back.2 = (f32[8,128]{1,0:T(8,128)}, bf16[4,512,144]{2,1,0:T(8,128)(2,1)}, bf16[4,1024,144]{2,1,0:T(8,128)(2,1)}, bf16[4,1024,144]{2,1,0:T(8,128)(2,1)}) custom-call(f32[8,128]{1,0:T(8,128)} %get-tuple-element.185.order_ref, bf16[4,512,288]{2,1,0:T(8,128)(2,1)} %get-tuple-element.154.refs_0_, bf16[4,1024,288]{2,1,0:T(8,128)(2,1)} %get-tuple-element.155.refs_1_, ...), custom_call_target="tpu_custom_call" | custom-call | flops 10569646080 | bytes 11239424 | tf_op jit(solution)/shard_map/attend_back/pallas_call | solution.py:219
  367.9 9.6 %weight_grads_near.12 = (f32[8,128]{1,0:T(8,128)}, bf16[4,576,768]{2,1,0:T(8,128)(2,1)}) custom-call(s32[2]{0:T(128)} %pad_add_fusion.place_ref, f32[8,128]{1,0:T(8,128)} %get-tuple-element.188.order_ref, bf16[4,2,144,1024]{3,2,1,0:T(8,128)(2,1)} %bitcast.165, bf16[4,2,144,512]{3,2,1,0:T(8,128)(2,1)} %bitcast.169, ...), custom_call_target="tpu_custom_call" | custom-call | flops 2378170368 | bytes 7667712 | tf_op jit(solution)/shard_map/weight_grads_near/pallas_call | solution.py:337
  387.7 2.7 fusion.10
  391.9 2.7 fusion.11
  395.9 12.9 %project_back.8 = (f32[8,128]{1,0:T(8,128)}, f32[1024,1152]{1,0:T(8,128)}) custom-call(f32[8,128]{1,0:T(8,128)} %get-tuple-element.204.order_ref, bf16[4,512,144]{2,1,0:T(8,128)(2,1)} %get-tuple-element.190.refs_2_.refs_0_, bf16[4,1024,144]{2,1,0:T(8,128)(2,1)} %get-tuple-element.191.refs_3_.refs_1_, ...), custom_call_target="tpu_custom_call" | custom-call | flops 3397386240 | bytes 28901376 | tf_op jit(solution)/shard_map/project_back/pallas_call | solution.py:219
  408.9 2.7 collective-permute-done.19
  411.5 10.5 %weight_grads_near.13 = (f32[8,128]{1,0:T(8,128)}, bf16[2,288,768]{2,1,0:T(8,128)(2,1)}, bf16[2,288,768]{2,1,0:T(8,128)(2,1)}, bf16[2,288,768]{2,1,0:T(8,128)(2,1)}, bf16[2,288,768]{2,1,0:T(8,128)(2,1)}) custom-call(s32[2]{0:T(128)} %pad_add_fusion.1.place_ref, f32[8,128]{1,0:T(8,128)} %get-tuple-element.217.order_ref, bf16[4,2,144,1024]{3,2,1,0:T(8,128)(2,1)} %bitcast.166, ...), custom_call_target="tpu_custom_call" | custom-call | flops 2378170368 | bytes 11206656 | tf_op jit(solution)/shard_map/weight_grads_near/pallas_call | solution.py:337
  422.1 15.1 %attend_back.3 = (f32[8,128]{1,0:T(8,128)}, bf16[4,512,144]{2,1,0:T(8,128)(2,1)}, bf16[4,1024,144]{2,1,0:T(8,128)(2,1)}, bf16[4,1024,144]{2,1,0:T(8,128)(2,1)}) custom-call(f32[8,128]{1,0:T(8,128)} %get-tuple-element.219.order_ref, bf16[4,512,288]{2,1,0:T(8,128)(2,1)} %get-tuple-element.154.refs_0_, bf16[4,1024,288]{2,1,0:T(8,128)(2,1)} %get-tuple-element.155.refs_1_, ...), custom_call_target="tpu_custom_call" | custom-call | flops 10569646080 | bytes 11239424 | tf_op jit(solution)/shard_map/attend_back/pallas_call | solution.py:219
  448.3 8.1 %weight_grads_near.14 = (f32[8,128]{1,0:T(8,128)}, bf16[4,576,512]{2,1,0:T(8,128)(2,1)}) custom-call(s32[2]{0:T(128)} %pad_add_fusion.place_ref, f32[8,128]{1,0:T(8,128)} %get-tuple-element.220.order_ref, bf16[4,2,144,1024]{3,2,1,0:T(8,128)(2,1)} %bitcast.167, bf16[4,512,144]{2,1,0:T(8,128)(2,1)} %get-tuple-element.221.refs_1_, ...), custom_call_target="tpu_custom_call" | custom-call | flops 1698693120 | bytes 5308416 | tf_op jit(solution)/shard_map/weight_grads_near/pallas_call | solution.py:337
  458.5 5.9 collective-permute-done.22
  478.8 14.9 %project_back.9 = (f32[8,128]{1,0:T(8,128)}, bf16[512,1152]{1,0:T(8,128)(2,1)}, f32[1024,1152]{1,0:T(8,128)}) custom-call(f32[8,128]{1,0:T(8,128)} %get-tuple-element.237.order_ref, f32[1024,1152]{1,0:T(8,128)} %get-tuple-element.238.refs_0_, bf16[4,512,144]{2,1,0:T(8,128)(2,1)} %get-tuple-element.221.refs_1_, ...), custom_call_target="tpu_custom_call" | custom-call | flops 3397386240 | bytes 34799616 | tf_op jit(solution)/shard_map/project_back/pallas_call | solution.py:219
  500.4 8.9 %weight_grads_near.15 = (f32[8,128]{1,0:T(8,128)}, bf16[2,288,512]{2,1,0:T(8,128)(2,1)}, bf16[2,288,512]{2,1,0:T(8,128)(2,1)}, bf16[2,288,512]{2,1,0:T(8,128)(2,1)}, bf16[2,288,512]{2,1,0:T(8,128)(2,1)}) custom-call(s32[2]{0:T(128)} %pad_add_fusion.1.place_ref, f32[8,128]{1,0:T(8,128)} %get-tuple-element.252.order_ref, bf16[4,2,144,1024]{3,2,1,0:T(8,128)(2,1)} %bitcast.168, ...), custom_call_target="tpu_custom_call" | custom-call | flops 1698693120 | bytes 7667712 | tf_op jit(solution)/shard_map/weight_grads_near/pallas_call | solution.py:337
  530.8 16.5 %collective-permute-done.40 = bf16[144,768]{1,0:T(8,128)(2,1)S(1)} collective-permute-done((bf16[144,768]{1,0:T(8,128)(2,1)S(1)}, bf16[144,768]{1,0:T(8,128)(2,1)S(1)}, u32[]{:S(2)}, u32[]{:S(2)}) %collective-permute-start.40) | collective-permute-done | bytes 221216 | tf_op jit(solution)/shard_map/ppermute | solution.py:47
  553.3 5.6 collective-permute-done.45
  560.9 2.9 collective-permute-start.46
  563.8 3.6 multiply_reduce_fusion.3
  568.4 5.0 multiply_add_fusion
  574.1 2.6 collective-permute-start.34
  584.0 3.6 collective-permute-done.47
  595.9 4.5 fusion.41
  (391 shorter events, 132.1 us)
Async XLA Ops:
  7.2 157.6 %all-gather.3.cloned.1.call-start = ((), (), s32[]{:S(2)}) async-start(), calls=%async_computation | async-start | bytes 21897216 | tf_op jit(solution)/shard_map/all_gather | solution.py:97
  11.9 241.4 %all-gather.5.cloned.1.call-start = ((), (), s32[]{:S(2)}) async-start(), calls=%async_computation.1 | async-start | bytes 10948608 | tf_op jit(solution)/shard_map/all_gather | solution.py:97
  12.8 10.3 %collective-permute-start.5 = (f32[1,576]{1,0:T(1,128)S(1)}, f32[1,576]{1,0:T(1,128)S(1)}, u32[]{:S(2)}, u32[]{:S(2)}) collective-permute-start(f32[1,576]{1,0:T(1,128)S(1)} %broadcast_in_dim.37), channel_id=1, source_target_pairs={{0,4},{4,0},{8,12},{12,8},{1,5},{5,1},{9,13},{13,9},{2,6},{6,2},{1... | collective-permute-start | bytes 6920 | tf_op jit(solution)/shard_map/ppermute | solution.py:47
  16.0 9.9 %collective-permute-start.3 = (f32[1,1728]{1,0:T(1,128)S(1)}, f32[1,1728]{1,0:T(1,128)S(1)}, u32[]{:S(2)}, u32[]{:S(2)}) collective-permute-start(f32[1,1728]{1,0:T(1,128)S(1)} %broadcast_in_dim.34), channel_id=1, source_target_pairs={{0,1},{1,0},{2,3},{3,2},{4,5},{5,4},{6,7},{7,6},{8,9},{9,8},{10,11... | collective-permute-start | bytes 20744 | tf_op jit(solution)/shard_map/ppermute | solution.py:47
  20.6 41.8 %collective-permute-start = (f32[4,6,1152]{2,0,1:T(4,128)S(1)}, f32[4,6,1152]{2,0,1:T(4,128)S(1)}, u32[]{:S(2)}, u32[]{:S(2)}) collective-permute-start(f32[4,6,1152]{2,0,1:T(4,128)S(1)} %dynamic-slice_bitcast_fusion.7), channel_id=1, source_target_pairs={{0,2},{1,3},{2,0},{3,1},{4,6},{5,7},{6,4},{7,5},{8,10},{9,11},{10,... | collective-permute-start | bytes 331784 | tf_op jit(solution)/shard_map/ppermute | solution.py:47
  22.1 49.0 %collective-permute-start.2 = (bf16[512,1152]{1,0:T(8,128)(2,1)S(1)}, bf16[512,1152]{1,0:T(8,128)(2,1)S(1)}, u32[]{:S(2)}, u32[]{:S(2)}) collective-permute-start(bf16[512,1152]{1,0:T(8,128)(2,1)S(1)} %copy-done.4), channel_id=1, source_target_pairs={{0,4},{4,0},{8,12},{12,8},{1,5},{5,1},{9,13},{13,9},{2,6},{6,2},{1... | collective-permute-start | bytes 3538952 | tf_op jit(solution)/shard_map/ppermute | solution.py:593
  23.2 38.9 %collective-permute-start.6 = (f32[2,576]{1,0:T(2,128)S(1)}, f32[2,576]{1,0:T(2,128)S(1)}, u32[]{:S(2)}, u32[]{:S(2)}) collective-permute-start(f32[2,576]{1,0:T(2,128)S(1)} %pad_maximum_fusion.21), channel_id=1, source_target_pairs={{0,8},{4,12},{8,0},{12,4},{1,9},{5,13},{9,1},{13,5},{2,10},{6,14},... | collective-permute-start | bytes 13832 | tf_op jit(solution)/shard_map/ppermute | solution.py:47
  25.9 36.4 %collective-permute-start.4 = (f32[2,1728]{1,0:T(2,128)S(1)}, f32[2,1728]{1,0:T(2,128)S(1)}, u32[]{:S(2)}, u32[]{:S(2)}) collective-permute-start(f32[2,1728]{1,0:T(2,128)S(1)} %pad_maximum_fusion.8), channel_id=1, source_target_pairs={{0,2},{1,3},{2,0},{3,1},{4,6},{5,7},{6,4},{7,5},{8,10},{9,11},{10,... | collective-permute-start | bytes 41480 | tf_op jit(solution)/shard_map/ppermute | solution.py:47
  62.6 5.5 collective-permute-start.1
  232.3 33.5 %collective-permute-start.7 = (bf16[4,576,1152]{2,1,0:T(8,128)(2,1)}, bf16[4,576,1152]{2,1,0:T(8,128)(2,1)}, u32[]{:S(2)}, u32[]{:S(2)}) collective-permute-start(bf16[4,576,1152]{2,1,0:T(8,128)(2,1)} %get-tuple-element.167), channel_id=1, source_target_pairs={{0,16},{16,0},{1,17},{17,1},{2,18},{18,2},{3,19},{19,3},{4,20},{20... | collective-permute-start | bytes 15925256 | tf_op jit(solution)/shard_map/ppermute | solution.py:47
  232.5 9.7 %collective-permute-start.37 = (bf16[8,288]{1,0:T(8,128)(2,1)S(1)}, bf16[8,288]{1,0:T(8,128)(2,1)S(1)}, u32[]{:S(2)}, u32[]{:S(2)}) collective-permute-start(bf16[8,288]{1,0:T(8,128)(2,1)S(1)} %fusion.47), channel_id=1, source_target_pairs={{0,16},{16,0},{1,17},{17,1},{2,18},{18,2},{3,19},{19,3},{4,20},{20... | collective-permute-start | bytes 13832 | tf_op jit(solution)/shard_map/ppermute | solution.py:47
  283.4 43.6 %collective-permute-start.10 = (bf16[4,576,1152]{2,1,0:T(8,128)(2,1)}, bf16[4,576,1152]{2,1,0:T(8,128)(2,1)}, u32[]{:S(2)}, u32[]{:S(2)}) collective-permute-start(bf16[4,576,1152]{2,1,0:T(8,128)(2,1)} %get-tuple-element.181), channel_id=1, source_target_pairs={{0,16},{16,0},{1,17},{17,1},{2,18},{18,2},{3,19},{19,3},{4,20},{20... | collective-permute-start | bytes 15925256 | tf_op jit(solution)/shard_map/ppermute | solution.py:47
  285.4 41.7 %collective-permute-start.8 = (bf16[2,288,1152]{2,1,0:T(8,128)(2,1)}, bf16[2,288,1152]{2,1,0:T(8,128)(2,1)}, u32[]{:S(2)}, u32[]{:S(2)}) collective-permute-start(bf16[2,288,1152]{2,1,0:T(8,128)(2,1)} %get-tuple-element.179), channel_id=1, source_target_pairs={{0,1},{1,0},{2,3},{3,2},{4,5},{5,4},{6,7},{7,6},{8,9},{9,8},{10,11... | collective-permute-start | bytes 3981320 | tf_op jit(solution)/shard_map/ppermute | solution.py:47
  286.9 40.2 %collective-permute-start.9 = (bf16[2,288,1152]{2,1,0:T(8,128)(2,1)}, bf16[2,288,1152]{2,1,0:T(8,128)(2,1)}, u32[]{:S(2)}, u32[]{:S(2)}) collective-permute-start(bf16[2,288,1152]{2,1,0:T(8,128)(2,1)} %get-tuple-element.180), channel_id=1, source_target_pairs={{0,2},{1,3},{2,0},{3,1},{4,6},{5,7},{6,4},{7,5},{8,10},{9,11},{10,... | collective-permute-start | bytes 3981320 | tf_op jit(solution)/shard_map/ppermute | solution.py:47
  322.1 55.4 %collective-permute-start.11 = (f32[7,1152]{1,0:T(8,128)S(1)}, f32[7,1152]{1,0:T(8,128)S(1)}, u32[]{:S(2)}, u32[]{:S(2)}) collective-permute-start(f32[7,1152]{1,0:T(8,128)S(1)} %select_maximum_fusion), channel_id=1, source_target_pairs={{0,16},{16,0},{1,17},{17,1},{2,18},{18,2},{3,19},{19,3},{4,20},{20... | collective-permute-start | bytes 96776 | tf_op jit(solution)/shard_map/ppermute | solution.py:47
  330.3 51.3 %collective-permute-start.12 = (bf16[288,1152]{1,0:T(8,128)(2,1)}, bf16[288,1152]{1,0:T(8,128)(2,1)S(1)}, u32[]{:S(2)}, u32[]{:S(2)}) collective-permute-start(bf16[288,1152]{1,0:T(8,128)(2,1)} %get-tuple-element.361), channel_id=1, source_target_pairs={{0,2},{1,3},{2,0},{3,1},{4,6},{5,7},{6,4},{7,5},{8,10},{9,11},{10,... | collective-permute-start | bytes 1990664 | tf_op jit(solution)/shard_map/ppermute | solution.py:47
  334.4 47.2 %collective-permute-start.13 = (bf16[288,1152]{1,0:T(8,128)(2,1)}, bf16[288,1152]{1,0:T(8,128)(2,1)}, u32[]{:S(2)}, u32[]{:S(2)}) collective-permute-start(bf16[288,1152]{1,0:T(8,128)(2,1)} %get-tuple-element.359), channel_id=1, source_target_pairs={{0,1},{1,0},{2,3},{3,2},{4,5},{5,4},{6,7},{7,6},{8,9},{9,8},{10,11... | collective-permute-start | bytes 1990664 | tf_op jit(solution)/shard_map/ppermute | solution.py:47
  344.6 37.0 %collective-permute-start.14 = (bf16[2,288,1152]{2,1,0:T(8,128)(2,1)}, bf16[2,288,1152]{2,1,0:T(8,128)(2,1)}, u32[]{:S(2)}, u32[]{:S(2)}) collective-permute-start(bf16[2,288,1152]{2,1,0:T(8,128)(2,1)} %get-tuple-element.202), channel_id=1, source_target_pairs={{0,1},{1,0},{2,3},{3,2},{4,5},{5,4},{6,7},{7,6},{8,9},{9,8},{10,11... | collective-permute-start | bytes 3981320 | tf_op jit(solution)/shard_map/ppermute | solution.py:47
  346.1 35.6 %collective-permute-start.15 = (bf16[2,288,1152]{2,1,0:T(8,128)(2,1)}, bf16[2,288,1152]{2,1,0:T(8,128)(2,1)}, u32[]{:S(2)}, u32[]{:S(2)}) collective-permute-start(bf16[2,288,1152]{2,1,0:T(8,128)(2,1)} %get-tuple-element.203), channel_id=1, source_target_pairs={{0,2},{1,3},{2,0},{3,1},{4,6},{5,7},{6,4},{7,5},{8,10},{9,11},{10,... | collective-permute-start | bytes 3981320 | tf_op jit(solution)/shard_map/ppermute | solution.py:47
  377.5 34.0 %collective-permute-start.20 = (bf16[4,576,768]{2,1,0:T(8,128)(2,1)}, bf16[4,576,768]{2,1,0:T(8,128)(2,1)}, u32[]{:S(2)}, u32[]{:S(2)}) collective-permute-start(bf16[4,576,768]{2,1,0:T(8,128)(2,1)} %get-tuple-element.216), channel_id=1, source_target_pairs={{0,16},{16,0},{1,17},{17,1},{2,18},{18,2},{3,19},{19,3},{4,20},{20... | collective-permute-start | bytes 10616840 | tf_op jit(solution)/shard_map/ppermute | solution.py:47
  386.4 22.5 %collective-permute-start.17 = (bf16[2,144,1152]{2,1,0:T(8,128)(2,1)}, bf16[2,144,1152]{2,1,0:T(8,128)(2,1)S(1)}, u32[]{:S(2)}, u32[]{:S(2)}) collective-permute-start(bf16[2,144,1152]{2,1,0:T(8,128)(2,1)} %get-tuple-element.375), channel_id=1, source_target_pairs={{0,4},{4,0},{8,12},{12,8},{1,5},{5,1},{9,13},{13,9},{2,6},{6,2},{1... | collective-permute-start | bytes 1990664 | tf_op jit(solution)/shard_map/ppermute | solution.py:47
  390.4 18.4 %collective-permute-start.18 = (bf16[288,1152]{1,0:T(8,128)(2,1)}, bf16[288,1152]{1,0:T(8,128)(2,1)}, u32[]{:S(2)}, u32[]{:S(2)}) collective-permute-start(bf16[288,1152]{1,0:T(8,128)(2,1)} %get-tuple-element.357), channel_id=1, source_target_pairs={{0,2},{1,3},{2,0},{3,1},{4,6},{5,7},{6,4},{7,5},{8,10},{9,11},{10,... | collective-permute-start | bytes 1990664 | tf_op jit(solution)/shard_map/ppermute | solution.py:47
  394.6 17.0 %collective-permute-start.19 = (bf16[288,1152]{1,0:T(8,128)(2,1)}, bf16[288,1152]{1,0:T(8,128)(2,1)}, u32[]{:S(2)}, u32[]{:S(2)}) collective-permute-start(bf16[288,1152]{1,0:T(8,128)(2,1)} %get-tuple-element.355), channel_id=1, source_target_pairs={{0,1},{1,0},{2,3},{3,2},{4,5},{5,4},{6,7},{7,6},{8,9},{9,8},{10,11... | collective-permute-start | bytes 1990664 | tf_op jit(solution)/shard_map/ppermute | solution.py:47
  395.2 13.6 %collective-permute-start.16 = (f32[7,1152]{1,0:T(8,128)S(1)}, f32[7,1152]{1,0:T(8,128)S(1)}, u32[]{:S(2)}, u32[]{:S(2)}) collective-permute-start(f32[7,1152]{1,0:T(8,128)S(1)} %maximum_select_fusion.4), channel_id=1, source_target_pairs={{0,4},{4,0},{8,12},{12,8},{1,5},{5,1},{9,13},{13,9},{2,6},{6,2},{1... | collective-permute-start | bytes 96776 | tf_op jit(solution)/shard_map/ppermute | solution.py:47
  437.3 21.2 %collective-permute-start.21 = (f32[7,1152]{1,0:T(8,128)S(1)}, f32[7,1152]{1,0:T(8,128)S(1)}, u32[]{:S(2)}, u32[]{:S(2)}) collective-permute-start(f32[7,1152]{1,0:T(8,128)S(1)} %maximum_select_fusion.3), channel_id=1, source_target_pairs={{0,8},{4,12},{8,0},{12,4},{1,9},{5,13},{9,1},{13,5},{2,10},{6,14},... | collective-permute-start | bytes 96776 | tf_op jit(solution)/shard_map/ppermute | solution.py:47
  442.6 23.0 %collective-permute-start.23 = (bf16[2,144,1152]{2,1,0:T(8,128)(2,1)}, bf16[2,144,1152]{2,1,0:T(8,128)(2,1)}, u32[]{:S(2)}, u32[]{:S(2)}) collective-permute-start(bf16[2,144,1152]{2,1,0:T(8,128)(2,1)} %get-tuple-element.373), channel_id=1, source_target_pairs={{0,4},{4,0},{8,12},{12,8},{1,5},{5,1},{9,13},{13,9},{2,6},{6,2},{1... | collective-permute-start | bytes 1990664 | tf_op jit(solution)/shard_map/ppermute | solution.py:47
  444.0 21.6 %collective-permute-start.24 = (bf16[2,288,768]{2,1,0:T(8,128)(2,1)}, bf16[2,288,768]{2,1,0:T(8,128)(2,1)}, u32[]{:S(2)}, u32[]{:S(2)}) collective-permute-start(bf16[2,288,768]{2,1,0:T(8,128)(2,1)} %get-tuple-element.235), channel_id=1, source_target_pairs={{0,1},{1,0},{2,3},{3,2},{4,5},{5,4},{6,7},{7,6},{8,9},{9,8},{10,11... | collective-permute-start | bytes 2654216 | tf_op jit(solution)/shard_map/ppermute | solution.py:47
  444.5 21.0 %collective-permute-start.25 = (bf16[2,288,768]{2,1,0:T(8,128)(2,1)}, bf16[2,288,768]{2,1,0:T(8,128)(2,1)}, u32[]{:S(2)}, u32[]{:S(2)}) collective-permute-start(bf16[2,288,768]{2,1,0:T(8,128)(2,1)} %get-tuple-element.236), channel_id=1, source_target_pairs={{0,2},{1,3},{2,0},{3,1},{4,6},{5,7},{6,4},{7,5},{8,10},{9,11},{10,... | collective-permute-start | bytes 2654216 | tf_op jit(solution)/shard_map/ppermute | solution.py:47
  447.0 17.4 %collective-permute-start.22 = (bf16[144,1152]{1,0:T(8,128)(2,1)}, bf16[144,1152]{1,0:T(8,128)(2,1)S(1)}, u32[]{:S(2)}, u32[]{:S(2)}) collective-permute-start(bf16[144,1152]{1,0:T(8,128)(2,1)} %get-tuple-element.386), channel_id=1, source_target_pairs={{0,8},{4,12},{8,0},{12,4},{1,9},{5,13},{9,1},{13,5},{2,10},{6,14},... | collective-permute-start | bytes 995336 | tf_op jit(solution)/shard_map/ppermute | solution.py:47
  458.5 35.3 %collective-permute-start.31 = (bf16[4,576,512]{2,1,0:T(8,128)(2,1)}, bf16[4,576,512]{2,1,0:T(8,128)(2,1)}, u32[]{:S(2)}, u32[]{:S(2)}) collective-permute-start(bf16[4,576,512]{2,1,0:T(8,128)(2,1)} %get-tuple-element.251), channel_id=1, source_target_pairs={{0,16},{16,0},{1,17},{17,1},{2,18},{18,2},{3,19},{19,3},{4,20},{20... | collective-permute-start | bytes 7077896 | tf_op jit(solution)/shard_map/ppermute | solution.py:47
  465.6 10.1 %collective-permute-start.26 = (f32[7,1152]{1,0:T(8,128)S(1)}, f32[7,1152]{1,0:T(8,128)S(1)}, u32[]{:S(2)}, u32[]{:S(2)}) collective-permute-start(f32[7,1152]{1,0:T(8,128)S(1)} %maximum_select_fusion.2), channel_id=1, source_target_pairs={{0,1},{1,0},{2,3},{3,2},{4,5},{5,4},{6,7},{7,6},{8,9},{9,8},{10,11... | collective-permute-start | bytes 96776 | tf_op jit(solution)/shard_map/ppermute | solution.py:47
  467.0 26.7 %collective-permute-start.27 = (bf16[144,1152]{1,0:T(8,128)(2,1)}, bf16[144,1152]{1,0:T(8,128)(2,1)}, u32[]{:S(2)}, u32[]{:S(2)}) collective-permute-start(bf16[144,1152]{1,0:T(8,128)(2,1)} %add_convert_fusion.23), channel_id=1, source_target_pairs={{0,16},{16,0},{1,17},{17,1},{2,18},{18,2},{3,19},{19,3},{4,20},{20... | collective-permute-start | bytes 995336 | tf_op jit(solution)/shard_map/ppermute | solution.py:47
  469.3 24.5 %collective-permute-start.29 = (bf16[288,768]{1,0:T(8,128)(2,1)}, bf16[288,768]{1,0:T(8,128)(2,1)}, u32[]{:S(2)}, u32[]{:S(2)}) collective-permute-start(bf16[288,768]{1,0:T(8,128)(2,1)} %get-tuple-element.371), channel_id=1, source_target_pairs={{0,2},{1,3},{2,0},{3,1},{4,6},{5,7},{6,4},{7,5},{8,10},{9,11},{10,... | collective-permute-start | bytes 1327112 | tf_op jit(solution)/shard_map/ppermute | solution.py:47
  473.0 20.7 %collective-permute-start.30 = (bf16[288,768]{1,0:T(8,128)(2,1)}, bf16[288,768]{1,0:T(8,128)(2,1)}, u32[]{:S(2)}, u32[]{:S(2)}) collective-permute-start(bf16[288,768]{1,0:T(8,128)(2,1)} %get-tuple-element.369), channel_id=1, source_target_pairs={{0,1},{1,0},{2,3},{3,2},{4,5},{5,4},{6,7},{7,6},{8,9},{9,8},{10,11... | collective-permute-start | bytes 1327112 | tf_op jit(solution)/shard_map/ppermute | solution.py:47
  475.7 18.0 %collective-permute-start.28 = (bf16[144,1152]{1,0:T(8,128)(2,1)}, bf16[144,1152]{1,0:T(8,128)(2,1)S(1)}, u32[]{:S(2)}, u32[]{:S(2)}) collective-permute-start(bf16[144,1152]{1,0:T(8,128)(2,1)} %get-tuple-element.384), channel_id=1, source_target_pairs={{0,8},{4,12},{8,0},{12,4},{1,9},{5,13},{9,1},{13,5},{2,10},{6,14},... | collective-permute-start | bytes 995336 | tf_op jit(solution)/shard_map/ppermute | solution.py:47
  494.7 20.3 %collective-permute-start.49 = (f32[7,1152]{1,0:T(8,128)S(1)}, f32[7,1152]{1,0:T(8,128)S(1)}, u32[]{:S(2)}, u32[]{:S(2)}) collective-permute-start(f32[7,1152]{1,0:T(8,128)S(1)} %maximum_select_fusion.1), channel_id=1, source_target_pairs={{0,2},{1,3},{2,0},{3,1},{4,6},{5,7},{6,4},{7,5},{8,10},{9,11},{10,... | collective-permute-start | bytes 96776 | tf_op jit(solution)/shard_map/ppermute | solution.py:47
  496.9 27.1 %collective-permute-start.50 = (bf16[144,1152]{1,0:T(8,128)(2,1)}, bf16[144,1152]{1,0:T(8,128)(2,1)}, u32[]{:S(2)}, u32[]{:S(2)}) collective-permute-start(bf16[144,1152]{1,0:T(8,128)(2,1)} %add_convert_fusion.22), channel_id=1, source_target_pairs={{0,16},{16,0},{1,17},{17,1},{2,18},{18,2},{3,19},{19,3},{4,20},{20... | collective-permute-start | bytes 995336 | tf_op jit(solution)/shard_map/ppermute | solution.py:47
  500.1 26.3 %collective-permute-start.39 = (bf16[2,144,768]{2,1,0:T(8,128)(2,1)}, bf16[2,144,768]{2,1,0:T(8,128)(2,1)}, u32[]{:S(2)}, u32[]{:S(2)}) collective-permute-start(bf16[2,144,768]{2,1,0:T(8,128)(2,1)} %fusion.28), channel_id=1, source_target_pairs={{0,4},{4,0},{8,12},{12,8},{1,5},{5,1},{9,13},{13,9},{2,6},{6,2},{1... | collective-permute-start | bytes 1327112 | tf_op jit(solution)/shard_map/ppermute | solution.py:47
  509.3 19.1 %collective-permute-start.42 = (bf16[2,288,512]{2,1,0:T(8,128)(2,1)}, bf16[2,288,512]{2,1,0:T(8,128)(2,1)}, u32[]{:S(2)}, u32[]{:S(2)}) collective-permute-start(bf16[2,288,512]{2,1,0:T(8,128)(2,1)} %get-tuple-element.263), channel_id=1, source_target_pairs={{0,1},{1,0},{2,3},{3,2},{4,5},{5,4},{6,7},{7,6},{8,9},{9,8},{10,11... | collective-permute-start | bytes 1769480 | tf_op jit(solution)/shard_map/ppermute | solution.py:47
  510.0 37.4 %collective-permute-start.44 = (bf16[2,288,512]{2,1,0:T(8,128)(2,1)}, bf16[2,288,512]{2,1,0:T(8,128)(2,1)}, u32[]{:S(2)}, u32[]{:S(2)}) collective-permute-start(bf16[2,288,512]{2,1,0:T(8,128)(2,1)} %get-tuple-element.265), channel_id=1, source_target_pairs={{0,2},{1,3},{2,0},{3,1},{4,6},{5,7},{6,4},{7,5},{8,10},{9,11},{10,... | collective-permute-start | bytes 1769480 | tf_op jit(solution)/shard_map/ppermute | solution.py:47
  515.6 48.2 %collective-permute-start.32 = (bf16[512,1152]{1,0:T(8,128)(2,1)}, bf16[512,1152]{1,0:T(8,128)(2,1)}, u32[]{:S(2)}, u32[]{:S(2)}) collective-permute-start(bf16[512,1152]{1,0:T(8,128)(2,1)} %get-tuple-element.256), channel_id=1, source_target_pairs={{4,0},{0,4},{12,8},{8,12},{5,1},{1,5},{13,9},{9,13},{6,2},{2,6},{1... | collective-permute-start | bytes 3538952 | tf_op jit(solution)/shard_map/ppermute | solution.py:710
  527.6 19.7 %collective-permute-start.40 = (bf16[144,768]{1,0:T(8,128)(2,1)S(1)}, bf16[144,768]{1,0:T(8,128)(2,1)S(1)}, u32[]{:S(2)}, u32[]{:S(2)}) collective-permute-start(bf16[144,768]{1,0:T(8,128)(2,1)S(1)} %dynamic-slice_bitcast_fusion.5), channel_id=1, source_target_pairs={{0,8},{4,12},{8,0},{12,4},{1,9},{5,13},{9,1},{13,5},{2,10},{6,14},... | collective-permute-start | bytes 663560 | tf_op jit(solution)/shard_map/ppermute | solution.py:47
  530.2 21.8 %collective-permute-start.43 = (bf16[288,512]{1,0:T(8,128)(2,1)}, bf16[288,512]{1,0:T(8,128)(2,1)}, u32[]{:S(2)}, u32[]{:S(2)}) collective-permute-start(bf16[288,512]{1,0:T(8,128)(2,1)} %fusion.33), channel_id=1, source_target_pairs={{0,2},{1,3},{2,0},{3,1},{4,6},{5,7},{6,4},{7,5},{8,10},{9,11},{10,... | collective-permute-start | bytes 884744 | tf_op jit(solution)/shard_map/ppermute | solution.py:47
  549.2 9.7 %collective-permute-start.45 = (bf16[288,512]{1,0:T(8,128)(2,1)}, bf16[288,512]{1,0:T(8,128)(2,1)}, u32[]{:S(2)}, u32[]{:S(2)}) collective-permute-start(bf16[288,512]{1,0:T(8,128)(2,1)} %fusion.35), channel_id=1, source_target_pairs={{0,1},{1,0},{2,3},{3,2},{4,5},{5,4},{6,7},{7,6},{8,9},{9,8},{10,11... | collective-permute-start | bytes 884744 | tf_op jit(solution)/shard_map/ppermute | solution.py:47
  560.9 15.8 %collective-permute-start.46 = (bf16[2,144,512]{2,1,0:T(8,128)(2,1)}, bf16[2,144,512]{2,1,0:T(8,128)(2,1)}, u32[]{:S(2)}, u32[]{:S(2)}) collective-permute-start(bf16[2,144,512]{2,1,0:T(8,128)(2,1)} %fusion.37), channel_id=1, source_target_pairs={{0,4},{4,0},{8,12},{12,8},{1,5},{5,1},{9,13},{13,9},{2,6},{6,2},{1... | collective-permute-start | bytes 884744 | tf_op jit(solution)/shard_map/ppermute | solution.py:47
  568.3 5.1 collective-permute-start.33
  574.1 4.9 collective-permute-start.34
  579.7 7.8 %collective-permute-start.47 = (bf16[144,512]{1,0:T(8,128)(2,1)S(1)}, bf16[144,512]{1,0:T(8,128)(2,1)S(1)}, u32[]{:S(2)}, u32[]{:S(2)}) collective-permute-start(bf16[144,512]{1,0:T(8,128)(2,1)S(1)} %dynamic-slice_bitcast_fusion.6), channel_id=1, source_target_pairs={{0,8},{4,12},{8,0},{12,4},{1,9},{5,13},{9,1},{13,5},{2,10},{6,14},... | collective-permute-start | bytes 442376 | tf_op jit(solution)/shard_map/ppermute | solution.py:47
  (58 other events, 852.5 us)
Sparse Core Ops, SparseCore 0:
  12.0 152.7 all-gather.2
  168.4 84.8 all-gather.4

commit v4 on v3

--- a/solution.py
+++ b/solution.py
@@ -648,8 +648,8 @@
     hidden_two = (normed_two * (1.0 + scale_two) + shift_two).astype(BF)
     activation, gelu_slope = project_up(order, hidden_two, up_w, up_bias_all)
     sum_down = Exchange(scatter_steps(order, [grad_mlp_t], [0], [activation]))
+    order.tick(sum_down)
     grad_up_low, up_sums = project_act_back(order, grad_mlp_low, down_w, gelu_slope)
-    order.tick(sum_down)
     sum_up = Exchange(scatter_steps(order, [hidden_two.T], [0], [grad_up_low]))
     grad_hidden_two = project_back(order, [grad_up_low], up_w, [0])
     mlp_out = project_back(order, [activation], down_w, [0]) + down_bias_all

time: 613 us -> 606 us (0.989)
  waiting for transfers between devices: 175 us -> 167 us
    all_gather x2, waiting for transfers between devices: 90.5 us -> 83.3 us  [gather_weight(): full = lax.all_gather(own_half(shard), EVERY, axis=0, tiled=True)]
  transfers between devices with their start and end apart: 53 -> 53, of which waited for: 13 -> 12; matrix products, arithmetic and copies ran while one was open for 20% -> 20% of each run, Pallas kernels for 31% -> 31%
where the time goes in v4:
time: 606 us; the launch traced here: 601 us
  Pallas kernels  232 us (38%)
  waiting for transfers between devices  167 us (28%)
  other arithmetic  98.7 us (16%)
  starting transfers between devices  50.3 us (8%)
  local copies, waits for them, and re-layouts  28.4 us (5%)
  between operations  15.6 us (3%)
  matrix products  8.5 us (1%)
    pallas_call x12, Pallas kernels, by_group(): pl.pallas_call(in_order, out_shape=[ORDER_SHAPE, *shapes], grid=(g,), in_...  155 us
    ppermute x49, waiting for transfers between devices, swap(): return lax.ppermute(values, axis, pairs)  83.6 us
    all_gather x2, waiting for transfers between devices, gather_weight(): full = lax.all_gather(own_half(shard), EVERY, axis=0, tiled=True)  83.3 us
    pallas_call x8, Pallas kernels, weight_grads_near(): pl.pallas_call(kernel, out_shape=[ORDER_SHAPE, *shapes], grid_spec=pltpu....  72.3 us
    ppermute x49, starting transfers between devices, swap(): return lax.ppermute(values, axis, pairs)  47.9 us
    convert_element_type x24, other arithmetic, add_low(): return (left.astype(F32) + right.astype(F32)).astype(BF)  34.6 us
    reduce_sum x3, other arithmetic, rows_sum(): return jnp.sum(values, axis=-2).reshape(-1, width)  12.3 us
  transfers between devices with their start and end apart: 53, of which 12 were waited for; matrix products, arithmetic and copies ran while one was open for 20% of the time, Pallas kernels for 31%

profile of v4, /device:TPU:0, one launch (start us, length us, event | category | flops | bytes accessed | tf_op | source)
XLA Modules:
  0.0 600.6 jit_solution(8274828866484240091)
XLA Ops:
  12.8 3.1 collective-permute-start.5
  17.5 2.9 fusion.53
  23.2 2.7 collective-permute-start.6
  26.5 35.6 %collective-permute-done.6 = f32[2,576]{1,0:T(2,128)S(1)} collective-permute-done((f32[2,576]{1,0:T(2,128)S(1)}, f32[2,576]{1,0:T(2,128)S(1)}, u32[]{:S(2)}, u32[]{:S(2)}) %collective-permute-start.6) | collective-permute-done | bytes 4640 | tf_op jit(solution)/shard_map/ppermute | solution.py:47
  64.5 3.5 collective-permute-done.1
  68.3 2.8 multiply_convert_fusion.1.refs_1_.refs_0_
  72.3 4.1 fusion
  77.0 4.5 transposed.1
  81.5 83.3 %all-gather.3.cloned.1.call-done = bf16[4608,2304]{1,0:T(8,128)(2,1)} async-done(((bf16[144,2304]{1,0:T(8,128)(2,1)}), bf16[4608,2304]{1,0:T(8,128)(2,1)}) %all-gather.3.cloned.1.call-update) | async-done | bytes 21233680 | tf_op jit(solution)/shard_map/all_gather | solution.py:97
  164.8 16.4 %project_qkv.1 = (f32[8,128]{1,0:T(8,128)}, bf16[4,512,288]{2,1,0:T(8,128)(2,1)}, bf16[4,1024,288]{2,1,0:T(8,128)(2,1)}, bf16[4,1024,288]{2,1,0:T(8,128)(2,1)}) custom-call(f32[8,128]{1,0:T(8,128)} %get-tuple-element.152.order_ref, bf16[1024,1152]{1,0:T(8,128)(2,1)} %get-tuple-element.368.refs_0_, bf16[4,1152,2304]{2,1,0:T(8,128)(2,1)} %bitcast.158, ...), custom_call_target="tpu_custom_call" | custom-call | flops 8153726976 | bytes 29500416 | tf_op jit(solution)/shard_map/project_qkv/pallas_call | solution.py:219
  181.2 17.7 %attend.1 = (f32[8,128]{1,0:T(8,128)}, bf16[4,512,288]{2,1,0:T(8,128)(2,1)}, f32[4,4,512]{2,1,0:T(4,128)}, f32[4,4,512]{2,1,0:T(4,128)}) custom-call(f32[8,128]{1,0:T(8,128)} %get-tuple-element.153.order_ref, bf16[4,512,288]{2,1,0:T(8,128)(2,1)} %get-tuple-element.154.refs_0_, bf16[4,1024,288]{2,1,0:T(8,128)(2,1)} %get-tuple-element.155.refs_1_, ...), custom_call_target="tpu_custom_call" | custom-call | flops 8455716864 | bytes 7143424 | tf_op jit(solution)/shard_map/attend/pallas_call | solution.py:219
  198.9 7.0 %project_back.5 = (f32[8,128]{1,0:T(8,128)}, f32[512,1152]{1,0:T(8,128)}) custom-call(f32[8,128]{1,0:T(8,128)} %get-tuple-element.157.order_ref, bf16[4,512,288]{2,1,0:T(8,128)(2,1)} %get-tuple-element.158.refs_0_.refs_3_.refs_5_, bf16[4,1152,2304]{2,1,0:T(8,128)(2,1)} %bitcast.159), custom_call_target="tpu_custom_call" | custom-call | flops 1358954496 | bytes 24772608 | tf_op jit(solution)/shard_map/project_back/pallas_call | solution.py:219
  210.2 14.2 %project_up.1 = (f32[8,128]{1,0:T(8,128)}, bf16[4,512,1152]{2,1,0:T(8,128)(2,1)}, bf16[4,512,1152]{2,1,0:T(8,128)(2,1)}) custom-call(f32[8,128]{1,0:T(8,128)} %get-tuple-element.160.order_ref, bf16[512,1152]{1,0:T(8,128)(2,1)} %add_convert_fusion.1.refs_0_, bf16[4,1152,2304]{2,1,0:T(8,128)(2,1)} %bitcast.160, f32[4,1,1152]{2,1,0:T(1,128)} %broadcast_in_dim.38.refs_2_), custom_call_target="tpu_custom_call" | custom-call | flops 5435817984 | bytes 31868928 | tf_op jit(solution)/shard_map/project_up/pallas_call | solution.py:219
  224.4 7.9 %weight_grads_near.8 = (f32[8,128]{1,0:T(8,128)}, bf16[4,576,1152]{2,1,0:T(8,128)(2,1)}) custom-call(s32[2]{0:T(128)} %pad_add_fusion.place_ref, f32[8,128]{1,0:T(8,128)} %get-tuple-element.161.order_ref, bf16[4,2,144,512]{3,2,1,0:T(8,128)(2,1)} %bitcast.185, bf16[4,512,1152]{2,1,0:T(8,128)(2,1)} %get-tuple-element.163.refs_1_.refs_0_), custom_call_target="tpu_custom_call" | custom-call | flops 2717908992 | bytes 10027008 | tf_op jit(solution)/shard_map/weight_grads_near/pallas_call | solution.py:337
  234.4 7.8 %collective-permute-done.37 = bf16[8,288]{1,0:T(8,128)(2,1)S(1)} collective-permute-done((bf16[8,288]{1,0:T(8,128)(2,1)S(1)}, bf16[8,288]{1,0:T(8,128)(2,1)S(1)}, u32[]{:S(2)}, u32[]{:S(2)}) %collective-permute-start.37) | collective-permute-done | bytes 4640 | tf_op jit(solution)/shard_map/ppermute | solution.py:47
  246.2 9.7 %weight_grads_near.9 = (f32[8,128]{1,0:T(8,128)}, bf16[2,288,1152]{2,1,0:T(8,128)(2,1)}, bf16[2,288,1152]{2,1,0:T(8,128)(2,1)}, bf16[2,288,1152]{2,1,0:T(8,128)(2,1)}, bf16[2,288,1152]{2,1,0:T(8,128)(2,1)}) custom-call(s32[2]{0:T(128)} %pad_add_fusion.1.place_ref, f32[8,128]{1,0:T(8,128)} %get-tuple-element.166.order_ref, ...), custom_call_target="tpu_custom_call" | custom-call | flops 2717908992 | bytes 15335424 | tf_op jit(solution)/shard_map/weight_grads_near/pallas_call | solution.py:337
  255.9 12.5 %project_act_back.1 = (f32[8,128]{1,0:T(8,128)}, bf16[4,512,1152]{2,1,0:T(8,128)(2,1)}, f32[4,1,1152]{2,1,0:T(1,128)}) custom-call(f32[8,128]{1,0:T(8,128)} %get-tuple-element.168.order_ref, bf16[512,1152]{1,0:T(8,128)(2,1)} %multiply_convert_fusion.1.refs_1_.refs_0_, bf16[4,1152,1152]{2,1,0:T(8,128)(2,1)} %bitcast.189, ...), custom_call_target="tpu_custom_call" | custom-call | flops 5435817984 | bytes 21252096 | tf_op jit(solution)/shard_map/project_act_back/pallas_call | solution.py:219
  268.4 8.0 %weight_grads_near.10 = (f32[8,128]{1,0:T(8,128)}, bf16[4,576,1152]{2,1,0:T(8,128)(2,1)}) custom-call(s32[2]{0:T(128)} %pad_add_fusion.place_ref, f32[8,128]{1,0:T(8,128)} %get-tuple-element.170.order_ref, bf16[4,2,144,512]{3,2,1,0:T(8,128)(2,1)} %bitcast.171, bf16[4,512,1152]{2,1,0:T(8,128)(2,1)} %get-tuple-element.171.refs_1_.refs_0_), custom_call_target="tpu_custom_call" | custom-call | flops 2717908992 | bytes 10027008 | tf_op jit(solution)/shard_map/weight_grads_near/pallas_call | solution.py:337
  280.8 11.5 %project_back.6 = (f32[8,128]{1,0:T(8,128)}, f32[512,1152]{1,0:T(8,128)}) custom-call(f32[8,128]{1,0:T(8,128)} %get-tuple-element.172.order_ref, bf16[4,512,1152]{2,1,0:T(8,128)(2,1)} %get-tuple-element.171.refs_1_.refs_0_, bf16[4,1152,2304]{2,1,0:T(8,128)(2,1)} %bitcast.161), custom_call_target="tpu_custom_call" | custom-call | flops 5435817984 | bytes 28311552 | tf_op jit(solution)/shard_map/project_back/pallas_call | solution.py:219
  292.3 2.7 multiply_reduce_fusion.1
  294.9 11.9 %project_back.7 = (f32[8,128]{1,0:T(8,128)}, f32[512,1152]{1,0:T(8,128)}) custom-call(f32[8,128]{1,0:T(8,128)} %get-tuple-element.173.order_ref, bf16[4,512,1152]{2,1,0:T(8,128)(2,1)} %get-tuple-element.163.refs_1_.refs_0_, bf16[4,1152,1152]{2,1,0:T(8,128)(2,1)} %bitcast.190), custom_call_target="tpu_custom_call" | custom-call | flops 5435817984 | bytes 17694720 | tf_op jit(solution)/shard_map/project_back/pallas_call | solution.py:219
  306.9 5.9 multiply_reduce_fusion
  316.6 2.6 copy.71
  320.9 2.7 fusion.6
  324.8 2.7 fusion.7
  328.1 9.6 %weight_grads_near.11 = (f32[8,128]{1,0:T(8,128)}, bf16[2,288,1152]{2,1,0:T(8,128)(2,1)}, bf16[2,288,1152]{2,1,0:T(8,128)(2,1)}, bf16[2,288,1152]{2,1,0:T(8,128)(2,1)}, bf16[2,288,1152]{2,1,0:T(8,128)(2,1)}) custom-call(s32[2]{0:T(128)} %pad_add_fusion.1.place_ref, f32[8,128]{1,0:T(8,128)} %get-tuple-element.182.order_ref, ...), custom_call_target="tpu_custom_call" | custom-call | flops 2717908992 | bytes 15335424 | tf_op jit(solution)/shard_map/weight_grads_near/pallas_call | solution.py:337
  340.0 6.6 %project_mixed_back.1 = (f32[8,128]{1,0:T(8,128)}, bf16[4,512,288]{2,1,0:T(8,128)(2,1)}) custom-call(f32[8,128]{1,0:T(8,128)} %get-tuple-element.184.order_ref, bf16[512,1152]{1,0:T(8,128)(2,1)} %multiply_convert_fusion.refs_0_, bf16[4,1152,2304]{2,1,0:T(8,128)(2,1)} %bitcast.162), custom_call_target="tpu_custom_call" | custom-call | flops 1358954496 | bytes 23592960 | tf_op jit(solution)/shard_map/project_mixed_back/pallas_call | solution.py:219
  346.6 14.6 %attend_back.2 = (f32[8,128]{1,0:T(8,128)}, bf16[4,512,144]{2,1,0:T(8,128)(2,1)}, bf16[4,1024,144]{2,1,0:T(8,128)(2,1)}, bf16[4,1024,144]{2,1,0:T(8,128)(2,1)}) custom-call(f32[8,128]{1,0:T(8,128)} %get-tuple-element.185.order_ref, bf16[4,512,288]{2,1,0:T(8,128)(2,1)} %get-tuple-element.154.refs_0_, bf16[4,1024,288]{2,1,0:T(8,128)(2,1)} %get-tuple-element.155.refs_1_, ...), custom_call_target="tpu_custom_call" | custom-call | flops 10569646080 | bytes 11239424 | tf_op jit(solution)/shard_map/attend_back/pallas_call | solution.py:219
  361.2 9.6 %weight_grads_near.12 = (f32[8,128]{1,0:T(8,128)}, bf16[4,576,768]{2,1,0:T(8,128)(2,1)}) custom-call(s32[2]{0:T(128)} %pad_add_fusion.place_ref, f32[8,128]{1,0:T(8,128)} %get-tuple-element.188.order_ref, bf16[4,2,144,1024]{3,2,1,0:T(8,128)(2,1)} %bitcast.165, bf16[4,2,144,512]{3,2,1,0:T(8,128)(2,1)} %bitcast.169, ...), custom_call_target="tpu_custom_call" | custom-call | flops 2378170368 | bytes 7667712 | tf_op jit(solution)/shard_map/weight_grads_near/pallas_call | solution.py:337
  372.4 2.5 convert_reduce_fusion.2
  379.7 2.8 fusion.10
  384.1 2.7 fusion.11
  388.9 13.0 %project_back.8 = (f32[8,128]{1,0:T(8,128)}, f32[1024,1152]{1,0:T(8,128)}) custom-call(f32[8,128]{1,0:T(8,128)} %get-tuple-element.204.order_ref, bf16[4,512,144]{2,1,0:T(8,128)(2,1)} %get-tuple-element.190.refs_2_.refs_0_, bf16[4,1024,144]{2,1,0:T(8,128)(2,1)} %get-tuple-element.191.refs_3_.refs_1_, ...), custom_call_target="tpu_custom_call" | custom-call | flops 3397386240 | bytes 28901376 | tf_op jit(solution)/shard_map/project_back/pallas_call | solution.py:219
  403.9 10.5 %weight_grads_near.13 = (f32[8,128]{1,0:T(8,128)}, bf16[2,288,768]{2,1,0:T(8,128)(2,1)}, bf16[2,288,768]{2,1,0:T(8,128)(2,1)}, bf16[2,288,768]{2,1,0:T(8,128)(2,1)}, bf16[2,288,768]{2,1,0:T(8,128)(2,1)}) custom-call(s32[2]{0:T(128)} %pad_add_fusion.1.place_ref, f32[8,128]{1,0:T(8,128)} %get-tuple-element.217.order_ref, bf16[4,2,144,1024]{3,2,1,0:T(8,128)(2,1)} %bitcast.166, ...), custom_call_target="tpu_custom_call" | custom-call | flops 2378170368 | bytes 11206656 | tf_op jit(solution)/shard_map/weight_grads_near/pallas_call | solution.py:337
  414.5 15.1 %attend_back.3 = (f32[8,128]{1,0:T(8,128)}, bf16[4,512,144]{2,1,0:T(8,128)(2,1)}, bf16[4,1024,144]{2,1,0:T(8,128)(2,1)}, bf16[4,1024,144]{2,1,0:T(8,128)(2,1)}) custom-call(f32[8,128]{1,0:T(8,128)} %get-tuple-element.219.order_ref, bf16[4,512,288]{2,1,0:T(8,128)(2,1)} %get-tuple-element.154.refs_0_, bf16[4,1024,288]{2,1,0:T(8,128)(2,1)} %get-tuple-element.155.refs_1_, ...), custom_call_target="tpu_custom_call" | custom-call | flops 10569646080 | bytes 11239424 | tf_op jit(solution)/shard_map/attend_back/pallas_call | solution.py:219
  441.3 8.1 %weight_grads_near.14 = (f32[8,128]{1,0:T(8,128)}, bf16[4,576,512]{2,1,0:T(8,128)(2,1)}) custom-call(s32[2]{0:T(128)} %pad_add_fusion.place_ref, f32[8,128]{1,0:T(8,128)} %get-tuple-element.220.order_ref, bf16[4,2,144,1024]{3,2,1,0:T(8,128)(2,1)} %bitcast.167, bf16[4,512,144]{2,1,0:T(8,128)(2,1)} %get-tuple-element.221.refs_1_, ...), custom_call_target="tpu_custom_call" | custom-call | flops 1698693120 | bytes 5308416 | tf_op jit(solution)/shard_map/weight_grads_near/pallas_call | solution.py:337
  451.6 5.9 collective-permute-done.22
  471.9 14.9 %project_back.9 = (f32[8,128]{1,0:T(8,128)}, bf16[512,1152]{1,0:T(8,128)(2,1)}, f32[1024,1152]{1,0:T(8,128)}) custom-call(f32[8,128]{1,0:T(8,128)} %get-tuple-element.237.order_ref, f32[1024,1152]{1,0:T(8,128)} %get-tuple-element.238.refs_0_, bf16[4,512,144]{2,1,0:T(8,128)(2,1)} %get-tuple-element.221.refs_1_, ...), custom_call_target="tpu_custom_call" | custom-call | flops 3397386240 | bytes 34799616 | tf_op jit(solution)/shard_map/project_back/pallas_call | solution.py:219
  493.5 8.9 %weight_grads_near.15 = (f32[8,128]{1,0:T(8,128)}, bf16[2,288,512]{2,1,0:T(8,128)(2,1)}, bf16[2,288,512]{2,1,0:T(8,128)(2,1)}, bf16[2,288,512]{2,1,0:T(8,128)(2,1)}, bf16[2,288,512]{2,1,0:T(8,128)(2,1)}) custom-call(s32[2]{0:T(128)} %pad_add_fusion.1.place_ref, f32[8,128]{1,0:T(8,128)} %get-tuple-element.252.order_ref, bf16[4,2,144,1024]{3,2,1,0:T(8,128)(2,1)} %bitcast.168, ...), custom_call_target="tpu_custom_call" | custom-call | flops 1698693120 | bytes 7667712 | tf_op jit(solution)/shard_map/weight_grads_near/pallas_call | solution.py:337
  523.9 16.6 %collective-permute-done.40 = bf16[144,768]{1,0:T(8,128)(2,1)S(1)} collective-permute-done((bf16[144,768]{1,0:T(8,128)(2,1)S(1)}, bf16[144,768]{1,0:T(8,128)(2,1)S(1)}, u32[]{:S(2)}, u32[]{:S(2)}) %collective-permute-start.40) | collective-permute-done | bytes 221216 | tf_op jit(solution)/shard_map/ppermute | solution.py:47
  546.4 5.7 collective-permute-done.45
  554.1 2.6 collective-permute-start.46
  556.7 3.6 multiply_reduce_fusion.3
  561.3 5.0 multiply_add_fusion
  567.0 2.9 collective-permute-start.34
  572.9 2.5 collective-permute-start.47
  577.0 3.6 collective-permute-done.47
  589.1 4.5 fusion.41
  (391 shorter events, 129.5 us)
Async XLA Ops:
  7.2 157.6 %all-gather.3.cloned.1.call-start = ((), (), s32[]{:S(2)}) async-start(), calls=%async_computation | async-start | bytes 21897216 | tf_op jit(solution)/shard_map/all_gather | solution.py:97
  11.9 244.0 %all-gather.5.cloned.1.call-start = ((), (), s32[]{:S(2)}) async-start(), calls=%async_computation.1 | async-start | bytes 10948608 | tf_op jit(solution)/shard_map/all_gather | solution.py:97
  12.8 10.3 %collective-permute-start.5 = (f32[1,576]{1,0:T(1,128)S(1)}, f32[1,576]{1,0:T(1,128)S(1)}, u32[]{:S(2)}, u32[]{:S(2)}) collective-permute-start(f32[1,576]{1,0:T(1,128)S(1)} %broadcast_in_dim.37), channel_id=1, source_target_pairs={{0,4},{4,0},{8,12},{12,8},{1,5},{5,1},{9,13},{13,9},{2,6},{6,2},{1... | collective-permute-start | bytes 6920 | tf_op jit(solution)/shard_map/ppermute | solution.py:47
  16.0 9.9 %collective-permute-start.3 = (f32[1,1728]{1,0:T(1,128)S(1)}, f32[1,1728]{1,0:T(1,128)S(1)}, u32[]{:S(2)}, u32[]{:S(2)}) collective-permute-start(f32[1,1728]{1,0:T(1,128)S(1)} %broadcast_in_dim.34), channel_id=1, source_target_pairs={{0,1},{1,0},{2,3},{3,2},{4,5},{5,4},{6,7},{7,6},{8,9},{9,8},{10,11... | collective-permute-start | bytes 20744 | tf_op jit(solution)/shard_map/ppermute | solution.py:47
  20.6 41.8 %collective-permute-start = (f32[4,6,1152]{2,0,1:T(4,128)S(1)}, f32[4,6,1152]{2,0,1:T(4,128)S(1)}, u32[]{:S(2)}, u32[]{:S(2)}) collective-permute-start(f32[4,6,1152]{2,0,1:T(4,128)S(1)} %dynamic-slice_bitcast_fusion.7), channel_id=1, source_target_pairs={{0,2},{1,3},{2,0},{3,1},{4,6},{5,7},{6,4},{7,5},{8,10},{9,11},{10,... | collective-permute-start | bytes 331784 | tf_op jit(solution)/shard_map/ppermute | solution.py:47
  22.1 49.0 %collective-permute-start.2 = (bf16[512,1152]{1,0:T(8,128)(2,1)S(1)}, bf16[512,1152]{1,0:T(8,128)(2,1)S(1)}, u32[]{:S(2)}, u32[]{:S(2)}) collective-permute-start(bf16[512,1152]{1,0:T(8,128)(2,1)S(1)} %copy-done.4), channel_id=1, source_target_pairs={{0,4},{4,0},{8,12},{12,8},{1,5},{5,1},{9,13},{13,9},{2,6},{6,2},{1... | collective-permute-start | bytes 3538952 | tf_op jit(solution)/shard_map/ppermute | solution.py:593
  23.2 38.9 %collective-permute-start.6 = (f32[2,576]{1,0:T(2,128)S(1)}, f32[2,576]{1,0:T(2,128)S(1)}, u32[]{:S(2)}, u32[]{:S(2)}) collective-permute-start(f32[2,576]{1,0:T(2,128)S(1)} %pad_maximum_fusion.21), channel_id=1, source_target_pairs={{0,8},{4,12},{8,0},{12,4},{1,9},{5,13},{9,1},{13,5},{2,10},{6,14},... | collective-permute-start | bytes 13832 | tf_op jit(solution)/shard_map/ppermute | solution.py:47
  25.9 36.4 %collective-permute-start.4 = (f32[2,1728]{1,0:T(2,128)S(1)}, f32[2,1728]{1,0:T(2,128)S(1)}, u32[]{:S(2)}, u32[]{:S(2)}) collective-permute-start(f32[2,1728]{1,0:T(2,128)S(1)} %pad_maximum_fusion.8), channel_id=1, source_target_pairs={{0,2},{1,3},{2,0},{3,1},{4,6},{5,7},{6,4},{7,5},{8,10},{9,11},{10,... | collective-permute-start | bytes 41480 | tf_op jit(solution)/shard_map/ppermute | solution.py:47
  62.6 5.5 collective-permute-start.1
  232.3 13.9 %collective-permute-start.7 = (bf16[4,576,1152]{2,1,0:T(8,128)(2,1)}, bf16[4,576,1152]{2,1,0:T(8,128)(2,1)}, u32[]{:S(2)}, u32[]{:S(2)}) collective-permute-start(bf16[4,576,1152]{2,1,0:T(8,128)(2,1)} %get-tuple-element.165), channel_id=1, source_target_pairs={{0,16},{16,0},{1,17},{17,1},{2,18},{18,2},{3,19},{19,3},{4,20},{20... | collective-permute-start | bytes 15925256 | tf_op jit(solution)/shard_map/ppermute | solution.py:47
  232.5 9.7 %collective-permute-start.37 = (bf16[8,288]{1,0:T(8,128)(2,1)S(1)}, bf16[8,288]{1,0:T(8,128)(2,1)S(1)}, u32[]{:S(2)}, u32[]{:S(2)}) collective-permute-start(bf16[8,288]{1,0:T(8,128)(2,1)S(1)} %fusion.47), channel_id=1, source_target_pairs={{0,16},{16,0},{1,17},{17,1},{2,18},{18,2},{3,19},{19,3},{4,20},{20... | collective-permute-start | bytes 13832 | tf_op jit(solution)/shard_map/ppermute | solution.py:47
  276.4 44.0 %collective-permute-start.10 = (bf16[4,576,1152]{2,1,0:T(8,128)(2,1)}, bf16[4,576,1152]{2,1,0:T(8,128)(2,1)}, u32[]{:S(2)}, u32[]{:S(2)}) collective-permute-start(bf16[4,576,1152]{2,1,0:T(8,128)(2,1)} %get-tuple-element.181), channel_id=1, source_target_pairs={{0,16},{16,0},{1,17},{17,1},{2,18},{18,2},{3,19},{19,3},{4,20},{20... | collective-permute-start | bytes 15925256 | tf_op jit(solution)/shard_map/ppermute | solution.py:47
  278.4 42.0 %collective-permute-start.8 = (bf16[2,288,1152]{2,1,0:T(8,128)(2,1)}, bf16[2,288,1152]{2,1,0:T(8,128)(2,1)}, u32[]{:S(2)}, u32[]{:S(2)}) collective-permute-start(bf16[2,288,1152]{2,1,0:T(8,128)(2,1)} %get-tuple-element.179), channel_id=1, source_target_pairs={{0,1},{1,0},{2,3},{3,2},{4,5},{5,4},{6,7},{7,6},{8,9},{9,8},{10,11... | collective-permute-start | bytes 3981320 | tf_op jit(solution)/shard_map/ppermute | solution.py:47
  280.0 40.4 %collective-permute-start.9 = (bf16[2,288,1152]{2,1,0:T(8,128)(2,1)}, bf16[2,288,1152]{2,1,0:T(8,128)(2,1)}, u32[]{:S(2)}, u32[]{:S(2)}) collective-permute-start(bf16[2,288,1152]{2,1,0:T(8,128)(2,1)} %get-tuple-element.180), channel_id=1, source_target_pairs={{0,2},{1,3},{2,0},{3,1},{4,6},{5,7},{6,4},{7,5},{8,10},{9,11},{10,... | collective-permute-start | bytes 3981320 | tf_op jit(solution)/shard_map/ppermute | solution.py:47
  315.4 55.4 %collective-permute-start.11 = (f32[7,1152]{1,0:T(8,128)S(1)}, f32[7,1152]{1,0:T(8,128)S(1)}, u32[]{:S(2)}, u32[]{:S(2)}) collective-permute-start(f32[7,1152]{1,0:T(8,128)S(1)} %select_maximum_fusion), channel_id=1, source_target_pairs={{0,16},{16,0},{1,17},{17,1},{2,18},{18,2},{3,19},{19,3},{4,20},{20... | collective-permute-start | bytes 96776 | tf_op jit(solution)/shard_map/ppermute | solution.py:47
  323.6 51.3 %collective-permute-start.12 = (bf16[288,1152]{1,0:T(8,128)(2,1)}, bf16[288,1152]{1,0:T(8,128)(2,1)S(1)}, u32[]{:S(2)}, u32[]{:S(2)}) collective-permute-start(bf16[288,1152]{1,0:T(8,128)(2,1)} %get-tuple-element.361), channel_id=1, source_target_pairs={{0,2},{1,3},{2,0},{3,1},{4,6},{5,7},{6,4},{7,5},{8,10},{9,11},{10,... | collective-permute-start | bytes 1990664 | tf_op jit(solution)/shard_map/ppermute | solution.py:47
  327.6 47.4 %collective-permute-start.13 = (bf16[288,1152]{1,0:T(8,128)(2,1)}, bf16[288,1152]{1,0:T(8,128)(2,1)}, u32[]{:S(2)}, u32[]{:S(2)}) collective-permute-start(bf16[288,1152]{1,0:T(8,128)(2,1)} %get-tuple-element.359), channel_id=1, source_target_pairs={{0,1},{1,0},{2,3},{3,2},{4,5},{5,4},{6,7},{7,6},{8,9},{9,8},{10,11... | collective-permute-start | bytes 1990664 | tf_op jit(solution)/shard_map/ppermute | solution.py:47
  337.7 37.3 %collective-permute-start.14 = (bf16[2,288,1152]{2,1,0:T(8,128)(2,1)}, bf16[2,288,1152]{2,1,0:T(8,128)(2,1)}, u32[]{:S(2)}, u32[]{:S(2)}) collective-permute-start(bf16[2,288,1152]{2,1,0:T(8,128)(2,1)} %get-tuple-element.202), channel_id=1, source_target_pairs={{0,1},{1,0},{2,3},{3,2},{4,5},{5,4},{6,7},{7,6},{8,9},{9,8},{10,11... | collective-permute-start | bytes 3981320 | tf_op jit(solution)/shard_map/ppermute | solution.py:47
  339.2 35.8 %collective-permute-start.15 = (bf16[2,288,1152]{2,1,0:T(8,128)(2,1)}, bf16[2,288,1152]{2,1,0:T(8,128)(2,1)}, u32[]{:S(2)}, u32[]{:S(2)}) collective-permute-start(bf16[2,288,1152]{2,1,0:T(8,128)(2,1)} %get-tuple-element.203), channel_id=1, source_target_pairs={{0,2},{1,3},{2,0},{3,1},{4,6},{5,7},{6,4},{7,5},{8,10},{9,11},{10,... | collective-permute-start | bytes 3981320 | tf_op jit(solution)/shard_map/ppermute | solution.py:47
  370.9 33.1 %collective-permute-start.20 = (bf16[4,576,768]{2,1,0:T(8,128)(2,1)}, bf16[4,576,768]{2,1,0:T(8,128)(2,1)}, u32[]{:S(2)}, u32[]{:S(2)}) collective-permute-start(bf16[4,576,768]{2,1,0:T(8,128)(2,1)} %get-tuple-element.216), channel_id=1, source_target_pairs={{0,16},{16,0},{1,17},{17,1},{2,18},{18,2},{3,19},{19,3},{4,20},{20... | collective-permute-start | bytes 10616840 | tf_op jit(solution)/shard_map/ppermute | solution.py:47
  379.7 22.2 %collective-permute-start.17 = (bf16[2,144,1152]{2,1,0:T(8,128)(2,1)}, bf16[2,144,1152]{2,1,0:T(8,128)(2,1)S(1)}, u32[]{:S(2)}, u32[]{:S(2)}) collective-permute-start(bf16[2,144,1152]{2,1,0:T(8,128)(2,1)} %get-tuple-element.375), channel_id=1, source_target_pairs={{0,4},{4,0},{8,12},{12,8},{1,5},{5,1},{9,13},{13,9},{2,6},{6,2},{1... | collective-permute-start | bytes 1990664 | tf_op jit(solution)/shard_map/ppermute | solution.py:47
  382.5 19.4 %collective-permute-start.18 = (bf16[288,1152]{1,0:T(8,128)(2,1)}, bf16[288,1152]{1,0:T(8,128)(2,1)}, u32[]{:S(2)}, u32[]{:S(2)}) collective-permute-start(bf16[288,1152]{1,0:T(8,128)(2,1)} %get-tuple-element.357), channel_id=1, source_target_pairs={{0,2},{1,3},{2,0},{3,1},{4,6},{5,7},{6,4},{7,5},{8,10},{9,11},{10,... | collective-permute-start | bytes 1990664 | tf_op jit(solution)/shard_map/ppermute | solution.py:47
  386.8 17.1 %collective-permute-start.19 = (bf16[288,1152]{1,0:T(8,128)(2,1)}, bf16[288,1152]{1,0:T(8,128)(2,1)}, u32[]{:S(2)}, u32[]{:S(2)}) collective-permute-start(bf16[288,1152]{1,0:T(8,128)(2,1)} %get-tuple-element.355), channel_id=1, source_target_pairs={{0,1},{1,0},{2,3},{3,2},{4,5},{5,4},{6,7},{7,6},{8,9},{9,8},{10,11... | collective-permute-start | bytes 1990664 | tf_op jit(solution)/shard_map/ppermute | solution.py:47
  387.5 14.4 %collective-permute-start.16 = (f32[7,1152]{1,0:T(8,128)S(1)}, f32[7,1152]{1,0:T(8,128)S(1)}, u32[]{:S(2)}, u32[]{:S(2)}) collective-permute-start(f32[7,1152]{1,0:T(8,128)S(1)} %maximum_select_fusion.4), channel_id=1, source_target_pairs={{0,4},{4,0},{8,12},{12,8},{1,5},{5,1},{9,13},{13,9},{2,6},{6,2},{1... | collective-permute-start | bytes 96776 | tf_op jit(solution)/shard_map/ppermute | solution.py:47
  429.6 21.9 %collective-permute-start.21 = (f32[7,1152]{1,0:T(8,128)S(1)}, f32[7,1152]{1,0:T(8,128)S(1)}, u32[]{:S(2)}, u32[]{:S(2)}) collective-permute-start(f32[7,1152]{1,0:T(8,128)S(1)} %maximum_select_fusion.3), channel_id=1, source_target_pairs={{0,8},{4,12},{8,0},{12,4},{1,9},{5,13},{9,1},{13,5},{2,10},{6,14},... | collective-permute-start | bytes 96776 | tf_op jit(solution)/shard_map/ppermute | solution.py:47
  435.3 23.2 %collective-permute-start.23 = (bf16[2,144,1152]{2,1,0:T(8,128)(2,1)}, bf16[2,144,1152]{2,1,0:T(8,128)(2,1)}, u32[]{:S(2)}, u32[]{:S(2)}) collective-permute-start(bf16[2,144,1152]{2,1,0:T(8,128)(2,1)} %get-tuple-element.373), channel_id=1, source_target_pairs={{0,4},{4,0},{8,12},{12,8},{1,5},{5,1},{9,13},{13,9},{2,6},{6,2},{1... | collective-permute-start | bytes 1990664 | tf_op jit(solution)/shard_map/ppermute | solution.py:47
  437.0 21.5 %collective-permute-start.24 = (bf16[2,288,768]{2,1,0:T(8,128)(2,1)}, bf16[2,288,768]{2,1,0:T(8,128)(2,1)}, u32[]{:S(2)}, u32[]{:S(2)}) collective-permute-start(bf16[2,288,768]{2,1,0:T(8,128)(2,1)} %get-tuple-element.235), channel_id=1, source_target_pairs={{0,1},{1,0},{2,3},{3,2},{4,5},{5,4},{6,7},{7,6},{8,9},{9,8},{10,11... | collective-permute-start | bytes 2654216 | tf_op jit(solution)/shard_map/ppermute | solution.py:47
  437.7 20.8 %collective-permute-start.25 = (bf16[2,288,768]{2,1,0:T(8,128)(2,1)}, bf16[2,288,768]{2,1,0:T(8,128)(2,1)}, u32[]{:S(2)}, u32[]{:S(2)}) collective-permute-start(bf16[2,288,768]{2,1,0:T(8,128)(2,1)} %get-tuple-element.236), channel_id=1, source_target_pairs={{0,2},{1,3},{2,0},{3,1},{4,6},{5,7},{6,4},{7,5},{8,10},{9,11},{10,... | collective-permute-start | bytes 2654216 | tf_op jit(solution)/shard_map/ppermute | solution.py:47
  440.2 17.3 %collective-permute-start.22 = (bf16[144,1152]{1,0:T(8,128)(2,1)}, bf16[144,1152]{1,0:T(8,128)(2,1)S(1)}, u32[]{:S(2)}, u32[]{:S(2)}) collective-permute-start(bf16[144,1152]{1,0:T(8,128)(2,1)} %get-tuple-element.386), channel_id=1, source_target_pairs={{0,8},{4,12},{8,0},{12,4},{1,9},{5,13},{9,1},{13,5},{2,10},{6,14},... | collective-permute-start | bytes 995336 | tf_op jit(solution)/shard_map/ppermute | solution.py:47
  451.6 35.3 %collective-permute-start.31 = (bf16[4,576,512]{2,1,0:T(8,128)(2,1)}, bf16[4,576,512]{2,1,0:T(8,128)(2,1)}, u32[]{:S(2)}, u32[]{:S(2)}) collective-permute-start(bf16[4,576,512]{2,1,0:T(8,128)(2,1)} %get-tuple-element.251), channel_id=1, source_target_pairs={{0,16},{16,0},{1,17},{17,1},{2,18},{18,2},{3,19},{19,3},{4,20},{20... | collective-permute-start | bytes 7077896 | tf_op jit(solution)/shard_map/ppermute | solution.py:47
  458.6 10.2 %collective-permute-start.26 = (f32[7,1152]{1,0:T(8,128)S(1)}, f32[7,1152]{1,0:T(8,128)S(1)}, u32[]{:S(2)}, u32[]{:S(2)}) collective-permute-start(f32[7,1152]{1,0:T(8,128)S(1)} %maximum_select_fusion.2), channel_id=1, source_target_pairs={{0,1},{1,0},{2,3},{3,2},{4,5},{5,4},{6,7},{7,6},{8,9},{9,8},{10,11... | collective-permute-start | bytes 96776 | tf_op jit(solution)/shard_map/ppermute | solution.py:47
  460.2 26.7 %collective-permute-start.27 = (bf16[144,1152]{1,0:T(8,128)(2,1)}, bf16[144,1152]{1,0:T(8,128)(2,1)}, u32[]{:S(2)}, u32[]{:S(2)}) collective-permute-start(bf16[144,1152]{1,0:T(8,128)(2,1)} %add_convert_fusion.23), channel_id=1, source_target_pairs={{0,16},{16,0},{1,17},{17,1},{2,18},{18,2},{3,19},{19,3},{4,20},{20... | collective-permute-start | bytes 995336 | tf_op jit(solution)/shard_map/ppermute | solution.py:47
  462.4 24.4 %collective-permute-start.29 = (bf16[288,768]{1,0:T(8,128)(2,1)}, bf16[288,768]{1,0:T(8,128)(2,1)}, u32[]{:S(2)}, u32[]{:S(2)}) collective-permute-start(bf16[288,768]{1,0:T(8,128)(2,1)} %get-tuple-element.371), channel_id=1, source_target_pairs={{0,2},{1,3},{2,0},{3,1},{4,6},{5,7},{6,4},{7,5},{8,10},{9,11},{10,... | collective-permute-start | bytes 1327112 | tf_op jit(solution)/shard_map/ppermute | solution.py:47
  466.2 20.7 %collective-permute-start.30 = (bf16[288,768]{1,0:T(8,128)(2,1)}, bf16[288,768]{1,0:T(8,128)(2,1)}, u32[]{:S(2)}, u32[]{:S(2)}) collective-permute-start(bf16[288,768]{1,0:T(8,128)(2,1)} %get-tuple-element.369), channel_id=1, source_target_pairs={{0,1},{1,0},{2,3},{3,2},{4,5},{5,4},{6,7},{7,6},{8,9},{9,8},{10,11... | collective-permute-start | bytes 1327112 | tf_op jit(solution)/shard_map/ppermute | solution.py:47
  468.9 18.0 %collective-permute-start.28 = (bf16[144,1152]{1,0:T(8,128)(2,1)}, bf16[144,1152]{1,0:T(8,128)(2,1)S(1)}, u32[]{:S(2)}, u32[]{:S(2)}) collective-permute-start(bf16[144,1152]{1,0:T(8,128)(2,1)} %get-tuple-element.384), channel_id=1, source_target_pairs={{0,8},{4,12},{8,0},{12,4},{1,9},{5,13},{9,1},{13,5},{2,10},{6,14},... | collective-permute-start | bytes 995336 | tf_op jit(solution)/shard_map/ppermute | solution.py:47
  487.8 20.2 %collective-permute-start.49 = (f32[7,1152]{1,0:T(8,128)S(1)}, f32[7,1152]{1,0:T(8,128)S(1)}, u32[]{:S(2)}, u32[]{:S(2)}) collective-permute-start(f32[7,1152]{1,0:T(8,128)S(1)} %maximum_select_fusion.1), channel_id=1, source_target_pairs={{0,2},{1,3},{2,0},{3,1},{4,6},{5,7},{6,4},{7,5},{8,10},{9,11},{10,... | collective-permute-start | bytes 96776 | tf_op jit(solution)/shard_map/ppermute | solution.py:47
  490.0 27.3 %collective-permute-start.50 = (bf16[144,1152]{1,0:T(8,128)(2,1)}, bf16[144,1152]{1,0:T(8,128)(2,1)}, u32[]{:S(2)}, u32[]{:S(2)}) collective-permute-start(bf16[144,1152]{1,0:T(8,128)(2,1)} %add_convert_fusion.22), channel_id=1, source_target_pairs={{0,16},{16,0},{1,17},{17,1},{2,18},{18,2},{3,19},{19,3},{4,20},{20... | collective-permute-start | bytes 995336 | tf_op jit(solution)/shard_map/ppermute | solution.py:47
  493.1 26.5 %collective-permute-start.39 = (bf16[2,144,768]{2,1,0:T(8,128)(2,1)}, bf16[2,144,768]{2,1,0:T(8,128)(2,1)}, u32[]{:S(2)}, u32[]{:S(2)}) collective-permute-start(bf16[2,144,768]{2,1,0:T(8,128)(2,1)} %fusion.28), channel_id=1, source_target_pairs={{0,4},{4,0},{8,12},{12,8},{1,5},{5,1},{9,13},{13,9},{2,6},{6,2},{1... | collective-permute-start | bytes 1327112 | tf_op jit(solution)/shard_map/ppermute | solution.py:47
  502.4 19.2 %collective-permute-start.42 = (bf16[2,288,512]{2,1,0:T(8,128)(2,1)}, bf16[2,288,512]{2,1,0:T(8,128)(2,1)}, u32[]{:S(2)}, u32[]{:S(2)}) collective-permute-start(bf16[2,288,512]{2,1,0:T(8,128)(2,1)} %get-tuple-element.263), channel_id=1, source_target_pairs={{0,1},{1,0},{2,3},{3,2},{4,5},{5,4},{6,7},{7,6},{8,9},{9,8},{10,11... | collective-permute-start | bytes 1769480 | tf_op jit(solution)/shard_map/ppermute | solution.py:47
  502.9 37.7 %collective-permute-start.44 = (bf16[2,288,512]{2,1,0:T(8,128)(2,1)}, bf16[2,288,512]{2,1,0:T(8,128)(2,1)}, u32[]{:S(2)}, u32[]{:S(2)}) collective-permute-start(bf16[2,288,512]{2,1,0:T(8,128)(2,1)} %get-tuple-element.265), channel_id=1, source_target_pairs={{0,2},{1,3},{2,0},{3,1},{4,6},{5,7},{6,4},{7,5},{8,10},{9,11},{10,... | collective-permute-start | bytes 1769480 | tf_op jit(solution)/shard_map/ppermute | solution.py:47
  508.6 48.1 %collective-permute-start.32 = (bf16[512,1152]{1,0:T(8,128)(2,1)}, bf16[512,1152]{1,0:T(8,128)(2,1)}, u32[]{:S(2)}, u32[]{:S(2)}) collective-permute-start(bf16[512,1152]{1,0:T(8,128)(2,1)} %get-tuple-element.256), channel_id=1, source_target_pairs={{4,0},{0,4},{12,8},{8,12},{5,1},{1,5},{13,9},{9,13},{6,2},{2,6},{1... | collective-permute-start | bytes 3538952 | tf_op jit(solution)/shard_map/ppermute | solution.py:710
  520.8 19.7 %collective-permute-start.40 = (bf16[144,768]{1,0:T(8,128)(2,1)S(1)}, bf16[144,768]{1,0:T(8,128)(2,1)S(1)}, u32[]{:S(2)}, u32[]{:S(2)}) collective-permute-start(bf16[144,768]{1,0:T(8,128)(2,1)S(1)} %dynamic-slice_bitcast_fusion.5), channel_id=1, source_target_pairs={{0,8},{4,12},{8,0},{12,4},{1,9},{5,13},{9,1},{13,5},{2,10},{6,14},... | collective-permute-start | bytes 663560 | tf_op jit(solution)/shard_map/ppermute | solution.py:47
  523.3 21.8 %collective-permute-start.43 = (bf16[288,512]{1,0:T(8,128)(2,1)}, bf16[288,512]{1,0:T(8,128)(2,1)}, u32[]{:S(2)}, u32[]{:S(2)}) collective-permute-start(bf16[288,512]{1,0:T(8,128)(2,1)} %fusion.33), channel_id=1, source_target_pairs={{0,2},{1,3},{2,0},{3,1},{4,6},{5,7},{6,4},{7,5},{8,10},{9,11},{10,... | collective-permute-start | bytes 884744 | tf_op jit(solution)/shard_map/ppermute | solution.py:47
  542.4 9.7 %collective-permute-start.45 = (bf16[288,512]{1,0:T(8,128)(2,1)}, bf16[288,512]{1,0:T(8,128)(2,1)}, u32[]{:S(2)}, u32[]{:S(2)}) collective-permute-start(bf16[288,512]{1,0:T(8,128)(2,1)} %fusion.35), channel_id=1, source_target_pairs={{0,1},{1,0},{2,3},{3,2},{4,5},{5,4},{6,7},{7,6},{8,9},{9,8},{10,11... | collective-permute-start | bytes 884744 | tf_op jit(solution)/shard_map/ppermute | solution.py:47
  554.1 15.8 %collective-permute-start.46 = (bf16[2,144,512]{2,1,0:T(8,128)(2,1)}, bf16[2,144,512]{2,1,0:T(8,128)(2,1)}, u32[]{:S(2)}, u32[]{:S(2)}) collective-permute-start(bf16[2,144,512]{2,1,0:T(8,128)(2,1)} %fusion.37), channel_id=1, source_target_pairs={{0,4},{4,0},{8,12},{12,8},{1,5},{5,1},{9,13},{13,9},{2,6},{6,2},{1... | collective-permute-start | bytes 884744 | tf_op jit(solution)/shard_map/ppermute | solution.py:47
  561.2 5.1 collective-permute-start.33
  567.0 4.9 collective-permute-start.34
  572.9 7.8 %collective-permute-start.47 = (bf16[144,512]{1,0:T(8,128)(2,1)S(1)}, bf16[144,512]{1,0:T(8,128)(2,1)S(1)}, u32[]{:S(2)}, u32[]{:S(2)}) collective-permute-start(bf16[144,512]{1,0:T(8,128)(2,1)S(1)} %dynamic-slice_bitcast_fusion.6), channel_id=1, source_target_pairs={{0,8},{4,12},{8,0},{12,4},{1,9},{5,13},{9,1},{13,5},{2,10},{6,14},... | collective-permute-start | bytes 442376 | tf_op jit(solution)/shard_map/ppermute | solution.py:47
  (58 other events, 837.3 us)
Sparse Core Ops, SparseCore 0:
  12.0 152.7 all-gather.2
  168.4 84.8 all-gather.4

commit v5 on v4

--- a/solution.py
+++ b/solution.py
@@ -705,13 +705,18 @@
             grad_low, grad_ctx = grad_ctx
         order.tick(early, sum_down, sum_up, *sum_attn)
     grad_hidden_one = grad_ctx[:rows]
-    order.token, grad_low = lax.optimization_barrier((order.token, grad_low))
-    backs = [
-        lax.ppermute(
-            grad_low[(s - 1) * rows : s * rows], "gx", [(b, a) for a, b in shift_pairs(s)]
-        )
-        for s in range(1, span)
-    ]
+    if span == 2:
+        pairs = [[i, i + 1] for i in range(0, size_gx, 2)]
+        both = lax.all_gather(grad_low, "gx", axis=0, axis_index_groups=pairs)
+        order.token, both = lax.optimization_barrier((order.token, both))
+        backs = [pick(both, 1 - at_gx % 2)]
+    else:
+        backs = [
+            lax.ppermute(
+                grad_low[(s - 1) * rows : s * rows], "gx", [(b, a) for a, b in shift_pairs(s)]
+            )
+            for s in range(1, span)
+        ]
     for back in backs:
         grad_hidden_one += back.astype(F32)
     grad_input = grad_after + normalize_back(

time: 606 us -> 598 us (0.987)
  waiting for transfers between devices: 167 us -> 160 us
    ppermute x49, waiting for transfers between devices: 83.6 us -> 71.4 us  [swap(): return lax.ppermute(values, axis, pairs)]
  transfers between devices with their start and end apart: 53 -> 53, of which waited for: 12 -> 14; matrix products, arithmetic and copies ran while one was open for 20% -> 21% of each run, Pallas kernels for 31% -> 31%
where the time goes in v5:
time: 598 us; the launch traced here: 592 us
  Pallas kernels  232 us (39%)
  waiting for transfers between devices  160 us (27%)
  other arithmetic  97.4 us (16%)
  starting transfers between devices  51 us (9%)
  local copies, waits for them, and re-layouts  27.8 us (5%)
  between operations  15.2 us (3%)
  matrix products  8.5 us (1%)
    pallas_call x12, Pallas kernels, by_group(): pl.pallas_call(in_order, out_shape=[ORDER_SHAPE, *shapes], grid=(g,), in_...  155 us
    all_gather x2, waiting for transfers between devices, gather_weight(): full = lax.all_gather(own_half(shard), EVERY, axis=0, tiled=True)  83.3 us
    pallas_call x8, Pallas kernels, weight_grads_near(): pl.pallas_call(kernel, out_shape=[ORDER_SHAPE, *shapes], grid_spec=pltpu....  72.3 us
    ppermute x49, waiting for transfers between devices, swap(): return lax.ppermute(values, axis, pairs)  71.4 us
    ppermute x49, starting transfers between devices, swap(): return lax.ppermute(values, axis, pairs)  50.4 us
    convert_element_type x24, other arithmetic, add_low(): return (left.astype(F32) + right.astype(F32)).astype(BF)  33.7 us
    reduce_sum x3, other arithmetic, rows_sum(): return jnp.sum(values, axis=-2).reshape(-1, width)  13.6 us
  transfers between devices with their start and end apart: 53, of which 14 were waited for; matrix products, arithmetic and copies ran while one was open for 21% of the time, Pallas kernels for 31%

profile of v5, /device:TPU:0, one launch (start us, length us, event | category | flops | bytes accessed | tf_op | source)
XLA Modules:
  0.0 592.5 jit_solution(9392189374679759408)
XLA Ops:
  8.5 2.5 concatenate.109
  12.9 3.1 collective-permute-start.5
  17.6 2.9 fusion.53
  23.3 2.7 collective-permute-start.6
  26.5 35.6 %collective-permute-done.6 = f32[2,576]{1,0:T(2,128)S(1)} collective-permute-done((f32[2,576]{1,0:T(2,128)S(1)}, f32[2,576]{1,0:T(2,128)S(1)}, u32[]{:S(2)}, u32[]{:S(2)}) %collective-permute-start.6) | collective-permute-done | bytes 4640 | tf_op jit(solution)/shard_map/ppermute | solution.py:47
  64.6 3.5 collective-permute-done.1
  68.3 2.8 multiply_convert_fusion.1.refs_1_.refs_0_
  72.3 4.1 fusion
  77.0 4.5 transposed.1
  81.6 83.3 %all-gather.5.cloned.1.call-done = bf16[4608,2304]{1,0:T(8,128)(2,1)} async-done(((bf16[144,2304]{1,0:T(8,128)(2,1)}), bf16[4608,2304]{1,0:T(8,128)(2,1)}) %all-gather.5.cloned.1.call-update) | async-done | bytes 21233680 | tf_op jit(solution)/shard_map/all_gather | solution.py:97
  164.9 16.4 %project_qkv.1 = (f32[8,128]{1,0:T(8,128)}, bf16[4,512,288]{2,1,0:T(8,128)(2,1)}, bf16[4,1024,288]{2,1,0:T(8,128)(2,1)}, bf16[4,1024,288]{2,1,0:T(8,128)(2,1)}) custom-call(f32[8,128]{1,0:T(8,128)} %get-tuple-element.152.order_ref, bf16[1024,1152]{1,0:T(8,128)(2,1)} %get-tuple-element.369.refs_0_, bf16[4,1152,2304]{2,1,0:T(8,128)(2,1)} %bitcast.163, ...), custom_call_target="tpu_custom_call" | custom-call | flops 8153726976 | bytes 29500416 | tf_op jit(solution)/shard_map/project_qkv/pallas_call | solution.py:219
  181.3 17.6 %attend.1 = (f32[8,128]{1,0:T(8,128)}, bf16[4,512,288]{2,1,0:T(8,128)(2,1)}, f32[4,4,512]{2,1,0:T(4,128)}, f32[4,4,512]{2,1,0:T(4,128)}) custom-call(f32[8,128]{1,0:T(8,128)} %get-tuple-element.153.order_ref, bf16[4,512,288]{2,1,0:T(8,128)(2,1)} %get-tuple-element.154.refs_0_, bf16[4,1024,288]{2,1,0:T(8,128)(2,1)} %get-tuple-element.155.refs_1_, ...), custom_call_target="tpu_custom_call" | custom-call | flops 8455716864 | bytes 7143424 | tf_op jit(solution)/shard_map/attend/pallas_call | solution.py:219
  198.9 7.0 %project_back.5 = (f32[8,128]{1,0:T(8,128)}, f32[512,1152]{1,0:T(8,128)}) custom-call(f32[8,128]{1,0:T(8,128)} %get-tuple-element.157.order_ref, bf16[4,512,288]{2,1,0:T(8,128)(2,1)} %get-tuple-element.158.refs_0_.refs_3_.refs_5_, bf16[4,1152,2304]{2,1,0:T(8,128)(2,1)} %bitcast.164), custom_call_target="tpu_custom_call" | custom-call | flops 1358954496 | bytes 24772608 | tf_op jit(solution)/shard_map/project_back/pallas_call | solution.py:219
  205.9 2.5 fusion.64
  210.3 14.2 %project_up.1 = (f32[8,128]{1,0:T(8,128)}, bf16[4,512,1152]{2,1,0:T(8,128)(2,1)}, bf16[4,512,1152]{2,1,0:T(8,128)(2,1)}) custom-call(f32[8,128]{1,0:T(8,128)} %get-tuple-element.160.order_ref, bf16[512,1152]{1,0:T(8,128)(2,1)} %add_convert_fusion.1.refs_0_, bf16[4,1152,2304]{2,1,0:T(8,128)(2,1)} %bitcast.165, f32[4,1,1152]{2,1,0:T(1,128)} %broadcast_in_dim.38.refs_2_), custom_call_target="tpu_custom_call" | custom-call | flops 5435817984 | bytes 31868928 | tf_op jit(solution)/shard_map/project_up/pallas_call | solution.py:219
  224.4 7.9 %weight_grads_near.8 = (f32[8,128]{1,0:T(8,128)}, bf16[4,576,1152]{2,1,0:T(8,128)(2,1)}) custom-call(s32[2]{0:T(128)} %pad_add_fusion.place_ref, f32[8,128]{1,0:T(8,128)} %get-tuple-element.161.order_ref, bf16[4,2,144,512]{3,2,1,0:T(8,128)(2,1)} %bitcast.190, bf16[4,512,1152]{2,1,0:T(8,128)(2,1)} %get-tuple-element.163.refs_1_.refs_0_), custom_call_target="tpu_custom_call" | custom-call | flops 2717908992 | bytes 10027008 | tf_op jit(solution)/shard_map/weight_grads_near/pallas_call | solution.py:337
  234.4 7.8 %collective-permute-done.36 = bf16[8,288]{1,0:T(8,128)(2,1)S(1)} collective-permute-done((bf16[8,288]{1,0:T(8,128)(2,1)S(1)}, bf16[8,288]{1,0:T(8,128)(2,1)S(1)}, u32[]{:S(2)}, u32[]{:S(2)}) %collective-permute-start.36) | collective-permute-done | bytes 4640 | tf_op jit(solution)/shard_map/ppermute | solution.py:47
  246.2 9.7 %weight_grads_near.9 = (f32[8,128]{1,0:T(8,128)}, bf16[2,288,1152]{2,1,0:T(8,128)(2,1)}, bf16[2,288,1152]{2,1,0:T(8,128)(2,1)}, bf16[2,288,1152]{2,1,0:T(8,128)(2,1)}, bf16[2,288,1152]{2,1,0:T(8,128)(2,1)}) custom-call(s32[2]{0:T(128)} %pad_add_fusion.1.place_ref, f32[8,128]{1,0:T(8,128)} %get-tuple-element.166.order_ref, ...), custom_call_target="tpu_custom_call" | custom-call | flops 2717908992 | bytes 15335424 | tf_op jit(solution)/shard_map/weight_grads_near/pallas_call | solution.py:337
  256.0 12.5 %project_act_back.1 = (f32[8,128]{1,0:T(8,128)}, bf16[4,512,1152]{2,1,0:T(8,128)(2,1)}, f32[4,1,1152]{2,1,0:T(1,128)}) custom-call(f32[8,128]{1,0:T(8,128)} %get-tuple-element.168.order_ref, bf16[512,1152]{1,0:T(8,128)(2,1)} %multiply_convert_fusion.1.refs_1_.refs_0_, bf16[4,1152,1152]{2,1,0:T(8,128)(2,1)} %bitcast.195, ...), custom_call_target="tpu_custom_call" | custom-call | flops 5435817984 | bytes 21252096 | tf_op jit(solution)/shard_map/project_act_back/pallas_call | solution.py:219
  268.5 8.0 %weight_grads_near.10 = (f32[8,128]{1,0:T(8,128)}, bf16[4,576,1152]{2,1,0:T(8,128)(2,1)}) custom-call(s32[2]{0:T(128)} %pad_add_fusion.place_ref, f32[8,128]{1,0:T(8,128)} %get-tuple-element.170.order_ref, bf16[4,2,144,512]{3,2,1,0:T(8,128)(2,1)} %bitcast.176, bf16[4,512,1152]{2,1,0:T(8,128)(2,1)} %get-tuple-element.171.refs_1_.refs_0_), custom_call_target="tpu_custom_call" | custom-call | flops 2717908992 | bytes 10027008 | tf_op jit(solution)/shard_map/weight_grads_near/pallas_call | solution.py:337
  280.8 11.5 %project_back.6 = (f32[8,128]{1,0:T(8,128)}, f32[512,1152]{1,0:T(8,128)}) custom-call(f32[8,128]{1,0:T(8,128)} %get-tuple-element.172.order_ref, bf16[4,512,1152]{2,1,0:T(8,128)(2,1)} %get-tuple-element.171.refs_1_.refs_0_, bf16[4,1152,2304]{2,1,0:T(8,128)(2,1)} %bitcast.166), custom_call_target="tpu_custom_call" | custom-call | flops 5435817984 | bytes 28311552 | tf_op jit(solution)/shard_map/project_back/pallas_call | solution.py:219
  292.3 2.7 multiply_reduce_fusion.1
  295.0 11.9 %project_back.7 = (f32[8,128]{1,0:T(8,128)}, f32[512,1152]{1,0:T(8,128)}) custom-call(f32[8,128]{1,0:T(8,128)} %get-tuple-element.173.order_ref, bf16[4,512,1152]{2,1,0:T(8,128)(2,1)} %get-tuple-element.163.refs_1_.refs_0_, bf16[4,1152,1152]{2,1,0:T(8,128)(2,1)} %bitcast.196), custom_call_target="tpu_custom_call" | custom-call | flops 5435817984 | bytes 17694720 | tf_op jit(solution)/shard_map/project_back/pallas_call | solution.py:219
  306.9 5.9 %multiply_reduce_fusion = (f32[1152]{0:T(1024)S(1)}, f32[1152]{0:T(1024)S(1)}, f32[512,1152]{1,0:T(8,128)}, f32[1152]{0:T(1024)S(1)}, f32[1152]{0:T(1024)S(1)}, /*index=5*/f32[512,1152]{1,0:T(8,128)S(1)}) fusion(f32[512,1152]{1,0:T(8,128)} %param.33, f32[512,1152]{1,0:T(8,128)} %get-tuple-element.174, f32[1152]{0:T(1024)S(1)} %add.369, ...), kind=kLoop, calls=%fused_computation.10 | loop fusion | flops 11791872 | bytes 16564736 | tf_op jit(solution)/shard_map/reduce_sum | solution.py:587
  316.6 2.6 copy.71
  320.9 2.7 fusion.6
  324.9 2.7 fusion.7
  328.1 9.6 %weight_grads_near.11 = (f32[8,128]{1,0:T(8,128)}, bf16[2,288,1152]{2,1,0:T(8,128)(2,1)}, bf16[2,288,1152]{2,1,0:T(8,128)(2,1)}, bf16[2,288,1152]{2,1,0:T(8,128)(2,1)}, bf16[2,288,1152]{2,1,0:T(8,128)(2,1)}) custom-call(s32[2]{0:T(128)} %pad_add_fusion.1.place_ref, f32[8,128]{1,0:T(8,128)} %get-tuple-element.182.order_ref, ...), custom_call_target="tpu_custom_call" | custom-call | flops 2717908992 | bytes 15335424 | tf_op jit(solution)/shard_map/weight_grads_near/pallas_call | solution.py:337
  340.0 6.5 %project_mixed_back.1 = (f32[8,128]{1,0:T(8,128)}, bf16[4,512,288]{2,1,0:T(8,128)(2,1)}) custom-call(f32[8,128]{1,0:T(8,128)} %get-tuple-element.184.order_ref, bf16[512,1152]{1,0:T(8,128)(2,1)} %multiply_convert_fusion.refs_0_, bf16[4,1152,2304]{2,1,0:T(8,128)(2,1)} %bitcast.167), custom_call_target="tpu_custom_call" | custom-call | flops 1358954496 | bytes 23592960 | tf_op jit(solution)/shard_map/project_mixed_back/pallas_call | solution.py:219
  346.6 14.6 %attend_back.2 = (f32[8,128]{1,0:T(8,128)}, bf16[4,512,144]{2,1,0:T(8,128)(2,1)}, bf16[4,1024,144]{2,1,0:T(8,128)(2,1)}, bf16[4,1024,144]{2,1,0:T(8,128)(2,1)}) custom-call(f32[8,128]{1,0:T(8,128)} %get-tuple-element.185.order_ref, bf16[4,512,288]{2,1,0:T(8,128)(2,1)} %get-tuple-element.154.refs_0_, bf16[4,1024,288]{2,1,0:T(8,128)(2,1)} %get-tuple-element.155.refs_1_, ...), custom_call_target="tpu_custom_call" | custom-call | flops 10569646080 | bytes 11239424 | tf_op jit(solution)/shard_map/attend_back/pallas_call | solution.py:219
  361.2 9.6 %weight_grads_near.12 = (f32[8,128]{1,0:T(8,128)}, bf16[4,576,768]{2,1,0:T(8,128)(2,1)}) custom-call(s32[2]{0:T(128)} %pad_add_fusion.place_ref, f32[8,128]{1,0:T(8,128)} %get-tuple-element.188.order_ref, bf16[4,2,144,1024]{3,2,1,0:T(8,128)(2,1)} %bitcast.170, bf16[4,2,144,512]{3,2,1,0:T(8,128)(2,1)} %bitcast.174, ...), custom_call_target="tpu_custom_call" | custom-call | flops 2378170368 | bytes 7667712 | tf_op jit(solution)/shard_map/weight_grads_near/pallas_call | solution.py:337
  372.4 2.5 convert_reduce_fusion.2
  379.7 2.8 fusion.10
  384.1 2.7 fusion.11
  389.0 12.9 %project_back.8 = (f32[8,128]{1,0:T(8,128)}, f32[1024,1152]{1,0:T(8,128)}) custom-call(f32[8,128]{1,0:T(8,128)} %get-tuple-element.204.order_ref, bf16[4,512,144]{2,1,0:T(8,128)(2,1)} %get-tuple-element.190.refs_2_.refs_0_, bf16[4,1024,144]{2,1,0:T(8,128)(2,1)} %get-tuple-element.191.refs_3_.refs_1_, ...), custom_call_target="tpu_custom_call" | custom-call | flops 3397386240 | bytes 28901376 | tf_op jit(solution)/shard_map/project_back/pallas_call | solution.py:219
  403.9 10.5 %weight_grads_near.13 = (f32[8,128]{1,0:T(8,128)}, bf16[2,288,768]{2,1,0:T(8,128)(2,1)}, bf16[2,288,768]{2,1,0:T(8,128)(2,1)}, bf16[2,288,768]{2,1,0:T(8,128)(2,1)}, bf16[2,288,768]{2,1,0:T(8,128)(2,1)}) custom-call(s32[2]{0:T(128)} %pad_add_fusion.1.place_ref, f32[8,128]{1,0:T(8,128)} %get-tuple-element.217.order_ref, bf16[4,2,144,1024]{3,2,1,0:T(8,128)(2,1)} %bitcast.171, ...), custom_call_target="tpu_custom_call" | custom-call | flops 2378170368 | bytes 11206656 | tf_op jit(solution)/shard_map/weight_grads_near/pallas_call | solution.py:337
  414.5 15.1 %attend_back.3 = (f32[8,128]{1,0:T(8,128)}, bf16[4,512,144]{2,1,0:T(8,128)(2,1)}, bf16[4,1024,144]{2,1,0:T(8,128)(2,1)}, bf16[4,1024,144]{2,1,0:T(8,128)(2,1)}) custom-call(f32[8,128]{1,0:T(8,128)} %get-tuple-element.219.order_ref, bf16[4,512,288]{2,1,0:T(8,128)(2,1)} %get-tuple-element.154.refs_0_, bf16[4,1024,288]{2,1,0:T(8,128)(2,1)} %get-tuple-element.155.refs_1_, ...), custom_call_target="tpu_custom_call" | custom-call | flops 10569646080 | bytes 11239424 | tf_op jit(solution)/shard_map/attend_back/pallas_call | solution.py:219
  441.4 8.1 %weight_grads_near.14 = (f32[8,128]{1,0:T(8,128)}, bf16[4,576,512]{2,1,0:T(8,128)(2,1)}) custom-call(s32[2]{0:T(128)} %pad_add_fusion.place_ref, f32[8,128]{1,0:T(8,128)} %get-tuple-element.220.order_ref, bf16[4,2,144,1024]{3,2,1,0:T(8,128)(2,1)} %bitcast.172, bf16[4,512,144]{2,1,0:T(8,128)(2,1)} %get-tuple-element.221.refs_1_, ...), custom_call_target="tpu_custom_call" | custom-call | flops 1698693120 | bytes 5308416 | tf_op jit(solution)/shard_map/weight_grads_near/pallas_call | solution.py:337
  451.7 5.8 collective-permute-done.22
  471.9 15.0 %project_back.9 = (f32[8,128]{1,0:T(8,128)}, bf16[512,1152]{1,0:T(8,128)(2,1)}, f32[1024,1152]{1,0:T(8,128)}) custom-call(f32[8,128]{1,0:T(8,128)} %get-tuple-element.237.order_ref, f32[1024,1152]{1,0:T(8,128)} %get-tuple-element.238.refs_0_, bf16[4,512,144]{2,1,0:T(8,128)(2,1)} %get-tuple-element.221.refs_1_, ...), custom_call_target="tpu_custom_call" | custom-call | flops 3397386240 | bytes 34799616 | tf_op jit(solution)/shard_map/project_back/pallas_call | solution.py:219
  493.7 8.8 %weight_grads_near.15 = (f32[8,128]{1,0:T(8,128)}, bf16[2,288,512]{2,1,0:T(8,128)(2,1)}, bf16[2,288,512]{2,1,0:T(8,128)(2,1)}, bf16[2,288,512]{2,1,0:T(8,128)(2,1)}, bf16[2,288,512]{2,1,0:T(8,128)(2,1)}) custom-call(s32[2]{0:T(128)} %pad_add_fusion.1.place_ref, f32[8,128]{1,0:T(8,128)} %get-tuple-element.252.order_ref, bf16[4,2,144,1024]{3,2,1,0:T(8,128)(2,1)} %bitcast.173, ...), custom_call_target="tpu_custom_call" | custom-call | flops 1698693120 | bytes 7667712 | tf_op jit(solution)/shard_map/weight_grads_near/pallas_call | solution.py:337
  524.9 4.5 collective-permute-done.39
  529.5 5.7 all-gather.9.cloned.1.call-done
  536.5 5.0 multiply_reduce_fusion.3
  544.0 3.7 multiply_add_fusion
  549.7 2.7 collective-permute-start.33
  570.2 5.8 collective-permute-done.46
  576.1 4.5 fusion.41
  (392 shorter events, 132.1 us)
Async XLA Ops:
  7.2 157.7 %all-gather.5.cloned.1.call-start = ((), (), s32[]{:S(2)}) async-start(), calls=%async_computation | async-start | bytes 21897216 | tf_op jit(solution)/shard_map/all_gather | solution.py:97
  11.9 244.1 %all-gather.7.cloned.1.call-start = ((), (), s32[]{:S(2)}) async-start(), calls=%async_computation.1 | async-start | bytes 10948608 | tf_op jit(solution)/shard_map/all_gather | solution.py:97
  12.7 522.5 %all-gather.9.cloned.1.call-start = ((), (), s32[]{:S(2)}) async-start(), calls=%async_computation.2 | async-start | bytes 3538944 | tf_op jit(solution)/shard_map/all_gather | solution.py:710
  12.9 10.3 %collective-permute-start.5 = (f32[1,576]{1,0:T(1,128)S(1)}, f32[1,576]{1,0:T(1,128)S(1)}, u32[]{:S(2)}, u32[]{:S(2)}) collective-permute-start(f32[1,576]{1,0:T(1,128)S(1)} %broadcast_in_dim.37), channel_id=1, source_target_pairs={{0,4},{4,0},{8,12},{12,8},{1,5},{5,1},{9,13},{13,9},{2,6},{6,2},{1... | collective-permute-start | bytes 6920 | tf_op jit(solution)/shard_map/ppermute | solution.py:47
  16.0 9.9 %collective-permute-start.3 = (f32[1,1728]{1,0:T(1,128)S(1)}, f32[1,1728]{1,0:T(1,128)S(1)}, u32[]{:S(2)}, u32[]{:S(2)}) collective-permute-start(f32[1,1728]{1,0:T(1,128)S(1)} %broadcast_in_dim.34), channel_id=1, source_target_pairs={{0,1},{1,0},{2,3},{3,2},{4,5},{5,4},{6,7},{7,6},{8,9},{9,8},{10,11... | collective-permute-start | bytes 20744 | tf_op jit(solution)/shard_map/ppermute | solution.py:47
  20.6 41.8 %collective-permute-start = (f32[4,6,1152]{2,0,1:T(4,128)S(1)}, f32[4,6,1152]{2,0,1:T(4,128)S(1)}, u32[]{:S(2)}, u32[]{:S(2)}) collective-permute-start(f32[4,6,1152]{2,0,1:T(4,128)S(1)} %dynamic-slice_bitcast_fusion.7), channel_id=1, source_target_pairs={{0,2},{1,3},{2,0},{3,1},{4,6},{5,7},{6,4},{7,5},{8,10},{9,11},{10,... | collective-permute-start | bytes 331784 | tf_op jit(solution)/shard_map/ppermute | solution.py:47
  22.2 49.0 %collective-permute-start.2 = (bf16[512,1152]{1,0:T(8,128)(2,1)S(1)}, bf16[512,1152]{1,0:T(8,128)(2,1)S(1)}, u32[]{:S(2)}, u32[]{:S(2)}) collective-permute-start(bf16[512,1152]{1,0:T(8,128)(2,1)S(1)} %copy-done.4), channel_id=1, source_target_pairs={{0,4},{4,0},{8,12},{12,8},{1,5},{5,1},{9,13},{13,9},{2,6},{6,2},{1... | collective-permute-start | bytes 3538952 | tf_op jit(solution)/shard_map/ppermute | solution.py:593
  23.3 38.9 %collective-permute-start.6 = (f32[2,576]{1,0:T(2,128)S(1)}, f32[2,576]{1,0:T(2,128)S(1)}, u32[]{:S(2)}, u32[]{:S(2)}) collective-permute-start(f32[2,576]{1,0:T(2,128)S(1)} %pad_maximum_fusion.21), channel_id=1, source_target_pairs={{0,8},{4,12},{8,0},{12,4},{1,9},{5,13},{9,1},{13,5},{2,10},{6,14},... | collective-permute-start | bytes 13832 | tf_op jit(solution)/shard_map/ppermute | solution.py:47
  26.0 36.4 %collective-permute-start.4 = (f32[2,1728]{1,0:T(2,128)S(1)}, f32[2,1728]{1,0:T(2,128)S(1)}, u32[]{:S(2)}, u32[]{:S(2)}) collective-permute-start(f32[2,1728]{1,0:T(2,128)S(1)} %pad_maximum_fusion.8), channel_id=1, source_target_pairs={{0,2},{1,3},{2,0},{3,1},{4,6},{5,7},{6,4},{7,5},{8,10},{9,11},{10,... | collective-permute-start | bytes 41480 | tf_op jit(solution)/shard_map/ppermute | solution.py:47
  232.3 13.9 %collective-permute-start.7 = (bf16[4,576,1152]{2,1,0:T(8,128)(2,1)}, bf16[4,576,1152]{2,1,0:T(8,128)(2,1)}, u32[]{:S(2)}, u32[]{:S(2)}) collective-permute-start(bf16[4,576,1152]{2,1,0:T(8,128)(2,1)} %get-tuple-element.165), channel_id=1, source_target_pairs={{0,16},{16,0},{1,17},{17,1},{2,18},{18,2},{3,19},{19,3},{4,20},{20... | collective-permute-start | bytes 15925256 | tf_op jit(solution)/shard_map/ppermute | solution.py:47
  232.6 9.6 %collective-permute-start.36 = (bf16[8,288]{1,0:T(8,128)(2,1)S(1)}, bf16[8,288]{1,0:T(8,128)(2,1)S(1)}, u32[]{:S(2)}, u32[]{:S(2)}) collective-permute-start(bf16[8,288]{1,0:T(8,128)(2,1)S(1)} %fusion.47), channel_id=1, source_target_pairs={{0,16},{16,0},{1,17},{17,1},{2,18},{18,2},{3,19},{19,3},{4,20},{20... | collective-permute-start | bytes 13832 | tf_op jit(solution)/shard_map/ppermute | solution.py:47
  276.5 43.9 %collective-permute-start.10 = (bf16[4,576,1152]{2,1,0:T(8,128)(2,1)}, bf16[4,576,1152]{2,1,0:T(8,128)(2,1)}, u32[]{:S(2)}, u32[]{:S(2)}) collective-permute-start(bf16[4,576,1152]{2,1,0:T(8,128)(2,1)} %get-tuple-element.181), channel_id=1, source_target_pairs={{0,16},{16,0},{1,17},{17,1},{2,18},{18,2},{3,19},{19,3},{4,20},{20... | collective-permute-start | bytes 15925256 | tf_op jit(solution)/shard_map/ppermute | solution.py:47
  278.5 41.9 %collective-permute-start.8 = (bf16[2,288,1152]{2,1,0:T(8,128)(2,1)}, bf16[2,288,1152]{2,1,0:T(8,128)(2,1)}, u32[]{:S(2)}, u32[]{:S(2)}) collective-permute-start(bf16[2,288,1152]{2,1,0:T(8,128)(2,1)} %get-tuple-element.179), channel_id=1, source_target_pairs={{0,1},{1,0},{2,3},{3,2},{4,5},{5,4},{6,7},{7,6},{8,9},{9,8},{10,11... | collective-permute-start | bytes 3981320 | tf_op jit(solution)/shard_map/ppermute | solution.py:47
  280.1 40.3 %collective-permute-start.9 = (bf16[2,288,1152]{2,1,0:T(8,128)(2,1)}, bf16[2,288,1152]{2,1,0:T(8,128)(2,1)}, u32[]{:S(2)}, u32[]{:S(2)}) collective-permute-start(bf16[2,288,1152]{2,1,0:T(8,128)(2,1)} %get-tuple-element.180), channel_id=1, source_target_pairs={{0,2},{1,3},{2,0},{3,1},{4,6},{5,7},{6,4},{7,5},{8,10},{9,11},{10,... | collective-permute-start | bytes 3981320 | tf_op jit(solution)/shard_map/ppermute | solution.py:47
  315.4 55.4 %collective-permute-start.11 = (f32[7,1152]{1,0:T(8,128)S(1)}, f32[7,1152]{1,0:T(8,128)S(1)}, u32[]{:S(2)}, u32[]{:S(2)}) collective-permute-start(f32[7,1152]{1,0:T(8,128)S(1)} %select_maximum_fusion), channel_id=1, source_target_pairs={{0,16},{16,0},{1,17},{17,1},{2,18},{18,2},{3,19},{19,3},{4,20},{20... | collective-permute-start | bytes 96776 | tf_op jit(solution)/shard_map/ppermute | solution.py:47
  323.7 51.3 %collective-permute-start.12 = (bf16[288,1152]{1,0:T(8,128)(2,1)}, bf16[288,1152]{1,0:T(8,128)(2,1)S(1)}, u32[]{:S(2)}, u32[]{:S(2)}) collective-permute-start(bf16[288,1152]{1,0:T(8,128)(2,1)} %get-tuple-element.362), channel_id=1, source_target_pairs={{0,2},{1,3},{2,0},{3,1},{4,6},{5,7},{6,4},{7,5},{8,10},{9,11},{10,... | collective-permute-start | bytes 1990664 | tf_op jit(solution)/shard_map/ppermute | solution.py:47
  327.6 47.3 %collective-permute-start.13 = (bf16[288,1152]{1,0:T(8,128)(2,1)}, bf16[288,1152]{1,0:T(8,128)(2,1)}, u32[]{:S(2)}, u32[]{:S(2)}) collective-permute-start(bf16[288,1152]{1,0:T(8,128)(2,1)} %get-tuple-element.360), channel_id=1, source_target_pairs={{0,1},{1,0},{2,3},{3,2},{4,5},{5,4},{6,7},{7,6},{8,9},{9,8},{10,11... | collective-permute-start | bytes 1990664 | tf_op jit(solution)/shard_map/ppermute | solution.py:47
  337.7 37.2 %collective-permute-start.14 = (bf16[2,288,1152]{2,1,0:T(8,128)(2,1)}, bf16[2,288,1152]{2,1,0:T(8,128)(2,1)}, u32[]{:S(2)}, u32[]{:S(2)}) collective-permute-start(bf16[2,288,1152]{2,1,0:T(8,128)(2,1)} %get-tuple-element.202), channel_id=1, source_target_pairs={{0,1},{1,0},{2,3},{3,2},{4,5},{5,4},{6,7},{7,6},{8,9},{9,8},{10,11... | collective-permute-start | bytes 3981320 | tf_op jit(solution)/shard_map/ppermute | solution.py:47
  339.3 35.7 %collective-permute-start.15 = (bf16[2,288,1152]{2,1,0:T(8,128)(2,1)}, bf16[2,288,1152]{2,1,0:T(8,128)(2,1)}, u32[]{:S(2)}, u32[]{:S(2)}) collective-permute-start(bf16[2,288,1152]{2,1,0:T(8,128)(2,1)} %get-tuple-element.203), channel_id=1, source_target_pairs={{0,2},{1,3},{2,0},{3,1},{4,6},{5,7},{6,4},{7,5},{8,10},{9,11},{10,... | collective-permute-start | bytes 3981320 | tf_op jit(solution)/shard_map/ppermute | solution.py:47
  370.8 33.1 %collective-permute-start.20 = (bf16[4,576,768]{2,1,0:T(8,128)(2,1)}, bf16[4,576,768]{2,1,0:T(8,128)(2,1)}, u32[]{:S(2)}, u32[]{:S(2)}) collective-permute-start(bf16[4,576,768]{2,1,0:T(8,128)(2,1)} %get-tuple-element.216), channel_id=1, source_target_pairs={{0,16},{16,0},{1,17},{17,1},{2,18},{18,2},{3,19},{19,3},{4,20},{20... | collective-permute-start | bytes 10616840 | tf_op jit(solution)/shard_map/ppermute | solution.py:47
  379.7 22.2 %collective-permute-start.17 = (bf16[2,144,1152]{2,1,0:T(8,128)(2,1)}, bf16[2,144,1152]{2,1,0:T(8,128)(2,1)S(1)}, u32[]{:S(2)}, u32[]{:S(2)}) collective-permute-start(bf16[2,144,1152]{2,1,0:T(8,128)(2,1)} %get-tuple-element.376), channel_id=1, source_target_pairs={{0,4},{4,0},{8,12},{12,8},{1,5},{5,1},{9,13},{13,9},{2,6},{6,2},{1... | collective-permute-start | bytes 1990664 | tf_op jit(solution)/shard_map/ppermute | solution.py:47
  382.5 19.4 %collective-permute-start.18 = (bf16[288,1152]{1,0:T(8,128)(2,1)}, bf16[288,1152]{1,0:T(8,128)(2,1)}, u32[]{:S(2)}, u32[]{:S(2)}) collective-permute-start(bf16[288,1152]{1,0:T(8,128)(2,1)} %get-tuple-element.358), channel_id=1, source_target_pairs={{0,2},{1,3},{2,0},{3,1},{4,6},{5,7},{6,4},{7,5},{8,10},{9,11},{10,... | collective-permute-start | bytes 1990664 | tf_op jit(solution)/shard_map/ppermute | solution.py:47
  386.8 17.1 %collective-permute-start.19 = (bf16[288,1152]{1,0:T(8,128)(2,1)}, bf16[288,1152]{1,0:T(8,128)(2,1)}, u32[]{:S(2)}, u32[]{:S(2)}) collective-permute-start(bf16[288,1152]{1,0:T(8,128)(2,1)} %get-tuple-element.356), channel_id=1, source_target_pairs={{0,1},{1,0},{2,3},{3,2},{4,5},{5,4},{6,7},{7,6},{8,9},{9,8},{10,11... | collective-permute-start | bytes 1990664 | tf_op jit(solution)/shard_map/ppermute | solution.py:47
  387.5 14.4 %collective-permute-start.16 = (f32[7,1152]{1,0:T(8,128)S(1)}, f32[7,1152]{1,0:T(8,128)S(1)}, u32[]{:S(2)}, u32[]{:S(2)}) collective-permute-start(f32[7,1152]{1,0:T(8,128)S(1)} %maximum_select_fusion.4), channel_id=1, source_target_pairs={{0,4},{4,0},{8,12},{12,8},{1,5},{5,1},{9,13},{13,9},{2,6},{6,2},{1... | collective-permute-start | bytes 96776 | tf_op jit(solution)/shard_map/ppermute | solution.py:47
  429.6 22.0 %collective-permute-start.21 = (f32[7,1152]{1,0:T(8,128)S(1)}, f32[7,1152]{1,0:T(8,128)S(1)}, u32[]{:S(2)}, u32[]{:S(2)}) collective-permute-start(f32[7,1152]{1,0:T(8,128)S(1)} %maximum_select_fusion.3), channel_id=1, source_target_pairs={{0,8},{4,12},{8,0},{12,4},{1,9},{5,13},{9,1},{13,5},{2,10},{6,14},... | collective-permute-start | bytes 96776 | tf_op jit(solution)/shard_map/ppermute | solution.py:47
  435.4 23.2 %collective-permute-start.23 = (bf16[2,144,1152]{2,1,0:T(8,128)(2,1)}, bf16[2,144,1152]{2,1,0:T(8,128)(2,1)}, u32[]{:S(2)}, u32[]{:S(2)}) collective-permute-start(bf16[2,144,1152]{2,1,0:T(8,128)(2,1)} %get-tuple-element.374), channel_id=1, source_target_pairs={{0,4},{4,0},{8,12},{12,8},{1,5},{5,1},{9,13},{13,9},{2,6},{6,2},{1... | collective-permute-start | bytes 1990664 | tf_op jit(solution)/shard_map/ppermute | solution.py:47
  437.1 21.6 %collective-permute-start.24 = (bf16[2,288,768]{2,1,0:T(8,128)(2,1)}, bf16[2,288,768]{2,1,0:T(8,128)(2,1)}, u32[]{:S(2)}, u32[]{:S(2)}) collective-permute-start(bf16[2,288,768]{2,1,0:T(8,128)(2,1)} %get-tuple-element.235), channel_id=1, source_target_pairs={{0,1},{1,0},{2,3},{3,2},{4,5},{5,4},{6,7},{7,6},{8,9},{9,8},{10,11... | collective-permute-start | bytes 2654216 | tf_op jit(solution)/shard_map/ppermute | solution.py:47
  437.7 20.9 %collective-permute-start.25 = (bf16[2,288,768]{2,1,0:T(8,128)(2,1)}, bf16[2,288,768]{2,1,0:T(8,128)(2,1)}, u32[]{:S(2)}, u32[]{:S(2)}) collective-permute-start(bf16[2,288,768]{2,1,0:T(8,128)(2,1)} %get-tuple-element.236), channel_id=1, source_target_pairs={{0,2},{1,3},{2,0},{3,1},{4,6},{5,7},{6,4},{7,5},{8,10},{9,11},{10,... | collective-permute-start | bytes 2654216 | tf_op jit(solution)/shard_map/ppermute | solution.py:47
  440.2 17.4 %collective-permute-start.22 = (bf16[144,1152]{1,0:T(8,128)(2,1)}, bf16[144,1152]{1,0:T(8,128)(2,1)S(1)}, u32[]{:S(2)}, u32[]{:S(2)}) collective-permute-start(bf16[144,1152]{1,0:T(8,128)(2,1)} %get-tuple-element.387), channel_id=1, source_target_pairs={{0,8},{4,12},{8,0},{12,4},{1,9},{5,13},{9,1},{13,5},{2,10},{6,14},... | collective-permute-start | bytes 995336 | tf_op jit(solution)/shard_map/ppermute | solution.py:47
  451.7 35.3 %collective-permute-start.31 = (bf16[4,576,512]{2,1,0:T(8,128)(2,1)}, bf16[4,576,512]{2,1,0:T(8,128)(2,1)}, u32[]{:S(2)}, u32[]{:S(2)}) collective-permute-start(bf16[4,576,512]{2,1,0:T(8,128)(2,1)} %get-tuple-element.251), channel_id=1, source_target_pairs={{0,16},{16,0},{1,17},{17,1},{2,18},{18,2},{3,19},{19,3},{4,20},{20... | collective-permute-start | bytes 7077896 | tf_op jit(solution)/shard_map/ppermute | solution.py:47
  458.7 10.2 %collective-permute-start.26 = (f32[7,1152]{1,0:T(8,128)S(1)}, f32[7,1152]{1,0:T(8,128)S(1)}, u32[]{:S(2)}, u32[]{:S(2)}) collective-permute-start(f32[7,1152]{1,0:T(8,128)S(1)} %maximum_select_fusion.2), channel_id=1, source_target_pairs={{0,1},{1,0},{2,3},{3,2},{4,5},{5,4},{6,7},{7,6},{8,9},{9,8},{10,11... | collective-permute-start | bytes 96776 | tf_op jit(solution)/shard_map/ppermute | solution.py:47
  460.2 26.7 %collective-permute-start.27 = (bf16[144,1152]{1,0:T(8,128)(2,1)}, bf16[144,1152]{1,0:T(8,128)(2,1)}, u32[]{:S(2)}, u32[]{:S(2)}) collective-permute-start(bf16[144,1152]{1,0:T(8,128)(2,1)} %add_convert_fusion.23), channel_id=1, source_target_pairs={{0,16},{16,0},{1,17},{17,1},{2,18},{18,2},{3,19},{19,3},{4,20},{20... | collective-permute-start | bytes 995336 | tf_op jit(solution)/shard_map/ppermute | solution.py:47
  462.4 24.5 %collective-permute-start.29 = (bf16[288,768]{1,0:T(8,128)(2,1)}, bf16[288,768]{1,0:T(8,128)(2,1)}, u32[]{:S(2)}, u32[]{:S(2)}) collective-permute-start(bf16[288,768]{1,0:T(8,128)(2,1)} %get-tuple-element.372), channel_id=1, source_target_pairs={{0,2},{1,3},{2,0},{3,1},{4,6},{5,7},{6,4},{7,5},{8,10},{9,11},{10,... | collective-permute-start | bytes 1327112 | tf_op jit(solution)/shard_map/ppermute | solution.py:47
  466.2 20.7 %collective-permute-start.30 = (bf16[288,768]{1,0:T(8,128)(2,1)}, bf16[288,768]{1,0:T(8,128)(2,1)}, u32[]{:S(2)}, u32[]{:S(2)}) collective-permute-start(bf16[288,768]{1,0:T(8,128)(2,1)} %get-tuple-element.370), channel_id=1, source_target_pairs={{0,1},{1,0},{2,3},{3,2},{4,5},{5,4},{6,7},{7,6},{8,9},{9,8},{10,11... | collective-permute-start | bytes 1327112 | tf_op jit(solution)/shard_map/ppermute | solution.py:47
  468.9 18.0 %collective-permute-start.28 = (bf16[144,1152]{1,0:T(8,128)(2,1)}, bf16[144,1152]{1,0:T(8,128)(2,1)S(1)}, u32[]{:S(2)}, u32[]{:S(2)}) collective-permute-start(bf16[144,1152]{1,0:T(8,128)(2,1)} %get-tuple-element.385), channel_id=1, source_target_pairs={{0,8},{4,12},{8,0},{12,4},{1,9},{5,13},{9,1},{13,5},{2,10},{6,14},... | collective-permute-start | bytes 995336 | tf_op jit(solution)/shard_map/ppermute | solution.py:47
  487.8 19.2 %collective-permute-start.48 = (f32[7,1152]{1,0:T(8,128)S(1)}, f32[7,1152]{1,0:T(8,128)}, u32[]{:S(2)}, u32[]{:S(2)}) collective-permute-start(f32[7,1152]{1,0:T(8,128)S(1)} %maximum_select_fusion.1), channel_id=1, source_target_pairs={{0,2},{1,3},{2,0},{3,1},{4,6},{5,7},{6,4},{7,5},{8,10},{9,11},{10,... | collective-permute-start | bytes 96776 | tf_op jit(solution)/shard_map/ppermute | solution.py:47
  490.1 23.7 %collective-permute-start.49 = (bf16[144,1152]{1,0:T(8,128)(2,1)}, bf16[144,1152]{1,0:T(8,128)(2,1)}, u32[]{:S(2)}, u32[]{:S(2)}) collective-permute-start(bf16[144,1152]{1,0:T(8,128)(2,1)} %add_convert_fusion.22), channel_id=1, source_target_pairs={{0,16},{16,0},{1,17},{17,1},{2,18},{18,2},{3,19},{19,3},{4,20},{20... | collective-permute-start | bytes 995336 | tf_op jit(solution)/shard_map/ppermute | solution.py:47
  493.4 22.7 %collective-permute-start.38 = (bf16[2,144,768]{2,1,0:T(8,128)(2,1)}, bf16[2,144,768]{2,1,0:T(8,128)(2,1)}, u32[]{:S(2)}, u32[]{:S(2)}) collective-permute-start(bf16[2,144,768]{2,1,0:T(8,128)(2,1)} %fusion.28), channel_id=1, source_target_pairs={{0,4},{4,0},{8,12},{12,8},{1,5},{5,1},{9,13},{13,9},{2,6},{6,2},{1... | collective-permute-start | bytes 1327112 | tf_op jit(solution)/shard_map/ppermute | solution.py:47
  502.5 16.7 %collective-permute-start.41 = (bf16[2,288,512]{2,1,0:T(8,128)(2,1)}, bf16[2,288,512]{2,1,0:T(8,128)(2,1)}, u32[]{:S(2)}, u32[]{:S(2)}) collective-permute-start(bf16[2,288,512]{2,1,0:T(8,128)(2,1)} %get-tuple-element.263), channel_id=1, source_target_pairs={{0,1},{1,0},{2,3},{3,2},{4,5},{5,4},{6,7},{7,6},{8,9},{9,8},{10,11... | collective-permute-start | bytes 1769480 | tf_op jit(solution)/shard_map/ppermute | solution.py:47
  503.1 18.4 %collective-permute-start.43 = (bf16[2,288,512]{2,1,0:T(8,128)(2,1)}, bf16[2,288,512]{2,1,0:T(8,128)(2,1)}, u32[]{:S(2)}, u32[]{:S(2)}) collective-permute-start(bf16[2,288,512]{2,1,0:T(8,128)(2,1)} %get-tuple-element.265), channel_id=1, source_target_pairs={{0,2},{1,3},{2,0},{3,1},{4,6},{5,7},{6,4},{7,5},{8,10},{9,11},{10,... | collective-permute-start | bytes 1769480 | tf_op jit(solution)/shard_map/ppermute | solution.py:47
  517.3 12.1 %collective-permute-start.39 = (bf16[144,768]{1,0:T(8,128)(2,1)S(1)}, bf16[144,768]{1,0:T(8,128)(2,1)S(1)}, u32[]{:S(2)}, u32[]{:S(2)}) collective-permute-start(bf16[144,768]{1,0:T(8,128)(2,1)S(1)} %dynamic-slice_bitcast_fusion.5), channel_id=1, source_target_pairs={{0,8},{4,12},{8,0},{12,4},{1,9},{5,13},{9,1},{13,5},{2,10},{6,14},... | collective-permute-start | bytes 663560 | tf_op jit(solution)/shard_map/ppermute | solution.py:47
  521.0 31.3 %collective-permute-start.42 = (bf16[288,512]{1,0:T(8,128)(2,1)}, bf16[288,512]{1,0:T(8,128)(2,1)}, u32[]{:S(2)}, u32[]{:S(2)}) collective-permute-start(bf16[288,512]{1,0:T(8,128)(2,1)} %fusion.33), channel_id=1, source_target_pairs={{0,2},{1,3},{2,0},{3,1},{4,6},{5,7},{6,4},{7,5},{8,10},{9,11},{10,... | collective-permute-start | bytes 884744 | tf_op jit(solution)/shard_map/ppermute | solution.py:47
  523.2 33.2 %collective-permute-start.44 = (bf16[288,512]{1,0:T(8,128)(2,1)}, bf16[288,512]{1,0:T(8,128)(2,1)}, u32[]{:S(2)}, u32[]{:S(2)}) collective-permute-start(bf16[288,512]{1,0:T(8,128)(2,1)} %fusion.35), channel_id=1, source_target_pairs={{0,1},{1,0},{2,3},{3,2},{4,5},{5,4},{6,7},{7,6},{8,9},{9,8},{10,11... | collective-permute-start | bytes 884744 | tf_op jit(solution)/shard_map/ppermute | solution.py:47
  529.5 13.4 %collective-permute-start.40 = (bf16[144,768]{1,0:T(8,128)(2,1)S(1)}, bf16[144,768]{1,0:T(8,128)(2,1)S(1)}, u32[]{:S(2)}, u32[]{:S(2)}) collective-permute-start(bf16[144,768]{1,0:T(8,128)(2,1)S(1)} %fusion.31), channel_id=1, source_target_pairs={{0,16},{16,0},{1,17},{17,1},{2,18},{18,2},{3,19},{19,3},{4,20},{20... | collective-permute-start | bytes 663560 | tf_op jit(solution)/shard_map/ppermute | solution.py:47
  542.4 6.4 %collective-permute-start.32 = (f32[8,1152]{1,0:T(8,128)S(1)}, f32[8,1152]{1,0:T(8,128)S(1)}, u32[]{:S(2)}, u32[]{:S(2)}) collective-permute-start(f32[8,1152]{1,0:T(8,128)S(1)} %broadcast_add_fusion), channel_id=1, source_target_pairs={{0,4},{4,0},{8,12},{12,8},{1,5},{5,1},{9,13},{13,9},{2,6},{6,2},{1... | collective-permute-start | bytes 110600 | tf_op jit(solution)/shard_map/ppermute | solution.py:47
  560.6 6.8 %collective-permute-start.45 = (bf16[2,144,512]{2,1,0:T(8,128)(2,1)S(1)}, bf16[2,144,512]{2,1,0:T(8,128)(2,1)S(1)}, u32[]{:S(2)}, u32[]{:S(2)}) collective-permute-start(bf16[2,144,512]{2,1,0:T(8,128)(2,1)S(1)} %fusion.37), channel_id=1, source_target_pairs={{0,4},{4,0},{8,12},{12,8},{1,5},{5,1},{9,13},{13,9},{2,6},{6,2},{1... | collective-permute-start | bytes 884744 | tf_op jit(solution)/shard_map/ppermute | solution.py:47
  567.5 8.5 %collective-permute-start.46 = (bf16[144,512]{1,0:T(8,128)(2,1)S(1)}, bf16[144,512]{1,0:T(8,128)(2,1)S(1)}, u32[]{:S(2)}, u32[]{:S(2)}) collective-permute-start(bf16[144,512]{1,0:T(8,128)(2,1)S(1)} %dynamic-slice_bitcast_fusion.6), channel_id=1, source_target_pairs={{0,8},{4,12},{8,0},{12,4},{1,9},{5,13},{9,1},{13,5},{2,10},{6,14},... | collective-permute-start | bytes 442376 | tf_op jit(solution)/shard_map/ppermute | solution.py:47
  576.0 6.6 %collective-permute-start.47 = (bf16[144,512]{1,0:T(8,128)(2,1)S(1)}, bf16[144,512]{1,0:T(8,128)(2,1)S(1)}, u32[]{:S(2)}, u32[]{:S(2)}) collective-permute-start(bf16[144,512]{1,0:T(8,128)(2,1)S(1)} %fusion.40), channel_id=1, source_target_pairs={{0,16},{16,0},{1,17},{17,1},{2,18},{18,2},{3,19},{19,3},{4,20},{20... | collective-permute-start | bytes 442376 | tf_op jit(solution)/shard_map/ppermute | solution.py:47
  (58 other events, 848.5 us)
Sparse Core Ops, SparseCore 0:
  12.0 152.8 all-gather.4
  168.5 84.8 all-gather.6
  487.0 48.1 all-gather.8
